TPU v7x, 32 devices: a whole 2x2x4 slice. The times are simulated.
32 devices in a mesh: dp: 8 (over z, y), tensor: 4 (over x, core).
Axes of the slice: x: 2, y: 2, z: 4, core: 2. Of those that a mesh axis runs over, the one named last changes fastest.
Arguments:
- block_weights: float32 [2, 9216, 768], P(None, ('dp', 'tensor')), as said below
- head_weights: float32 [2, 5120, 1024], P(None, ('dp', 'tensor')), as said below
- head_rest: float32 [4992, 1024], P('dp', 'tensor'), as said below
- embed_tables: float32 [768, 1723], P('dp'), as said below
- bias_rows: float32 [212, 128], replicated, as said below
- first_blocks: float32 [2, 9216, 768], P(None, ('dp', 'tensor')), as said below
- second_blocks: float32 [2, 9216, 768], P(None, ('dp', 'tensor')), as said below
- first_head: float32 [2, 5120, 1024], P(None, ('dp', 'tensor')), as said below
- second_head: float32 [2, 5120, 1024], P(None, ('dp', 'tensor')), as said below
- first_rest: float32 [4992, 1024], P('dp', 'tensor'), as said below
- second_rest: float32 [4992, 1024], P('dp', 'tensor'), as said below
- first_tables: float32 [768, 1723], P('dp'), as said below
- second_tables: float32 [768, 1723], P('dp'), as said below
- first_bias: float32 [212, 128], replicated, as said below
- second_bias: float32 [212, 128], replicated, as said below
- patches: bfloat16 [8, 256, 64], P('dp'), may hold values from -6 to 6
- noise: bfloat16 [1, 8, 256, 64], P(None, 'dp'), may hold values from -6 to 6
- token_mask: int32 [8, 256], P('dp'), may hold values 0 or 1
- labels: int32 [8], P('dp'), may hold values from 0 to 999
- drop_marks: int32 [8], P('dp'), may hold values 0 or 1
- timesteps: int32 [1, 8, 256], P(None, 'dp'), may hold values from 0 to 999
- step_weights: float32 [1000], replicated, may hold values from 0.3 to 3
- step_count: int32 [1], replicated, may hold values from 1 to 20
Outputs:
- loss_value: float32 [], replicated
- grad_norm: float32 [], replicated
- blocks_new: float32 [2, 9216, 768], P(None, ('dp', 'tensor'))
- blocks_first: float32 [2, 9216, 768], P(None, ('dp', 'tensor'))
- blocks_second: float32 [2, 9216, 768], P(None, ('dp', 'tensor'))
- blocks_low: bfloat16 [2, 9216, 768], P(None, ('dp', 'tensor'))
- head_new: float32 [2, 5120, 1024], P(None, ('dp', 'tensor'))
- head_first: float32 [2, 5120, 1024], P(None, ('dp', 'tensor'))
- head_second: float32 [2, 5120, 1024], P(None, ('dp', 'tensor'))
- head_low: bfloat16 [2, 5120, 1024], P(None, ('dp', 'tensor'))
- rest_new: float32 [4992, 1024], P('dp', 'tensor')
- rest_first: float32 [4992, 1024], P('dp', 'tensor')
- rest_second: float32 [4992, 1024], P('dp', 'tensor')
- rest_low: bfloat16 [4992, 1024], P('dp', 'tensor')
- tables_new: float32 [768, 1723], P('dp')
- tables_first: float32 [768, 1723], P('dp')
- tables_second: float32 [768, 1723], P('dp')
- tables_low: bfloat16 [768, 1723], P('dp')
- bias_new: float32 [212, 128], replicated
- bias_first: float32 [212, 128], replicated
- bias_second: float32 [212, 128], replicated
- bias_low: bfloat16 [212, 128], replicated
Inputs may be any that keep to these rules, and one draw needn't show every extreme that they name: `block_weights`: real values. `head_weights`: real values. `head_rest`: real values. `embed_tables`: real values. `bias_rows`: real values. `first_blocks`: real values. `second_blocks`: positive. `first_head`: real values. `second_head`: positive. `first_rest`: real values. `second_rest`: positive. `first_tables`: real values. `second_tables`: positive. `first_bias`: real values. `second_bias`: positive.
All inputs are finite; a program needn't handle non-finite values. No bound on the sum of `token_mask` or of `drop_marks` on one device may be relied on, other than what follows from the above.
Results may differ from a plain program's by a relative error of at most 0.0019.
The roundings to bfloat16 on the way count: a program that leaves them out, or rounds other values in their place, can miss the bound.
Values may be sent and summed in bfloat16 or wider, within the bound.
A program may use at most 256 MiB of HBM per device.

v0:
```python
import math

import jax
import jax.numpy as jnp
from jax import lax
from jax.sharding import PartitionSpec as P

D = 768
HEAD = 64
FF = 3072
HW = 1024
TOKD = 64
CLASSES = 1000
BUF = 64
TOK = 256
T_STEPS = 1000
COPIES = 1
LAYERS = 2
HB = 2


highest = lax.Precision.HIGHEST
norm_eps = 1e-06
beta_first = 0.9
beta_second = 0.95
adam_eps = 1e-08
learn_rate = 0.02
decay_rate = 0.05
clip_limit = 0.002


def layer_norm(inputs, gain_vec, offset_vec):
    average = jnp.mean(inputs, axis=-1, keepdims=True)
    centred = inputs - average
    spread = jnp.mean(centred * centred, axis=-1, keepdims=True)
    return centred * lax.rsqrt(spread + norm_eps) * gain_vec + offset_vec


def modulate(inputs, shift_vec, scale_vec):
    return layer_norm(inputs, 1.0, 0.0) * (1.0 + scale_vec) + shift_vec


def exact_gelu(inputs):
    return jax.nn.gelu(inputs, approximate=False)


def local_back(function, inputs, incoming):
    return jax.vjp(function, inputs)[1](incoming)[0]


def sinusoid(step_ids):
    half_width = HW // 2
    frequency = jnp.exp(-math.log(10000.0) * jnp.arange(half_width, dtype=jnp.float32) / half_width)
    angles = step_ids.astype(jnp.float32)[..., None] * frequency
    return jnp.concatenate([jnp.cos(angles), jnp.sin(angles)], axis=-1)


def cut_rows(packed, counts):
    pieces = []
    begin_at = 0
    for count in counts:
        pieces.append(packed[begin_at : begin_at + count])
        begin_at = begin_at + count
    return pieces


def narrow(inputs):
    return inputs.astype(jnp.bfloat16)


def product(left, right):
    return jnp.dot(left, right, preferred_element_type=jnp.float32)


def product_left(left, right):
    return lax.dot_general(
        left, right, (((0,), (0,)), ((), ())), preferred_element_type=jnp.float32
    )


def product_right(left, right):
    return lax.dot_general(
        left, right, (((1,), (1,)), ((), ())), preferred_element_type=jnp.float32
    )


def column_sum(inputs):
    return jnp.sum(inputs.astype(jnp.float32), axis=0)


def branch_sum(partial_term):
    return lax.psum(partial_term, "tensor")


def input_sum(partial_term):
    return lax.psum(partial_term.astype(jnp.bfloat16), "tensor").astype(jnp.float32)


def take_pieces(vector, starts, counts):
    return jnp.concatenate(
        [lax.dynamic_slice_in_dim(vector, start, count) for start, count in zip(starts, counts)]
    )


def place_pieces(total, pieces, starts):
    full = jnp.zeros((total,), jnp.float32)
    for piece, start in zip(pieces, starts):
        full = lax.dynamic_update_slice_in_dim(full, piece, start, 0)
    return full


def score_block(queries, key_rows, visible):
    scores = jnp.einsum(
        "bqhd,bkhd->bhqk", queries, key_rows, preferred_element_type=jnp.float32
    ) * HEAD ** (-0.5)
    return scores + (visible[:, None, None, :] - 1.0) * 1000000000.0


def attention(queries, key_rows, value_rows, visible):
    scores = score_block(queries, key_rows, visible)
    largest = jnp.max(scores, axis=-1, keepdims=True)
    exponent = jnp.exp(scores - largest)
    normaliser = jnp.sum(exponent, axis=-1, keepdims=True)
    chance = narrow(exponent / normaliser)
    attended = narrow(
        jnp.einsum("bhqk,bkhd->bqhd", chance, value_rows, preferred_element_type=jnp.float32)
    )
    return (attended, largest + jnp.log(normaliser))


def attention_back(queries, key_rows, value_rows, visible, log_total, grad_attended):
    chance = jnp.exp(score_block(queries, key_rows, visible) - log_total)
    grad_values = jnp.einsum(
        "bhqk,bqhd->bkhd", narrow(chance), grad_attended, preferred_element_type=jnp.float32
    )
    grad_chance = jnp.einsum(
        "bqhd,bkhd->bhqk", grad_attended, value_rows, preferred_element_type=jnp.float32
    )
    grad_scores = narrow(
        chance * (grad_chance - jnp.sum(chance * grad_chance, axis=-1, keepdims=True))
    )
    grad_queries = jnp.einsum(
        "bhqk,bkhd->bqhd", grad_scores, key_rows, preferred_element_type=jnp.float32
    ) * HEAD ** (-0.5)
    grad_keys = jnp.einsum(
        "bhqk,bqhd->bkhd", grad_scores, queries, preferred_element_type=jnp.float32
    ) * HEAD ** (-0.5)
    return (grad_queries, grad_keys, grad_values)


def block_forward(stream, visible, layer_rows, layer_bias, vectors):
    images = visible.shape[0]
    local_width = D // lax.axis_size("tensor")
    local_ff = FF // lax.axis_size("tensor")
    heads_here = local_width // HEAD
    flat = stream.reshape(-1, D)
    normed = narrow(layer_norm(flat, vectors[0], vectors[1]))
    mixed = narrow(
        product_right(normed, layer_rows[: 3 * local_width]) + layer_bias[: 3 * local_width]
    )
    parts = [
        mixed[:, slot * local_width : (slot + 1) * local_width].reshape(
            images, -1, heads_here, HEAD
        )
        for slot in range(3)
    ]
    attended, log_total = attention(parts[0], parts[1], parts[2], visible)
    attended = attended.reshape(-1, local_width)
    middle = (
        flat
        + branch_sum(
            product(attended, layer_rows[3 * local_width + local_ff : 4 * local_width + local_ff])
        )
        + vectors[4]
    )
    second = narrow(layer_norm(middle, vectors[2], vectors[3]))
    inner = (
        product_right(second, layer_rows[3 * local_width : 3 * local_width + local_ff])
        + layer_bias[3 * local_width :]
    )
    active = narrow(exact_gelu(inner))
    result = (
        middle + branch_sum(product(active, layer_rows[4 * local_width + local_ff :])) + vectors[5]
    )
    return (
        result.reshape(stream.shape),
        (flat, normed, parts, log_total, attended, middle, second, inner, active),
    )


def block_back(incoming, visible, layer_rows, vectors, stored):
    flat, normed, parts, log_total, attended, middle, second, inner, active = stored
    local_width = D // lax.axis_size("tensor")
    local_ff = FF // lax.axis_size("tensor")
    mix_rows = layer_rows[: 3 * local_width]
    up_rows = layer_rows[3 * local_width : 3 * local_width + local_ff]
    proj_rows = layer_rows[3 * local_width + local_ff : 4 * local_width + local_ff]
    down_rows = layer_rows[4 * local_width + local_ff :]
    flow = incoming.reshape(-1, D)
    grad_branch = narrow(flow)
    grad_down = product_left(active, grad_branch)
    grad_active = product_right(grad_branch, down_rows)
    grad_inner = narrow(local_back(exact_gelu, inner, grad_active))
    grad_up = product_left(grad_inner, second)
    grad_second = input_sum(product(grad_inner, up_rows))
    grad_middle, grad_gain_two, grad_shift_two = jax.vjp(
        layer_norm, middle, vectors[2], vectors[3]
    )[1](grad_second)
    grad_middle = flow + grad_middle
    grad_attn = narrow(grad_middle)
    grad_proj = product_left(attended, grad_attn)
    grad_attended = narrow(product_right(grad_attn, proj_rows)).reshape(parts[0].shape)
    grads_mixed = attention_back(parts[0], parts[1], parts[2], visible, log_total, grad_attended)
    grad_mixed = narrow(
        jnp.concatenate([piece.reshape(-1, local_width) for piece in grads_mixed], axis=1)
    )
    grad_mix = product_left(grad_mixed, normed)
    grad_normed = input_sum(product(grad_mixed, mix_rows))
    grad_flat, grad_gain_one, grad_shift_one = jax.vjp(layer_norm, flat, vectors[0], vectors[1])[1](
        grad_normed
    )
    grad_rows = jnp.concatenate([grad_mix, grad_up, grad_proj, grad_down], axis=0)
    grad_bias = jnp.concatenate([column_sum(grad_mixed), column_sum(grad_inner)])
    grad_vectors = jnp.stack(
        [
            grad_gain_one,
            grad_shift_one,
            grad_gain_two,
            grad_shift_two,
            column_sum(grad_attn),
            column_sum(grad_branch),
        ]
    )
    return ((grad_middle + grad_flat).reshape(incoming.shape), grad_rows, grad_bias, grad_vectors)


def head_block(hidden_state, cond_act, segment_rows, segment_bias, last_bias):
    local_hidden = HW // lax.axis_size("tensor")
    adaptive = (
        product_right(cond_act, segment_rows[: 3 * local_hidden]) + segment_bias[: 3 * local_hidden]
    )
    shift_vec, scale_vec, gate_vec = (
        lax.all_gather(adaptive[:, :local_hidden], "tensor", axis=1, tiled=True),
        lax.all_gather(adaptive[:, local_hidden : 2 * local_hidden], "tensor", axis=1, tiled=True),
        lax.all_gather(adaptive[:, 2 * local_hidden :], "tensor", axis=1, tiled=True),
    )
    modulated = narrow(modulate(hidden_state, shift_vec, scale_vec))
    inner = (
        product_right(modulated, segment_rows[3 * local_hidden : 4 * local_hidden])
        + segment_bias[3 * local_hidden :]
    )
    active = narrow(jax.nn.silu(inner))
    branch = branch_sum(product(active, segment_rows[4 * local_hidden :])) + last_bias
    return (
        hidden_state + gate_vec * branch,
        (hidden_state, shift_vec, scale_vec, gate_vec, modulated, inner, active, branch),
    )


def head_block_back(incoming, cond_act, segment_rows, offset, stored):
    hidden_state, shift_vec, scale_vec, gate_vec, modulated, inner, active, branch = stored
    local_hidden = HW // lax.axis_size("tensor")
    grad_gate = incoming * branch
    grad_branch = narrow(incoming * gate_vec)
    grad_down = product_left(active, grad_branch)
    grad_active = product_right(grad_branch, segment_rows[4 * local_hidden :])
    grad_inner = narrow(local_back(jax.nn.silu, inner, grad_active))
    grad_up = product_left(grad_inner, modulated)
    grad_modulated = input_sum(
        product(grad_inner, segment_rows[3 * local_hidden : 4 * local_hidden])
    )
    grad_hidden, grad_shift, grad_scale = jax.vjp(modulate, hidden_state, shift_vec, scale_vec)[1](
        grad_modulated
    )
    grad_adaptive = narrow(
        jnp.concatenate(
            [
                lax.dynamic_slice_in_dim(piece, offset, local_hidden, 1)
                for piece in (grad_shift, grad_scale, grad_gate)
            ],
            axis=1,
        )
    )
    grad_ada = product_left(grad_adaptive, cond_act)
    grad_cond = product(grad_adaptive, segment_rows[: 3 * local_hidden])
    grad_rows = jnp.concatenate([grad_ada, grad_up, grad_down], axis=0)
    grad_bias = jnp.concatenate([column_sum(grad_adaptive), column_sum(grad_inner)])
    return (incoming + grad_hidden, grad_cond, grad_rows, grad_bias, column_sum(grad_branch))


def adam_update(weight, moment_one, moment_two, gradient, factor, step_num):
    gradient = gradient * factor
    moment_one = beta_first * moment_one + (1.0 - beta_first) * gradient
    moment_two = beta_second * moment_two + (1.0 - beta_second) * gradient * gradient
    fixed_one = moment_one / (1.0 - beta_first**step_num)
    fixed_two = moment_two / (1.0 - beta_second**step_num)
    weight = weight - learn_rate * (
        fixed_one / (jnp.sqrt(fixed_two) + adam_eps) + decay_rate * weight
    )
    return (weight, moment_one, moment_two)


def local(
    block_weights,
    head_weights,
    head_rest,
    embed_tables,
    bias_rows,
    first_blocks,
    second_blocks,
    first_head,
    second_head,
    first_rest,
    second_rest,
    first_tables,
    second_tables,
    first_bias,
    second_bias,
    patches,
    noise,
    token_mask,
    labels,
    drop_marks,
    timesteps,
    step_weights,
    step_count,
):
    tensor_size = lax.axis_size("tensor")
    tensor_index = lax.axis_index("tensor")
    local_width = D // tensor_size
    local_ff = FF // tensor_size
    local_hidden = HW // tensor_size
    offset = tensor_index * local_hidden
    column_starts = [slot * D + tensor_index * local_width for slot in range(3)] + [
        3 * D + tensor_index * local_ff
    ]
    column_counts = [local_width] * 3 + [local_ff]
    head_starts = [slot * HW + offset for slot in range(4)]
    block_all, head_all = (
        lax.all_gather(narrow(block_weights), "dp", axis=1, tiled=True),
        lax.all_gather(narrow(head_weights), "dp", axis=1, tiled=True),
    )
    rest_rows, table_cols = (
        lax.all_gather(head_rest, "dp", axis=0, tiled=True),
        lax.all_gather(embed_tables, "dp", axis=0, tiled=True),
    )
    rest_all = lax.all_gather(narrow(rest_rows), "tensor", axis=1, tiled=True)
    rest_parts = cut_rows(rest_all, (D, TOKD, TOKD, HW, HW, HW, HW))
    cond_weight, input_weight, output_weight, time_first, time_second, final_shift, final_scale = [
        narrow(piece) for piece in rest_parts
    ]
    flat_bias = bias_rows.reshape(-1)
    rest_bias = flat_bias[: 6 * HW].reshape(6, HW)
    head_bias = flat_bias[6 * HW : 6 * HW + 5 * HB * HW].reshape(HB, 5 * HW)
    column_bias = flat_bias[6 * HW + 5 * HB * HW :].reshape(LAYERS, 3 * D + FF)
    table_parts = cut_rows(
        table_cols.T, (TOKD, 1, CLASSES + 1, TOK + BUF, TOK + BUF, 1, 6 * LAYERS, 4)
    )
    layer_vectors = table_parts[6].reshape(LAYERS, 6, D)
    final_norms = table_parts[7]
    images = patches.shape[0]
    mask_float = token_mask.astype(jnp.float32)
    matches = timesteps[..., None] == jnp.arange(T_STEPS)
    row_weight = (
        jnp.sum(jnp.where(matches, step_weights, 0.0), axis=-1) * mask_float[None]
    ).reshape(-1)
    weight_total = lax.psum(jnp.sum(row_weight), "dp")
    chosen = jnp.where(drop_marks == 1, CLASSES, labels)
    picker = (chosen[:, None] == jnp.arange(CLASSES + 1)[None, :]).astype(jnp.float32)
    class_rows = jnp.dot(picker, table_parts[2], precision=highest)
    patch_flat = patches.reshape(-1, TOKD)
    tokens = product(patch_flat, narrow(table_parts[0])) + table_parts[1][0]
    stream = (
        jnp.concatenate(
            [
                jnp.broadcast_to(class_rows[:, None, :], (images, BUF, D)),
                tokens.reshape(images, TOK, D),
            ],
            axis=1,
        )
        + table_parts[3]
    )
    buffer_ones = jnp.ones((images, BUF), jnp.float32)
    visible_enc = jnp.concatenate([buffer_ones, 1.0 - mask_float], axis=1)
    visible_all = jnp.ones((images, TOK + BUF), jnp.float32)
    hidden_rows = jnp.concatenate([0.0 * buffer_ones, mask_float], axis=1)[..., None]
    layer_bias = [
        take_pieces(column_bias[layer], column_starts, column_counts) for layer in range(LAYERS)
    ]
    encoded, stored_enc = block_forward(
        stream, visible_enc, block_all[0], layer_bias[0], layer_vectors[0]
    )
    enc_normed = layer_norm(encoded, final_norms[0], final_norms[1])
    decoder_in = enc_normed * (1.0 - hidden_rows) + table_parts[5][0] * hidden_rows + table_parts[4]
    decoded, stored_dec = block_forward(
        decoder_in, visible_all, block_all[1], layer_bias[1], layer_vectors[1]
    )
    latent = narrow(layer_norm(decoded, final_norms[2], final_norms[3])[:, BUF:].reshape(-1, D))
    condition = product(latent, cond_weight) + rest_bias[0]
    step_rows = timesteps.reshape(COPIES, -1)
    time_feat = narrow(sinusoid(step_rows).reshape(-1, HW))
    time_pre = product(time_feat, time_first) + rest_bias[2]
    time_act = narrow(jax.nn.silu(time_pre))
    time_embed = product(time_act, time_second) + rest_bias[3]
    cond_vec = (condition[None] + time_embed.reshape(COPIES, -1, HW)).reshape(-1, HW)
    cond_act = narrow(jax.nn.silu(cond_vec))
    phase = step_rows.astype(jnp.float32)[..., None] * (math.pi / (2 * T_STEPS))
    signal_coef = jnp.cos(phase)
    noise_coef = jnp.sin(phase)
    clean = patch_flat.astype(jnp.float32)[None]
    noise_rows = noise.reshape(COPIES, -1, TOKD).astype(jnp.float32)
    noisy_rows = narrow((signal_coef * clean + noise_coef * noise_rows).reshape(-1, TOKD))
    target = (signal_coef * noise_rows - noise_coef * clean).reshape(-1, TOKD)
    hidden_state = product(noisy_rows, input_weight) + rest_bias[1]
    stored_head = []
    for segment in range(HB):
        segment_bias = take_pieces(head_bias[segment], head_starts, [local_hidden] * 4)
        hidden_state, stored = head_block(
            hidden_state, cond_act, head_all[segment], segment_bias, head_bias[segment, 4 * HW :]
        )
        stored_head.append(stored)
    shift_last = product(cond_act, final_shift) + rest_bias[4]
    scale_last = product(cond_act, final_scale) + rest_bias[5]
    final_in = narrow(modulate(hidden_state, shift_last, scale_last))
    predicted = product_right(final_in, output_weight)
    sq_error = jnp.mean((predicted - target) ** 2, axis=-1)
    numerator = jnp.sum(row_weight * sq_error)
    loss_sum = lax.psum(numerator, "dp")
    grad_pred = narrow(2.0 / (TOKD * weight_total) * row_weight[:, None] * (predicted - target))
    grad_output = product_left(grad_pred, final_in)
    grad_final = product(grad_pred, output_weight)
    grad_hidden, grad_shift_last, grad_scale_last = jax.vjp(
        modulate, hidden_state, shift_last, scale_last
    )[1](grad_final)
    grad_shift_last = narrow(grad_shift_last)
    grad_scale_last = narrow(grad_scale_last)
    cond_shared = product_right(grad_shift_last, final_shift) + product_right(
        grad_scale_last, final_scale
    )
    cond_split = jnp.zeros_like(cond_vec)
    head_grads = []
    head_bias_grads = []
    for segment in reversed(range(HB)):
        grad_hidden, grad_cond, grad_segment, grad_segment_bias, grad_last_bias = head_block_back(
            grad_hidden, cond_act, head_all[segment], offset, stored_head[segment]
        )
        cond_split = cond_split + grad_cond
        head_grads.insert(0, grad_segment)
        pieces = [
            grad_segment_bias[slot * local_hidden : (slot + 1) * local_hidden] for slot in range(4)
        ] + [grad_last_bias / tensor_size]
        head_bias_grads.insert(0, place_pieces(5 * HW, pieces, head_starts + [4 * HW]))
    grad_head = jnp.stack(head_grads)
    grad_input = narrow(grad_hidden)
    grad_cond_vec = narrow(local_back(jax.nn.silu, cond_vec, input_sum(cond_split) + cond_shared))
    cond_bias_grad = column_sum(grad_cond_vec)
    grad_time_act = product_right(grad_cond_vec, time_second)
    grad_time_pre = narrow(local_back(jax.nn.silu, time_pre, grad_time_act))
    grad_latent = jnp.sum(product(grad_cond_vec, cond_weight.T).reshape(COPIES, -1, D), axis=0)
    grad_rest = jnp.concatenate(
        [
            product_left(jnp.tile(latent, (COPIES, 1)), grad_cond_vec),
            product_left(noisy_rows, grad_input),
            grad_output,
            product_left(time_feat, grad_time_pre),
            product_left(time_act, grad_cond_vec),
            product_left(cond_act, grad_shift_last),
            product_left(cond_act, grad_scale_last),
        ],
        axis=0,
    )
    grad_rest_cols = lax.dynamic_slice_in_dim(grad_rest, offset, local_hidden, 1)
    rest_bias_grad = (
        jnp.stack(
            [
                cond_bias_grad,
                column_sum(grad_input),
                column_sum(grad_time_pre),
                cond_bias_grad,
                column_sum(grad_shift_last),
                column_sum(grad_scale_last),
            ]
        )
        / tensor_size
    )
    grad_top = jnp.concatenate(
        [jnp.zeros((images, BUF, D), jnp.float32), grad_latent.reshape(images, TOK, D)], axis=1
    )
    grad_decoded, grad_gain_dec, grad_shift_dec = jax.vjp(
        layer_norm, decoded, final_norms[2], final_norms[3]
    )[1](grad_top)
    grad_dec_in, grad_rows_dec, grad_bias_dec, grad_vec_dec = block_back(
        grad_decoded, visible_all, block_all[1], layer_vectors[1], stored_dec
    )
    grad_encoded, grad_gain_enc, grad_shift_enc = jax.vjp(
        layer_norm, encoded, final_norms[0], final_norms[1]
    )[1](grad_dec_in * (1.0 - hidden_rows))
    grad_stream, grad_rows_enc, grad_bias_enc, grad_vec_enc = block_back(
        grad_encoded, visible_enc, block_all[0], layer_vectors[0], stored_enc
    )
    grad_tokens = narrow(grad_stream[:, BUF:].reshape(-1, D))
    grad_tables = jnp.concatenate(
        [
            product_left(patch_flat, grad_tokens),
            column_sum(grad_tokens)[None],
            jnp.dot(picker.T, jnp.sum(grad_stream[:, :BUF], axis=1), precision=highest),
            jnp.sum(grad_stream, axis=0),
            jnp.sum(grad_dec_in, axis=0),
            jnp.sum(grad_dec_in * hidden_rows, axis=(0, 1))[None],
            jnp.stack([grad_vec_enc, grad_vec_dec]).reshape(6 * LAYERS, D),
            jnp.stack([grad_gain_enc, grad_shift_enc, grad_gain_dec, grad_shift_dec]),
        ],
        axis=0,
    )
    grad_blocks = jnp.stack([grad_rows_enc, grad_rows_dec])
    column_grads = []
    for grad_local in (grad_bias_enc, grad_bias_dec):
        pieces = [
            grad_local[slot * local_width : (slot + 1) * local_width] for slot in range(3)
        ] + [grad_local[3 * local_width :]]
        column_grads.append(place_pieces(3 * D + FF, pieces, column_starts))
    bias_local = jnp.concatenate(
        [
            rest_bias_grad.reshape(-1),
            jnp.concatenate(head_bias_grads),
            jnp.concatenate(column_grads),
        ]
    )
    bias_grad = lax.psum(bias_local, ("dp", "tensor")).reshape(bias_rows.shape)
    owned_blocks, owned_head = (
        lax.psum_scatter(grad_blocks, "dp", scatter_dimension=1, tiled=True),
        lax.psum_scatter(grad_head, "dp", scatter_dimension=1, tiled=True),
    )
    owned_rest, owned_tables = (
        lax.psum_scatter(grad_rest_cols, "dp", scatter_dimension=0, tiled=True),
        lax.psum_scatter(grad_tables.T, "dp", scatter_dimension=0, tiled=True),
    )
    split_squares = (
        jnp.sum(owned_blocks * owned_blocks)
        + jnp.sum(owned_head * owned_head)
        + jnp.sum(owned_rest * owned_rest)
    )
    shared_squares = jnp.sum(owned_tables * owned_tables) / tensor_size
    every_squares = jnp.sum(bias_grad * bias_grad) / (tensor_size * lax.axis_size("dp"))
    norm_square = lax.psum(split_squares + shared_squares + every_squares, ("dp", "tensor"))
    loss_value = loss_sum / weight_total
    grad_norm = jnp.sqrt(norm_square)
    factor = jnp.minimum(1.0, clip_limit / (grad_norm + 1e-06))
    step_num = step_count[0].astype(jnp.float32)
    blocks_new, blocks_first, blocks_second = adam_update(
        block_weights, first_blocks, second_blocks, owned_blocks, factor, step_num
    )
    head_new, head_first, head_second = adam_update(
        head_weights, first_head, second_head, owned_head, factor, step_num
    )
    rest_new, rest_first, rest_second = adam_update(
        head_rest, first_rest, second_rest, owned_rest, factor, step_num
    )
    tables_new, tables_first, tables_second = adam_update(
        embed_tables, first_tables, second_tables, owned_tables, factor, step_num
    )
    bias_new, bias_first, bias_second = adam_update(
        bias_rows, first_bias, second_bias, bias_grad, factor, step_num
    )
    return (
        loss_value,
        grad_norm,
        blocks_new,
        blocks_first,
        blocks_second,
        narrow(blocks_new),
        head_new,
        head_first,
        head_second,
        narrow(head_new),
        rest_new,
        rest_first,
        rest_second,
        narrow(rest_new),
        tables_new,
        tables_first,
        tables_second,
        narrow(tables_new),
        bias_new,
        bias_first,
        bias_second,
        narrow(bias_new),
    )


def solution(mesh):
    in_specs = (
        P(None, ("dp", "tensor"), None),
        P(None, ("dp", "tensor"), None),
        P("dp", "tensor"),
        P("dp", None),
        P(),
        P(None, ("dp", "tensor"), None),
        P(None, ("dp", "tensor"), None),
        P(None, ("dp", "tensor"), None),
        P(None, ("dp", "tensor"), None),
        P("dp", "tensor"),
        P("dp", "tensor"),
        P("dp", None),
        P("dp", None),
        P(),
        P(),
        P("dp", None, None),
        P(None, "dp", None, None),
        P("dp", None),
        P("dp"),
        P("dp"),
        P(None, "dp", None),
        P(),
        P(),
    )
    out_specs = (
        P(),
        P(),
        P(None, ("dp", "tensor"), None),
        P(None, ("dp", "tensor"), None),
        P(None, ("dp", "tensor"), None),
        P(None, ("dp", "tensor"), None),
        P(None, ("dp", "tensor"), None),
        P(None, ("dp", "tensor"), None),
        P(None, ("dp", "tensor"), None),
        P(None, ("dp", "tensor"), None),
        P("dp", "tensor"),
        P("dp", "tensor"),
        P("dp", "tensor"),
        P("dp", "tensor"),
        P("dp", None),
        P("dp", None),
        P("dp", None),
        P("dp", None),
        P(),
        P(),
        P(),
        P(),
    )
    return jax.shard_map(local, mesh=mesh, in_specs=in_specs, out_specs=out_specs, check_vma=False)
```

profile of v0, /device:TPU:0, one launch (start us, length us, event | category | flops | bytes accessed | tf_op | source)
XLA Modules:
  0.0 1997.0 jit_solution(7858391242031659642)
XLA Ops:
  12.2 90.2 %all-gather.16.cloned.1.call-done = f32[768,1723]{1,0:T(8,128)} async-done(((f32[96,1723]{1,0:T(8,128)}), f32[768,1723]{1,0:T(8,128)}) %all-gather.16.cloned.1.call-update) | async-done | bytes 5293072 | tf_op jit(solution)/shard_map/all_gather | solution.py:345
  102.4 6.1 copy.119
  117.1 95.1 %all-gather.18.cloned.1.call-done = bf16[2,2304,768]{2,1,0:T(8,128)(2,1)} async-done(((bf16[2,288,768]{2,1,0:T(8,128)(2,1)}), bf16[2,2304,768]{2,1,0:T(8,128)(2,1)}) %all-gather.18.cloned.1.call-update) | async-done | bytes 7077904 | tf_op jit(solution)/shard_map/all_gather | solution.py:340
  218.6 33.9 %all-reduce.19.cloned.1.call-done = f32[320,768]{1,0:T(8,128)} async-done(((f32[320,768]{1,0:T(8,128)}), f32[320,768]{1,0:T(8,128)}) %all-reduce.19.cloned.1.call-update) | async-done | bytes 983056 | tf_op jit(solution)/shard_map/psum | solution.py:92
  263.9 35.5 %all-reduce.21.cloned.1.call-done = f32[320,768]{1,0:T(8,128)} async-done(((f32[320,768]{1,0:T(8,128)}), f32[320,768]{1,0:T(8,128)}) %all-reduce.21.cloned.1.call-update) | async-done | bytes 983056 | tf_op jit(solution)/shard_map/psum | solution.py:92
  315.5 34.0 %all-reduce.23.cloned.1.call-done = f32[320,768]{1,0:T(8,128)} async-done(((f32[320,768]{1,0:T(8,128)}), f32[320,768]{1,0:T(8,128)}) %all-reduce.23.cloned.1.call-update) | async-done | bytes 983056 | tf_op jit(solution)/shard_map/psum | solution.py:92
  360.0 46.6 %all-gather.12.cloned.1.call-done = bf16[4992,256]{1,0:T(8,128)(2,1)} async-done(((bf16[624,256]{1,0:T(8,128)(2,1)}), bf16[4992,256]{1,0:T(8,128)(2,1)}) %all-gather.12.cloned.1.call-update) | async-done | bytes 2555920 | tf_op jit(solution)/shard_map/all_gather | solution.py:344
  413.2 30.8 %all-reduce.25.cloned.1.call-done = f32[320,768]{1,0:T(8,128)} async-done(((f32[320,768]{1,0:T(8,128)}), f32[320,768]{1,0:T(8,128)}) %all-reduce.25.cloned.1.call-update) | async-done | bytes 983056 | tf_op jit(solution)/shard_map/psum | solution.py:92
  447.6 68.2 %all-gather.14.cloned.1.call-done = bf16[4992,1024]{1,0:T(8,128)(2,1)} async-done(((bf16[4992,256]{1,0:T(8,128)(2,1)}), bf16[4992,1024]{1,0:T(8,128)(2,1)}) %all-gather.14.cloned.1.call-update) | async-done | bytes 10223632 | tf_op jit(solution)/shard_map/all_gather | solution.py:347
  524.1 80.8 %all-gather.20.cloned.1.call-done = bf16[2,1280,1024]{2,1,0:T(8,128)(2,1)} async-done(((bf16[2,160,1024]{2,1,0:T(8,128)(2,1)}), bf16[2,1280,1024]{2,1,0:T(8,128)(2,1)}) %all-gather.20.cloned.1.call-update) | async-done | bytes 5242896 | tf_op jit(solution)/shard_map/all_gather | solution.py:341
  614.4 8.5 all-gather.24.cloned.1.call-done
  622.9 18.9 all-gather.26.cloned.1.call-done
  660.6 39.1 %all-reduce.27.cloned.1.call-done = f32[256,1024]{1,0:T(8,128)} async-done(((f32[256,1024]{1,0:T(8,128)}), f32[256,1024]{1,0:T(8,128)}) %all-reduce.27.cloned.1.call-update) | async-done | bytes 1048592 | tf_op jit(solution)/shard_map/psum | solution.py:92
  704.1 14.8 all-gather.30.cloned.1.call-done
  718.9 18.8 all-gather.32.cloned.1.call-done
  749.7 6.8 all-gather.28.cloned.1.call-done
  756.5 38.4 %all-reduce.29.cloned.1.call-done = f32[256,1024]{1,0:T(8,128)} async-done(((f32[256,1024]{1,0:T(8,128)}), f32[256,1024]{1,0:T(8,128)}) %all-reduce.29.cloned.1.call-update) | async-done | bytes 1048592 | tf_op jit(solution)/shard_map/psum | solution.py:92
  805.2 22.0 %all-reduce.3 = (f32[]{:T(128)}, f32[]{:T(128)}) all-reduce(f32[]{:T(128)} %get-tuple-element.66, f32[]{:T(128)} %get-tuple-element.65), channel_id=1, replica_groups=mesh['dp'=8,'tensor'=4] {'dp'}, use_global_device_ids=true, to_apply=%region_31.32 | all-reduce | flops 2 | bytes 16 | tf_op jit(solution)/shard_map/psum | solution.py:428
  847.0 24.6 %all-reduce.31.cloned.1.call-done = bf16[256,1024]{1,0:T(8,128)(2,1)} async-done(((bf16[256,1024]{1,0:T(8,128)(2,1)}), bf16[256,1024]{1,0:T(8,128)(2,1)}) %all-reduce.31.cloned.1.call-update) | async-done | bytes 524304 | tf_op jit(solution)/shard_map/psum | solution.py:96
  889.1 28.7 %all-reduce.33.cloned.1.call-done = bf16[256,1024]{1,0:T(8,128)(2,1)} async-done(((bf16[256,1024]{1,0:T(8,128)(2,1)}), bf16[256,1024]{1,0:T(8,128)(2,1)}) %all-reduce.33.cloned.1.call-update) | async-done | bytes 524304 | tf_op jit(solution)/shard_map/psum | solution.py:96
  940.0 27.5 %all-reduce.35.cloned.1.call-done = bf16[256,1024]{1,0:T(8,128)(2,1)} async-done(((bf16[256,1024]{1,0:T(8,128)(2,1)}), bf16[256,1024]{1,0:T(8,128)(2,1)}) %all-reduce.35.cloned.1.call-update) | async-done | bytes 524304 | tf_op jit(solution)/shard_map/psum | solution.py:96
  1013.8 14.7 all-reduce.37.cloned.1.call-done
  1043.6 31.2 %all-reduce.39.cloned.1.call-done = bf16[320,768]{1,0:T(8,128)(2,1)} async-done(((bf16[320,768]{1,0:T(8,128)(2,1)}), bf16[320,768]{1,0:T(8,128)(2,1)}) %all-reduce.39.cloned.1.call-update) | async-done | bytes 491536 | tf_op jit(solution)/shard_map/psum | solution.py:96
  1091.6 32.3 %all-reduce.41.cloned.1.call-done = bf16[320,768]{1,0:T(8,128)(2,1)} async-done(((bf16[320,768]{1,0:T(8,128)(2,1)}), bf16[320,768]{1,0:T(8,128)(2,1)}) %all-reduce.41.cloned.1.call-update) | async-done | bytes 491536 | tf_op jit(solution)/shard_map/psum | solution.py:96
  1193.9 9.0 concatenate.84
  1233.2 11.0 pad_maximum_fusion
  1245.0 52.4 %all-reduce.45.cloned.1.call-done = f32[27136]{0:T(1024)} async-done(((f32[27136]{0:T(1024)}), f32[27136]{0:T(1024)}) %all-reduce.45.cloned.1.call-update) | async-done | bytes 108560 | tf_op jit(solution)/shard_map/psum | solution.py:529
  1299.6 103.1 %reduce-scatter.9.cloned.1.call-done = f32[624,256]{1,0:T(8,128)} async-done(((f32[4992,256]{1,0:T(8,128)}), f32[624,256]{1,0:T(8,128)}) %reduce-scatter.9.cloned.1.call-update) | async-done | bytes 638992 | tf_op jit(solution)/shard_map/reduce_scatter | solution.py:535
  1404.6 107.7 %reduce-scatter.11.cloned.1.call-done = f32[96,1723]{1,0:T(8,128)} async-done(((f32[768,1723]{1,0:T(8,128)}), f32[96,1723]{1,0:T(8,128)}) %reduce-scatter.11.cloned.1.call-update) | async-done | bytes 661648 | tf_op jit(solution)/shard_map/reduce_scatter | solution.py:536
  1514.9 179.2 %reduce-scatter.7.cloned.1.call-done = f32[2,160,1024]{2,1,0:T(8,128)} async-done(((f32[2,1280,1024]{2,1,0:T(8,128)}), f32[2,160,1024]{2,1,0:T(8,128)}) %reduce-scatter.7.cloned.1.call-update) | async-done | bytes 1310736 | tf_op jit(solution)/shard_map/reduce_scatter | solution.py:532
  1696.3 230.2 %reduce-scatter.5.cloned.1.call-done = f32[2,288,768]{2,1,0:T(8,128)} async-done(((f32[2,2304,768]{2,1,0:T(8,128)}), f32[2,288,768]{2,1,0:T(8,128)}) %reduce-scatter.5.cloned.1.call-update) | async-done | bytes 1769488 | tf_op jit(solution)/shard_map/reduce_scatter | solution.py:531
  1932.4 39.6 %psum.135 = f32[]{:T(128)} all-reduce(f32[]{:T(128)S(6)} %add.850), channel_id=1, replica_groups=mesh['dp'=8,'tensor'=4] {'dp','tensor'}, use_global_device_ids=true, to_apply=%region_105.106 | all-reduce | flops 1 | bytes 8 | tf_op jit(solution)/shard_map/psum | solution.py:545
  (870 shorter events, 389.3 us)
Async XLA Ops:
  7.2 95.2 %all-gather.16.cloned.1.call-start = ((), (), s32[]{:S(2)}) async-start(), calls=%async_computation.6 | async-start | bytes 6193152 | tf_op jit(solution)/shard_map/all_gather | solution.py:345
  7.9 204.3 %all-gather.18.cloned.1.call-start = ((), (), s32[]{:S(2)}) async-start(), calls=%async_computation.7 | async-start | bytes 7962624 | tf_op jit(solution)/shard_map/all_gather | solution.py:340
  10.5 242.0 %all-reduce.19.cloned.1.call-start = ((), (), s32[]{:S(2)}) async-start(), calls=%async_computation.8 | async-start | bytes 1966080 | tf_op jit(solution)/shard_map/psum | solution.py:92
  110.6 922.7 %copy-start.138 = (f32[768]{0:T(1024)}, f32[768]{0:T(1024)S(1)}, u32[]{:S(2)}) copy-start(f32[768]{0:T(1024)S(1)} %get-tuple-element.26) | copy-start | bytes 9220
  218.5 81.0 %all-reduce.21.cloned.1.call-start = ((), (), s32[]{:S(2)}) async-start(), calls=%async_computation.9 | async-start | bytes 1966080 | tf_op jit(solution)/shard_map/psum | solution.py:92
  263.4 86.1 %all-reduce.23.cloned.1.call-start = ((), (), s32[]{:S(2)}) async-start(), calls=%async_computation.10 | async-start | bytes 1966080 | tf_op jit(solution)/shard_map/psum | solution.py:92
  313.4 93.2 %all-gather.12.cloned.1.call-start = ((), (), s32[]{:S(2)}) async-start(), calls=%async_computation.4 | async-start | bytes 2875392 | tf_op jit(solution)/shard_map/all_gather | solution.py:344
  315.3 128.6 %all-reduce.25.cloned.1.call-start = ((), (), s32[]{:S(2)}) async-start(), calls=%async_computation.11 | async-start | bytes 1966080 | tf_op jit(solution)/shard_map/psum | solution.py:92
  350.9 682.4 %copy-start.149 = (f32[320]{0:T(512)}, f32[320]{0:T(512)S(1)}, u32[]{:S(2)}) copy-start(f32[320]{0:T(512)S(1)} %broadcast_multiply_fusion.3) | copy-start | bytes 3844
  359.9 155.9 %all-gather.14.cloned.1.call-start = ((), (), s32[]{:S(2)}) async-start(), calls=%async_computation.5 | async-start | bytes 12779520 | tf_op jit(solution)/shard_map/all_gather | solution.py:347
  406.6 198.3 %all-gather.20.cloned.1.call-start = ((), (), s32[]{:S(2)}) async-start(), calls=%async_computation.12 | async-start | bytes 5898240 | tf_op jit(solution)/shard_map/all_gather | solution.py:341
  408.9 214.0 %all-gather.24.cloned.1.call-start = ((), (), s32[]{:S(2)}) async-start(), calls=%async_computation.14 | async-start | bytes 1310720 | tf_op jit(solution)/shard_map/all_gather | solution.py:244
  607.9 34.0 %all-gather.26.cloned.1.call-start = ((), (), s32[]{:S(2)}) async-start(), calls=%async_computation.15 | async-start | bytes 1310720 | tf_op jit(solution)/shard_map/all_gather | solution.py:243
  608.6 52.0 %all-gather.22.cloned.1.call-start = ((), (), s32[]{:S(2)}) async-start(), calls=%async_computation.13 | async-start | bytes 1310720 | tf_op jit(solution)/shard_map/all_gather | solution.py:245
  611.2 88.4 %all-reduce.27.cloned.1.call-start = ((), (), s32[]{:S(2)}) async-start(), calls=%async_computation.16 | async-start | bytes 2097152 | tf_op jit(solution)/shard_map/psum | solution.py:92
  650.2 68.6 %all-gather.30.cloned.1.call-start = ((), (), s32[]{:S(2)}) async-start(), calls=%async_computation.18 | async-start | bytes 1310720 | tf_op jit(solution)/shard_map/all_gather | solution.py:244
  653.3 84.4 %all-gather.32.cloned.1.call-start = ((), (), s32[]{:S(2)}) async-start(), calls=%async_computation.19 | async-start | bytes 1310720 | tf_op jit(solution)/shard_map/all_gather | solution.py:243
  653.9 102.7 %all-gather.28.cloned.1.call-start = ((), (), s32[]{:S(2)}) async-start(), calls=%async_computation.17 | async-start | bytes 1310720 | tf_op jit(solution)/shard_map/all_gather | solution.py:245
  658.1 136.8 %all-reduce.29.cloned.1.call-start = ((), (), s32[]{:S(2)}) async-start(), calls=%async_computation.20 | async-start | bytes 2097152 | tf_op jit(solution)/shard_map/psum | solution.py:92
  746.2 125.4 %all-reduce.31.cloned.1.call-start = ((), (), s32[]{:S(2)}) async-start(), calls=%async_computation.21 | async-start | bytes 1048576 | tf_op jit(solution)/shard_map/psum | solution.py:96
  841.5 76.3 %all-reduce.33.cloned.1.call-start = ((), (), s32[]{:S(2)}) async-start(), calls=%async_computation.22 | async-start | bytes 1048576 | tf_op jit(solution)/shard_map/psum | solution.py:96
  884.4 83.0 %all-reduce.35.cloned.1.call-start = ((), (), s32[]{:S(2)}) async-start(), calls=%async_computation.23 | async-start | bytes 1048576 | tf_op jit(solution)/shard_map/psum | solution.py:96
  934.1 94.5 %all-reduce.37.cloned.1.call-start = ((), (), s32[]{:S(2)}) async-start(), calls=%async_computation.24 | async-start | bytes 983040 | tf_op jit(solution)/shard_map/psum | solution.py:96
  995.5 79.3 %all-reduce.39.cloned.1.call-start = ((), (), s32[]{:S(2)}) async-start(), calls=%async_computation.25 | async-start | bytes 983040 | tf_op jit(solution)/shard_map/psum | solution.py:96
  1041.6 82.2 %all-reduce.41.cloned.1.call-start = ((), (), s32[]{:S(2)}) async-start(), calls=%async_computation.26 | async-start | bytes 983040 | tf_op jit(solution)/shard_map/psum | solution.py:96
  1090.5 80.0 %all-reduce.43.cloned.1.call-start = ((), (), s32[]{:S(2)}) async-start(), calls=%async_computation.30 | async-start | bytes 983040 | tf_op jit(solution)/shard_map/psum | solution.py:96
  1137.4 160.0 %all-reduce.45.cloned.1.call-start = ((), (), s32[]{:S(2)}) async-start(), calls=%async_computation.32 | async-start | bytes 221184 | tf_op jit(solution)/shard_map/psum | solution.py:529
  1143.5 259.3 %reduce-scatter.9.cloned.1.call-start = ((), (), s32[]{:S(2)}) async-start(), calls=%async_computation.29 | async-start | bytes 5750784 | tf_op jit(solution)/shard_map/reduce_scatter | solution.py:535
  1148.6 363.6 %reduce-scatter.11.cloned.1.call-start = ((), (), s32[]{:S(2)}) async-start(), calls=%async_computation.31 | async-start | bytes 6193152 | tf_op jit(solution)/shard_map/reduce_scatter | solution.py:536
  1202.9 491.2 %reduce-scatter.7.cloned.1.call-start = ((), (), s32[]{:S(2)}) async-start(), calls=%async_computation.28 | async-start | bytes 11796480 | tf_op jit(solution)/shard_map/reduce_scatter | solution.py:532
  1215.0 711.5 %reduce-scatter.5.cloned.1.call-start = ((), (), s32[]{:S(2)}) async-start(), calls=%async_computation.27 | async-start | bytes 15925248 | tf_op jit(solution)/shard_map/reduce_scatter | solution.py:531
  1299.6 673.2 %copy-start.110 = (f32[212,128]{1,0:T(8,128)S(1)}, f32[212,128]{1,0:T(8,128)}, u32[]{:S(2)}) copy-start(f32[212,128]{1,0:T(8,128)} %param.27) | copy-start | bytes 325636
  (256 other events, 6195.8 us)
Sparse Core Ops, SparseCore 0:
  10.2 92.1 all-gather.15
  105.2 106.9 all-gather.17
  218.6 33.8 all-reduce.18
  263.5 35.8 all-reduce.20
  313.5 35.8 all-reduce.22
  352.3 54.2 all-gather.11
  409.7 34.2 all-reduce.24
  445.5 70.3 all-gather.13
  518.6 86.2 all-gather.19
  608.0 14.8 all-gather.23
  625.1 16.7 all-gather.25
  643.8 16.7 all-gather.21
  663.5 36.0 all-reduce.26
  701.7 17.0 all-gather.29
  720.9 16.7 all-gather.31
  739.8 16.7 all-gather.27
  758.9 36.0 all-reduce.28
  841.6 29.9 all-reduce.30
  884.5 33.1 all-reduce.32
  934.2 33.1 all-reduce.34
  995.6 32.9 all-reduce.36
  1041.7 33.0 all-reduce.38
  1090.6 33.1 all-reduce.40
  1137.5 33.0 all-reduce.42
  1176.7 120.6 all-reduce.44
  1300.9 101.7 reduce-scatter.8
  1406.2 106.0 reduce-scatter.10
  1516.3 177.7 reduce-scatter.6
  1698.2 228.3 reduce-scatter.4
where the time goes:
time: 2010 us; the launch traced here: 2000 us
  waiting for transfers between devices  1500 us (75%)
  other arithmetic  154 us (8%)
  matrix products  146 us (7%)
  local copies, waits for them, and re-layouts  101 us (5%)
  blocking collectives  61.6 us (3%)
  between operations  27.7 us (1%)
    reduce_scatter x1, waiting for transfers between devices, local(): lax.psum_scatter(grad_blocks, 'dp', scatter_dimension=1, tiled=True)  230 us
    psum x6, waiting for transfers between devices, branch_sum(): return lax.psum(partial_term, 'tensor')  212 us
    reduce_scatter x1, waiting for transfers between devices, local(): lax.psum_scatter(grad_head, 'dp', scatter_dimension=1, tiled=True)  179 us
    psum x7, waiting for transfers between devices, input_sum(): lax.psum(partial_term.astype(jnp.bfloat16), 'tensor').astype(jnp.float32)  165 us
    reduce_scatter x1, waiting for transfers between devices, local(): lax.psum_scatter(grad_tables.T, 'dp', scatter_dimension=0, tiled=True)  108 us
    reduce_scatter x1, waiting for transfers between devices, local(): lax.psum_scatter(grad_rest_cols, 'dp', scatter_dimension=0, tiled=True)  103 us
    all_gather x1, waiting for transfers between devices, local(): lax.all_gather(narrow(block_weights), 'dp', axis=1, tiled=True)  95.1 us
    all_gather x1, waiting for transfers between devices, local(): lax.all_gather(embed_tables, 'dp', axis=0, tiled=True)  90.2 us
  transfers between devices with their start and end apart: 29, of which 29 were waited for; matrix products, arithmetic and copies ran while one was open for 11% of the time, Pallas kernels for 0%

commit v1 on v0

--- a/solution.py
+++ b/solution.py
@@ -88,12 +88,111 @@
     return jnp.sum(inputs.astype(jnp.float32), axis=0)
 
 
+def swap(value, axis, step):
+    return lax.ppermute(value, axis, [(i, i ^ step) for i in range(lax.axis_size(axis))])
+
+
+def tensor_sum(partial_term, cross_type):
+    if lax.axis_size("tensor") != 4:
+        return lax.psum(partial_term, "tensor")
+    low = lax.axis_index("tensor") % 2
+    half = partial_term.shape[0] // 2
+    keep = lax.dynamic_slice_in_dim(partial_term, low * half, half, 0)
+    give = lax.dynamic_slice_in_dim(partial_term, (1 - low) * half, half, 0)
+    pair = (keep + swap(give, "tensor", 1)).astype(cross_type)
+    total = pair.astype(jnp.float32) + swap(pair, "tensor", 2).astype(jnp.float32)
+    back = swap(total, "tensor", 1)
+    first = jnp.where(low == 0, total, back)
+    second = jnp.where(low == 0, back, total)
+    return jnp.concatenate([first, second], axis=0)
+
+
 def branch_sum(partial_term):
-    return lax.psum(partial_term, "tensor")
+    return tensor_sum(partial_term, jnp.float32)
 
 
 def input_sum(partial_term):
-    return lax.psum(partial_term.astype(jnp.bfloat16), "tensor").astype(jnp.float32)
+    return tensor_sum(partial_term, jnp.bfloat16)
+
+
+def tensor_blocks(piece):
+    if lax.axis_size("tensor") != 4:
+        return list(lax.all_gather(piece, "tensor"))
+    rank = lax.axis_index("tensor")
+    near = swap(piece, "tensor", 1)
+    far = swap(piece, "tensor", 2)
+    cross = swap(far, "tensor", 1)
+    blocks = []
+    for index in range(4):
+        same_pair = jnp.where(rank == index, piece, near)
+        other_pair = jnp.where(rank == index ^ 2, far, cross)
+        blocks.append(jnp.where(rank // 2 == index // 2, same_pair, other_pair))
+    return blocks
+
+
+def tensor_columns(piece):
+    return jnp.concatenate(tensor_blocks(piece), axis=1)
+
+
+def sum_everywhere(value, axes):
+    for axis in axes:
+        step = 1
+        while step < lax.axis_size(axis):
+            value = value + swap(value, axis, step)
+            step = 2 * step
+    return value
+
+
+def pick(blocks, index):
+    return lax.dynamic_index_in_dim(blocks, index, 0, keepdims=False)
+
+
+def coded(values, level):
+    body = (values * jnp.exp2(13.0 - level)).astype(jnp.float16)
+    return jnp.concatenate([body, jnp.full((16, values.shape[1]), level).astype(jnp.float16)])
+
+
+def decoded(message):
+    level = message[-1, 0].astype(jnp.float32)
+    return message[:-16].astype(jnp.float32) * jnp.exp2(level - 13.0), level
+
+
+def scatter_sum(grad):
+    if lax.axis_size("dp") != 8:
+        return lax.psum_scatter(grad, "dp", scatter_dimension=0, tiled=True)
+    rank = lax.axis_index("dp")
+    low, high = rank % 2, rank // 2
+    slab, columns = grad.shape[0] // 8, grad.shape[1]
+    blocks = grad.reshape(4, 2 * slab, columns)
+    peak = jnp.maximum(jnp.max(jnp.abs(grad)), 2.0**-100)
+    level = jnp.ceil(jnp.log2(peak))
+    keep = lax.dynamic_slice_in_dim(blocks, low * slab, slab, 1)
+    give = lax.dynamic_slice_in_dim(blocks, (1 - low) * slab, slab, 1)
+    got, got_level = decoded(swap(coded(give.reshape(4 * slab, columns), level), "dp", 1))
+    pairs = keep + got.reshape(4, slab, columns)
+    level = jnp.maximum(level, got_level) + 1.0
+    total = pick(pairs, high)
+    arrived = [
+        decoded(swap(coded(pick(pairs, high ^ step), level), "dp", 2 * step))[0]
+        for step in (1, 2, 3)
+    ]
+    return total + arrived[0] + arrived[1] + arrived[2]
+
+
+def scatter_small(grad):
+    if lax.axis_size("dp") != 8:
+        return lax.psum_scatter(grad, "dp", scatter_dimension=0, tiled=True)
+    rank = lax.axis_index("dp")
+    low, high = rank % 2, rank // 2
+    slab, columns = grad.shape[0] // 8, grad.shape[1]
+    blocks = grad.reshape(4, 2 * slab, columns)
+    keep = lax.dynamic_slice_in_dim(blocks, low * slab, slab, 1)
+    give = lax.dynamic_slice_in_dim(blocks, (1 - low) * slab, slab, 1)
+    pairs = keep + swap(give, "dp", 1)
+    total = pick(pairs, high)
+    for step in (1, 2, 3):
+        total = total + swap(pick(pairs, high ^ step), "dp", 2 * step)
+    return total
 
 
 def take_pieces(vector, starts, counts):
@@ -234,16 +333,26 @@
     return ((grad_middle + grad_flat).reshape(incoming.shape), grad_rows, grad_bias, grad_vectors)
 
 
-def head_block(hidden_state, cond_act, segment_rows, segment_bias, last_bias):
+def gathered_parts(columns, count):
+    width = columns.shape[1] // count
+    blocks = tensor_blocks(columns)
+    return [
+        jnp.concatenate([block[:, slot * width : (slot + 1) * width] for block in blocks], axis=1)
+        for slot in range(count)
+    ]
+
+
+def adaptive_vectors(cond_act, segment_rows, segment_bias):
     local_hidden = HW // lax.axis_size("tensor")
     adaptive = (
         product_right(cond_act, segment_rows[: 3 * local_hidden]) + segment_bias[: 3 * local_hidden]
     )
-    shift_vec, scale_vec, gate_vec = (
-        lax.all_gather(adaptive[:, :local_hidden], "tensor", axis=1, tiled=True),
-        lax.all_gather(adaptive[:, local_hidden : 2 * local_hidden], "tensor", axis=1, tiled=True),
-        lax.all_gather(adaptive[:, 2 * local_hidden :], "tensor", axis=1, tiled=True),
-    )
+    return gathered_parts(adaptive, 3)
+
+
+def head_block(hidden_state, vectors, segment_rows, segment_bias, last_bias):
+    local_hidden = HW // lax.axis_size("tensor")
+    shift_vec, scale_vec, gate_vec = vectors
     modulated = narrow(modulate(hidden_state, shift_vec, scale_vec))
     inner = (
         product_right(modulated, segment_rows[3 * local_hidden : 4 * local_hidden])
@@ -336,38 +445,68 @@
     ]
     column_counts = [local_width] * 3 + [local_ff]
     head_starts = [slot * HW + offset for slot in range(4)]
-    block_all, head_all = (
-        lax.all_gather(narrow(block_weights), "dp", axis=1, tiled=True),
-        lax.all_gather(narrow(head_weights), "dp", axis=1, tiled=True),
-    )
-    rest_rows, table_cols = (
-        lax.all_gather(head_rest, "dp", axis=0, tiled=True),
-        lax.all_gather(embed_tables, "dp", axis=0, tiled=True),
-    )
-    rest_all = lax.all_gather(narrow(rest_rows), "tensor", axis=1, tiled=True)
-    rest_parts = cut_rows(rest_all, (D, TOKD, TOKD, HW, HW, HW, HW))
-    cond_weight, input_weight, output_weight, time_first, time_second, final_shift, final_scale = [
-        narrow(piece) for piece in rest_parts
+    dp_size = lax.axis_size("dp")
+    dp_index = lax.axis_index("dp")
+    images = patches.shape[0]
+    all_images = dp_size * images
+    mask_float = token_mask.astype(jnp.float32)
+    matches = timesteps[..., None] == jnp.arange(T_STEPS)
+    row_weight = (
+        jnp.sum(jnp.where(matches, step_weights, 0.0), axis=-1) * mask_float[None]
+    ).reshape(-1)
+    chosen = jnp.where(drop_marks == 1, CLASSES, labels)
+    shared_values = lax.dynamic_update_slice_in_dim(
+        jnp.zeros((all_images,), jnp.float32), chosen.astype(jnp.float32), dp_index * images, 0
+    )
+    shared_values = sum_everywhere(
+        jnp.concatenate([shared_values, jnp.sum(row_weight)[None]]), ("dp",)
+    )
+    weight_total = shared_values[all_images]
+    picker = (shared_values[:all_images, None] == jnp.arange(CLASSES + 1)[None, :]).astype(
+        jnp.float32
+    )
+    class_at = TOKD + 1
+    class_end = class_at + CLASSES + 1
+    table_share = jnp.concatenate(
+        [
+            embed_tables[:, :class_at],
+            embed_tables[:, class_end:],
+            lax.dot_general(
+                embed_tables[:, class_at:class_end],
+                picker,
+                (((1,), (1,)), ((), ())),
+                precision=highest,
+            ),
+        ],
+        axis=1,
+    )
+    block_share = narrow(block_weights)
+    block_all = [lax.all_gather(block_share[0], "dp", axis=0, tiled=True)]
+    table_cols = lax.all_gather(table_share, "dp", axis=0, tiled=True)
+    for layer in range(1, LAYERS):
+        block_all.append(lax.all_gather(block_share[layer], "dp", axis=0, tiled=True))
+    rest_rows = lax.all_gather(narrow(head_rest), "dp", axis=0, tiled=True)
+    head_share = narrow(head_weights)
+    head_all = [
+        lax.all_gather(head_share[segment], "dp", axis=0, tiled=True) for segment in range(HB)
     ]
+    cond_mine, input_mine, output_mine, time_first, second_mine, final_shift, final_scale = cut_rows(
+        rest_rows, (D, TOKD, TOKD, HW, HW, HW, HW)
+    )
+    cond_weight, input_weight, output_weight, time_second = cut_rows(
+        tensor_columns(jnp.concatenate([cond_mine, input_mine, output_mine, second_mine], axis=0)),
+        (D, TOKD, TOKD, HW),
+    )
     flat_bias = bias_rows.reshape(-1)
     rest_bias = flat_bias[: 6 * HW].reshape(6, HW)
     head_bias = flat_bias[6 * HW : 6 * HW + 5 * HB * HW].reshape(HB, 5 * HW)
     column_bias = flat_bias[6 * HW + 5 * HB * HW :].reshape(LAYERS, 3 * D + FF)
     table_parts = cut_rows(
-        table_cols.T, (TOKD, 1, CLASSES + 1, TOK + BUF, TOK + BUF, 1, 6 * LAYERS, 4)
-    )
-    layer_vectors = table_parts[6].reshape(LAYERS, 6, D)
-    final_norms = table_parts[7]
-    images = patches.shape[0]
-    mask_float = token_mask.astype(jnp.float32)
-    matches = timesteps[..., None] == jnp.arange(T_STEPS)
-    row_weight = (
-        jnp.sum(jnp.where(matches, step_weights, 0.0), axis=-1) * mask_float[None]
-    ).reshape(-1)
-    weight_total = lax.psum(jnp.sum(row_weight), "dp")
-    chosen = jnp.where(drop_marks == 1, CLASSES, labels)
-    picker = (chosen[:, None] == jnp.arange(CLASSES + 1)[None, :]).astype(jnp.float32)
-    class_rows = jnp.dot(picker, table_parts[2], precision=highest)
+        table_cols.T, (TOKD, 1, TOK + BUF, TOK + BUF, 1, 6 * LAYERS, 4, all_images)
+    )
+    layer_vectors = table_parts[5].reshape(LAYERS, 6, D)
+    final_norms = table_parts[6]
+    class_rows = lax.dynamic_slice_in_dim(table_parts[7], dp_index * images, images, 0)
     patch_flat = patches.reshape(-1, TOKD)
     tokens = product(patch_flat, narrow(table_parts[0])) + table_parts[1][0]
     stream = (
@@ -378,7 +517,7 @@
             ],
             axis=1,
         )
-        + table_parts[3]
+        + table_parts[2]
     )
     buffer_ones = jnp.ones((images, BUF), jnp.float32)
     visible_enc = jnp.concatenate([buffer_ones, 1.0 - mask_float], axis=1)
@@ -391,7 +530,7 @@
         stream, visible_enc, block_all[0], layer_bias[0], layer_vectors[0]
     )
     enc_normed = layer_norm(encoded, final_norms[0], final_norms[1])
-    decoder_in = enc_normed * (1.0 - hidden_rows) + table_parts[5][0] * hidden_rows + table_parts[4]
+    decoder_in = enc_normed * (1.0 - hidden_rows) + table_parts[4][0] * hidden_rows + table_parts[3]
     decoded, stored_dec = block_forward(
         decoder_in, visible_all, block_all[1], layer_bias[1], layer_vectors[1]
     )
@@ -399,8 +538,10 @@
     condition = product(latent, cond_weight) + rest_bias[0]
     step_rows = timesteps.reshape(COPIES, -1)
     time_feat = narrow(sinusoid(step_rows).reshape(-1, HW))
-    time_pre = product(time_feat, time_first) + rest_bias[2]
-    time_act = narrow(jax.nn.silu(time_pre))
+    time_pre = product(time_feat, time_first) + lax.dynamic_slice_in_dim(
+        rest_bias[2], offset, local_hidden
+    )
+    time_act = tensor_columns(narrow(jax.nn.silu(time_pre)))
     time_embed = product(time_act, time_second) + rest_bias[3]
     cond_vec = (condition[None] + time_embed.reshape(COPIES, -1, HW)).reshape(-1, HW)
     cond_act = narrow(jax.nn.silu(cond_vec))
@@ -413,31 +554,44 @@
     target = (signal_coef * noise_rows - noise_coef * clean).reshape(-1, TOKD)
     hidden_state = product(noisy_rows, input_weight) + rest_bias[1]
     stored_head = []
+    segment_biases = [
+        take_pieces(head_bias[segment], head_starts, [local_hidden] * 4) for segment in range(HB)
+    ]
+    head_vectors = [
+        adaptive_vectors(cond_act, head_all[segment], segment_biases[segment])
+        for segment in range(HB)
+    ]
+    last_pair = jnp.concatenate(
+        [product(cond_act, final_shift), product(cond_act, final_scale)], axis=1
+    ) + take_pieces(flat_bias, [4 * HW + offset, 5 * HW + offset], [local_hidden] * 2)
+    shift_last, scale_last = gathered_parts(last_pair, 2)
     for segment in range(HB):
-        segment_bias = take_pieces(head_bias[segment], head_starts, [local_hidden] * 4)
         hidden_state, stored = head_block(
-            hidden_state, cond_act, head_all[segment], segment_bias, head_bias[segment, 4 * HW :]
+            hidden_state,
+            head_vectors[segment],
+            head_all[segment],
+            segment_biases[segment],
+            head_bias[segment, 4 * HW :],
         )
         stored_head.append(stored)
-    shift_last = product(cond_act, final_shift) + rest_bias[4]
-    scale_last = product(cond_act, final_scale) + rest_bias[5]
     final_in = narrow(modulate(hidden_state, shift_last, scale_last))
     predicted = product_right(final_in, output_weight)
     sq_error = jnp.mean((predicted - target) ** 2, axis=-1)
     numerator = jnp.sum(row_weight * sq_error)
-    loss_sum = lax.psum(numerator, "dp")
     grad_pred = narrow(2.0 / (TOKD * weight_total) * row_weight[:, None] * (predicted - target))
-    grad_output = product_left(grad_pred, final_in)
     grad_final = product(grad_pred, output_weight)
     grad_hidden, grad_shift_last, grad_scale_last = jax.vjp(
         modulate, hidden_state, shift_last, scale_last
     )[1](grad_final)
-    grad_shift_last = narrow(grad_shift_last)
-    grad_scale_last = narrow(grad_scale_last)
-    cond_shared = product_right(grad_shift_last, final_shift) + product_right(
+
+    def own_columns(value):
+        return lax.dynamic_slice_in_dim(value, offset, local_hidden, 1)
+
+    grad_shift_last = narrow(own_columns(grad_shift_last))
+    grad_scale_last = narrow(own_columns(grad_scale_last))
+    cond_split = product_right(grad_shift_last, final_shift) + product_right(
         grad_scale_last, final_scale
     )
-    cond_split = jnp.zeros_like(cond_vec)
     head_grads = []
     head_bias_grads = []
     for segment in reversed(range(HB)):
@@ -450,39 +604,41 @@
             grad_segment_bias[slot * local_hidden : (slot + 1) * local_hidden] for slot in range(4)
         ] + [grad_last_bias / tensor_size]
         head_bias_grads.insert(0, place_pieces(5 * HW, pieces, head_starts + [4 * HW]))
-    grad_head = jnp.stack(head_grads)
     grad_input = narrow(grad_hidden)
-    grad_cond_vec = narrow(local_back(jax.nn.silu, cond_vec, input_sum(cond_split) + cond_shared))
+    grad_cond_vec = narrow(local_back(jax.nn.silu, cond_vec, input_sum(cond_split)))
     cond_bias_grad = column_sum(grad_cond_vec)
-    grad_time_act = product_right(grad_cond_vec, time_second)
+    grad_time_act = product_right(
+        grad_cond_vec, lax.dynamic_slice_in_dim(time_second, offset, local_hidden, 0)
+    )
     grad_time_pre = narrow(local_back(jax.nn.silu, time_pre, grad_time_act))
     grad_latent = jnp.sum(product(grad_cond_vec, cond_weight.T).reshape(COPIES, -1, D), axis=0)
+    grad_cond_mine = own_columns(grad_cond_vec)
     grad_rest = jnp.concatenate(
         [
-            product_left(jnp.tile(latent, (COPIES, 1)), grad_cond_vec),
-            product_left(noisy_rows, grad_input),
-            grad_output,
+            product_left(jnp.tile(latent, (COPIES, 1)), grad_cond_mine),
+            product_left(noisy_rows, own_columns(grad_input)),
+            product_left(grad_pred, own_columns(final_in)),
             product_left(time_feat, grad_time_pre),
-            product_left(time_act, grad_cond_vec),
+            product_left(time_act, grad_cond_mine),
             product_left(cond_act, grad_shift_last),
             product_left(cond_act, grad_scale_last),
         ],
         axis=0,
     )
-    grad_rest_cols = lax.dynamic_slice_in_dim(grad_rest, offset, local_hidden, 1)
-    rest_bias_grad = (
-        jnp.stack(
-            [
-                cond_bias_grad,
-                column_sum(grad_input),
-                column_sum(grad_time_pre),
-                cond_bias_grad,
-                column_sum(grad_shift_last),
-                column_sum(grad_scale_last),
-            ]
-        )
-        / tensor_size
-    )
+    rest_bias_grad = place_pieces(
+        6 * HW,
+        [
+            cond_bias_grad / tensor_size,
+            column_sum(grad_input) / tensor_size,
+            column_sum(grad_time_pre),
+            cond_bias_grad / tensor_size,
+            column_sum(grad_shift_last),
+            column_sum(grad_scale_last),
+        ],
+        [0, HW, 2 * HW + offset, 3 * HW, 4 * HW + offset, 5 * HW + offset],
+    )
+    owned_head = jnp.stack([scatter_sum(grad) for grad in head_grads])
+    owned_rest = scatter_sum(grad_rest)
     grad_top = jnp.concatenate(
         [jnp.zeros((images, BUF, D), jnp.float32), grad_latent.reshape(images, TOK, D)], axis=1
     )
@@ -499,42 +655,53 @@
         grad_encoded, visible_enc, block_all[0], layer_vectors[0], stored_enc
     )
     grad_tokens = narrow(grad_stream[:, BUF:].reshape(-1, D))
+    grad_class = lax.dynamic_update_slice_in_dim(
+        jnp.zeros((all_images, D), jnp.float32),
+        jnp.sum(grad_stream[:, :BUF], axis=1),
+        dp_index * images,
+        0,
+    )
     grad_tables = jnp.concatenate(
         [
             product_left(patch_flat, grad_tokens),
             column_sum(grad_tokens)[None],
-            jnp.dot(picker.T, jnp.sum(grad_stream[:, :BUF], axis=1), precision=highest),
             jnp.sum(grad_stream, axis=0),
             jnp.sum(grad_dec_in, axis=0),
             jnp.sum(grad_dec_in * hidden_rows, axis=(0, 1))[None],
             jnp.stack([grad_vec_enc, grad_vec_dec]).reshape(6 * LAYERS, D),
             jnp.stack([grad_gain_enc, grad_shift_enc, grad_gain_dec, grad_shift_dec]),
+            grad_class,
         ],
         axis=0,
     )
-    grad_blocks = jnp.stack([grad_rows_enc, grad_rows_dec])
+    table_count = grad_tables.shape[0]
+    quarter = -(-table_count // (8 * tensor_size)) * 8
+    grad_tables = jnp.pad(grad_tables, ((0, quarter * tensor_size - table_count), (0, 0)))
+    grad_tables = lax.dynamic_slice_in_dim(grad_tables, tensor_index * quarter, quarter, 0)
+    owned_cols = tensor_columns(scatter_small(grad_tables.T))
+    kept_cols = table_count - all_images
+    owned_tables = jnp.concatenate(
+        [
+            owned_cols[:, :class_at],
+            jnp.dot(owned_cols[:, kept_cols:table_count], picker, precision=highest),
+            owned_cols[:, class_at:kept_cols],
+        ],
+        axis=1,
+    )
+    owned_blocks = jnp.stack([scatter_sum(grad_rows_enc), scatter_sum(grad_rows_dec)])
     column_grads = []
     for grad_local in (grad_bias_enc, grad_bias_dec):
         pieces = [
             grad_local[slot * local_width : (slot + 1) * local_width] for slot in range(3)
         ] + [grad_local[3 * local_width :]]
         column_grads.append(place_pieces(3 * D + FF, pieces, column_starts))
-    bias_local = jnp.concatenate(
-        [
-            rest_bias_grad.reshape(-1),
-            jnp.concatenate(head_bias_grads),
-            jnp.concatenate(column_grads),
-        ]
-    )
-    bias_grad = lax.psum(bias_local, ("dp", "tensor")).reshape(bias_rows.shape)
-    owned_blocks, owned_head = (
-        lax.psum_scatter(grad_blocks, "dp", scatter_dimension=1, tiled=True),
-        lax.psum_scatter(grad_head, "dp", scatter_dimension=1, tiled=True),
-    )
-    owned_rest, owned_tables = (
-        lax.psum_scatter(grad_rest_cols, "dp", scatter_dimension=0, tiled=True),
-        lax.psum_scatter(grad_tables.T, "dp", scatter_dimension=0, tiled=True),
-    )
+    lanes = bias_rows.shape[1]
+    both = ("tensor", "dp")
+    bias_head = sum_everywhere(
+        jnp.concatenate([rest_bias_grad] + head_bias_grads).reshape(-1, lanes), both
+    )
+    bias_layers = [sum_everywhere(grad.reshape(-1, lanes), both) for grad in column_grads]
+    bias_grad = jnp.concatenate([bias_head] + bias_layers, axis=0)
     split_squares = (
         jnp.sum(owned_blocks * owned_blocks)
         + jnp.sum(owned_head * owned_head)
@@ -542,8 +709,11 @@
     )
     shared_squares = jnp.sum(owned_tables * owned_tables) / tensor_size
     every_squares = jnp.sum(bias_grad * bias_grad) / (tensor_size * lax.axis_size("dp"))
-    norm_square = lax.psum(split_squares + shared_squares + every_squares, ("dp", "tensor"))
-    loss_value = loss_sum / weight_total
+    last_sums = sum_everywhere(
+        jnp.stack([split_squares + shared_squares + every_squares, numerator / tensor_size]), both
+    )
+    norm_square = last_sums[0]
+    loss_value = last_sums[1] / weight_total
     grad_norm = jnp.sqrt(norm_square)
     factor = jnp.minimum(1.0, clip_limit / (grad_norm + 1e-06))
     step_num = step_count[0].astype(jnp.float32)

time: 2010 us -> 1060 us (0.53)
  waiting for transfers between devices: 1500 us -> 504 us
  starting transfers between devices: 2.57 us -> 98.3 us
  blocking collectives: 61.6 us -> 0 us
  matrix products: 146 us -> 93.6 us
  other arithmetic: 154 us -> 185 us
  between operations: 27.7 us -> 48.8 us
    reduce_scatter x4 -> x0, waiting for transfers between devices: 620 us -> none  [the longest x1 230 us: local(): lax.psum_scatter(grad_blocks, 'dp', scatter_dimension=1, tiled=True)]
    psum x14 -> x0, waiting for transfers between devices: 429 us -> none  [the longest x6 212 us: branch_sum(): return lax.psum(partial_term, 'tensor')]
    ppermute x0 -> x104, waiting for transfers between devices: none -> 290 us  [swap(): lax.ppermute(value, axis, [(i, i ^ step) for i in range(lax.axis_size(axi...]
    all_gather x11 -> x6, waiting for transfers between devices: 451 us -> 213 us  [the longest x1 62.7 us: local(): block_all = [lax.all_gather(block_share[0], 'dp', axis=0, tiled=True)]]
    ppermute x0 -> x104, starting transfers between devices: none -> 97.8 us  [swap(): lax.ppermute(value, axis, [(i, i ^ step) for i in range(lax.axis_size(axi...]
    psum x2 -> x0, blocking collectives: 61.6 us -> none  [the longest x1 39.6 us: local(): lax.psum(split_squares + shared_squares + every_squares, ('dp', 'tensor'))]
    add x0 -> x50, other arithmetic: none -> 34.3 us  [the longest x5 17.2 us: scatter_sum(): pairs = keep + got.reshape(4, slab, columns)]
    dot_general x23, matrix products: 55.4 us -> 27.2 us  [product(): return jnp.dot(left, right, preferred_element_type=jnp.float32)]
  transfers between devices with their start and end apart: 29 -> 110, of which waited for: 29 -> 45; matrix products, arithmetic and copies ran while one was open for 11% -> 29% of each run, Pallas kernels for 0% -> 0%
where the time goes in v1:
time: 1060 us; the launch traced here: 1050 us
  waiting for transfers between devices  504 us (48%)
  other arithmetic  185 us (17%)
  local copies, waits for them, and re-layouts  120 us (11%)
  starting transfers between devices  98.3 us (9%)
  matrix products  93.6 us (9%)
  between operations  48.8 us (5%)
    ppermute x104, waiting for transfers between devices, swap(): lax.ppermute(value, axis, [(i, i ^ step) for i in range(lax.axis_size(axi...  290 us
    ppermute x104, starting transfers between devices, swap(): lax.ppermute(value, axis, [(i, i ^ step) for i in range(lax.axis_size(axi...  97.8 us
    all_gather x1, waiting for transfers between devices, local(): block_all = [lax.all_gather(block_share[0], 'dp', axis=0, tiled=True)]  62.7 us
    all_gather x1, waiting for transfers between devices, local(): table_cols = lax.all_gather(table_share, 'dp', axis=0, tiled=True)  51.3 us
    all_gather x1, waiting for transfers between devices, local(): rest_rows = lax.all_gather(narrow(head_rest), 'dp', axis=0, tiled=True)  49.6 us
    dot_general x18, matrix products, product_right(): lax.dot_general(left, right, (((1,), (1,)), ((), ())), preferred_element_...  33.8 us
    all_gather x2, waiting for transfers between devices, local(): lax.all_gather(head_share[segment], 'dp', axis=0, tiled=True)  33.7 us
    dot_general x23, matrix products, product(): return jnp.dot(left, right, preferred_element_type=jnp.float32)  27.2 us
  transfers between devices with their start and end apart: 110, of which 45 were waited for; matrix products, arithmetic and copies ran while one was open for 29% of the time, Pallas kernels for 0%

profile of v1, /device:TPU:0, one launch (start us, length us, event | category | flops | bytes accessed | tf_op | source)
XLA Modules:
  0.0 1049.0 jit_solution(39904121806659785)
XLA Ops:
  31.1 51.3 %all-gather.11.cloned.1.call-done = f32[768,730]{1,0:T(8,128)} async-done(((f32[96,730]{1,0:T(8,128)}), f32[768,730]{1,0:T(8,128)}) %all-gather.11.cloned.1.call-update) | async-done | bytes 2242576 | tf_op jit(solution)/shard_map/all_gather | solution.py:485
  86.2 62.7 %all-gather.15.cloned.1.call-done = bf16[1,2304,768]{2,1,0:T(8,128)(2,1)} async-done(((bf16[1,288,768]{2,1,0:T(8,128)(2,1)}), bf16[1,2304,768]{2,1,0:T(8,128)(2,1)}) %all-gather.15.cloned.1.call-update) | async-done | bytes 3538960 | tf_op jit(solution)/shard_map/all_gather | solution.py:484
  159.8 11.0 %collective-permute-done.7 = f32[160,768]{1,0:T(8,128)S(1)} collective-permute-done((f32[160,768]{1,0:T(8,128)S(1)}, f32[160,768]{1,0:T(8,128)S(1)}, u32[]{:S(2)}, u32[]{:S(2)}) %collective-permute-start.7) | collective-permute-done | bytes 491552 | tf_op jit(solution)/shard_map/ppermute | solution.py:92
  184.4 10.6 %collective-permute-done.10 = f32[160,768]{1,0:T(8,128)S(1)} collective-permute-done((f32[160,768]{1,0:T(8,128)S(1)}, f32[160,768]{1,0:T(8,128)S(1)}, u32[]{:S(2)}, u32[]{:S(2)}) %collective-permute-start.10) | collective-permute-done | bytes 491552 | tf_op jit(solution)/shard_map/ppermute | solution.py:92
  199.6 15.7 %all-gather.17.cloned.1.call-done = bf16[1,2304,768]{2,1,0:T(8,128)(2,1)} async-done(((bf16[1,288,768]{2,1,0:T(8,128)(2,1)}), bf16[1,2304,768]{2,1,0:T(8,128)(2,1)}) %all-gather.17.cloned.1.call-update) | async-done | bytes 3538960 | tf_op jit(solution)/shard_map/all_gather | solution.py:487
  220.9 49.6 %all-gather.13.cloned.1.call-done = bf16[4992,256]{1,0:T(8,128)(2,1)} async-done(((bf16[624,256]{1,0:T(8,128)(2,1)}), bf16[4992,256]{1,0:T(8,128)(2,1)}) %all-gather.13.cloned.1.call-update) | async-done | bytes 2555920 | tf_op jit(solution)/shard_map/all_gather | solution.py:488
  278.8 9.3 collective-permute-done.13
  294.8 13.4 %collective-permute-done.4 = bf16[1920,256]{1,0:T(8,128)(2,1)} collective-permute-done((bf16[1920,256]{1,0:T(8,128)(2,1)}, bf16[1920,256]{1,0:T(8,128)(2,1)}, u32[]{:S(2)}, u32[]{:S(2)}) %collective-permute-start.4) | collective-permute-done | bytes 983072 | tf_op jit(solution)/shard_map/ppermute | solution.py:92
  310.7 4.5 multiply_convert_fusion.10
  327.1 8.9 collective-permute-done.16
  348.6 33.7 %all-gather.21.cloned.1.call-done = bf16[1,1280,1024]{2,1,0:T(8,128)(2,1)} async-done(((bf16[1,160,1024]{2,1,0:T(8,128)(2,1)}), bf16[1,1280,1024]{2,1,0:T(8,128)(2,1)}) %all-gather.21.cloned.1.call-update) | async-done | bytes 2621456 | tf_op jit(solution)/shard_map/all_gather | solution.py:491
  387.9 14.4 %collective-permute-done.28 = f32[256,768]{1,0:T(8,128)S(1)} collective-permute-done((f32[256,768]{1,0:T(8,128)S(1)}, f32[256,768]{1,0:T(8,128)S(1)}, u32[]{:S(2)}, u32[]{:S(2)}) %collective-permute-start.28) | collective-permute-done | bytes 786464 | tf_op jit(solution)/shard_map/ppermute | solution.py:92
  415.2 22.5 %collective-permute-done.25 = f32[128,1024]{1,0:T(8,128)S(1)} collective-permute-done((f32[128,1024]{1,0:T(8,128)S(1)}, f32[128,1024]{1,0:T(8,128)S(1)}, u32[]{:S(2)}, u32[]{:S(2)}) %collective-permute-start.25) | collective-permute-done | bytes 524320 | tf_op jit(solution)/shard_map/ppermute | solution.py:92
  448.2 12.4 %collective-permute-done.31 = f32[128,1024]{1,0:T(8,128)S(1)} collective-permute-done((f32[128,1024]{1,0:T(8,128)S(1)}, f32[128,1024]{1,0:T(8,128)S(1)}, u32[]{:S(2)}, u32[]{:S(2)}) %collective-permute-start.31) | collective-permute-done | bytes 524320 | tf_op jit(solution)/shard_map/ppermute | solution.py:92
  475.9 6.4 collective-permute-done.37
  504.2 5.3 collective-permute-done.40
  519.5 3.8 abs_reduce_fusion.2
  524.0 6.6 abs_reduce_fusion.3
  596.3 3.9 dynamic-slice_add_fusion.2
  628.3 10.7 %collective-permute-done.87 = f32[128,128]{1,0:T(8,128)} collective-permute-done((f32[128,128]{1,0:T(8,128)S(1)}, f32[128,128]{1,0:T(8,128)}, u32[]{:S(2)}, u32[]{:S(2)}) %collective-permute-start.87) | collective-permute-done | bytes 65568 | tf_op jit(solution)/shard_map/ppermute | solution.py:92
  659.7 14.0 %collective-permute-done.64 = f16[176,1024]{1,0:T(8,128)(2,1)S(1)} collective-permute-done((f16[176,1024]{1,0:T(8,128)(2,1)S(1)}, f16[176,1024]{1,0:T(8,128)(2,1)S(1)}, u32[]{:S(2)}, u32[]{:S(2)}) %collective-permute-start.64) | collective-permute-done | bytes 360480 | tf_op jit(solution)/shard_map/ppermute | solution.py:92
  699.9 5.2 abs_reduce_fusion
  727.1 30.9 %collective-permute-done.96 = f32[42,128]{1,0:T(8,128)S(1)} collective-permute-done((f32[42,128]{1,0:T(8,128)S(1)}, f32[42,128]{1,0:T(8,128)S(1)}, u32[]{:S(2)}, u32[]{:S(2)}) %collective-permute-start.96) | collective-permute-done | bytes 21536 | tf_op jit(solution)/shard_map/ppermute | solution.py:92
  758.0 5.3 collective-permute-start.97
  818.5 6.3 collective-permute-done.75
  825.7 4.0 abs_reduce_fusion.1
  837.7 13.6 %concatenate.350 = f32[730,768]{1,0:T(8,128)} concatenate(f32[64,768]{1,0:T(8,128)S(1)} %convolution_bitcast_fusion, f32[1,768]{1,0:T(1,128)S(1)} %broadcast_in_dim.87, f32[320,768]{1,0:T(8,128)S(1)} %bitcast.499, f32[320,768]{1,0:T(8,128)S(1)} %bitcast.508, f32[1,768]{1,0:T(1,128)S(1)} %copy-done.276, f32[12,768]{1,0:T(8,128)S(1)} %reshape.2487, f32[1,768]{1,0:T(1,128)S(1)} %copy-done.274, ...), dimensions={0} | concatenate | bytes 4485120 | tf_op jit(solution)/shard_map/concatenate | solution.py:664
  860.7 5.2 collective-permute-done.77
  875.7 28.3 %collective-permute-done.91 = f32[42,128]{1,0:T(8,128)S(1)} collective-permute-done((f32[42,128]{1,0:T(8,128)S(1)}, f32[42,128]{1,0:T(8,128)S(1)}, u32[]{:S(2)}, u32[]{:S(2)}) %collective-permute-start.91) | collective-permute-done | bytes 21536 | tf_op jit(solution)/shard_map/ppermute | solution.py:92
  931.6 7.1 collective-permute-done.59
  961.8 27.1 %collective-permute-done.56 = f16[304,768]{1,0:T(8,128)(2,1)} collective-permute-done((f16[304,768]{1,0:T(8,128)(2,1)}, f16[304,768]{1,0:T(8,128)(2,1)}, u32[]{:S(2)}, u32[]{:S(2)}) %collective-permute-start.56) | collective-permute-done | bytes 466976 | tf_op jit(solution)/shard_map/ppermute | solution.py:92
  1007.8 8.4 collective-permute-start.102
  (1309 shorter events, 488.3 us)
Async XLA Ops:
  7.2 75.2 %all-gather.11.cloned.1.call-start = ((), (), s32[]{:S(2)}) async-start(), calls=%async_computation | async-start | bytes 2654208 | tf_op jit(solution)/shard_map/all_gather | solution.py:485
  28.8 120.1 %all-gather.15.cloned.1.call-start = ((), (), s32[]{:S(2)}) async-start(), calls=%async_computation.2 | async-start | bytes 3981312 | tf_op jit(solution)/shard_map/all_gather | solution.py:484
  30.0 185.4 %all-gather.17.cloned.1.call-start = ((), (), s32[]{:S(2)}) async-start(), calls=%async_computation.3 | async-start | bytes 3981312 | tf_op jit(solution)/shard_map/all_gather | solution.py:487
  30.7 239.7 %all-gather.13.cloned.1.call-start = ((), (), s32[]{:S(2)}) async-start(), calls=%async_computation.1 | async-start | bytes 2875392 | tf_op jit(solution)/shard_map/all_gather | solution.py:488
  159.7 182.5 %all-gather.19.cloned.1.call-start = ((), (), s32[]{:S(2)}) async-start(), calls=%async_computation.4 | async-start | bytes 2949120 | tf_op jit(solution)/shard_map/all_gather | solution.py:491
  184.1 198.2 %all-gather.21.cloned.1.call-start = ((), (), s32[]{:S(2)}) async-start(), calls=%async_computation.5 | async-start | bytes 2949120 | tf_op jit(solution)/shard_map/all_gather | solution.py:491
  220.7 52.0 %collective-permute-start.12 = (f32[160,768]{1,0:T(8,128)S(1)}, f32[160,768]{1,0:T(8,128)}, u32[]{:S(2)}, u32[]{:S(2)}) collective-permute-start(f32[160,768]{1,0:T(8,128)S(1)} %constant_dynamic-slice_fusion.15), channel_id=1, source_target_pairs={{0,1},{1,0},{2,3},{3,2},{4,5},{5,4},{6,7},{7,6},{8,9},{9,8},{10,11... | collective-permute-start | bytes 1474568 | tf_op jit(solution)/shard_map/ppermute | solution.py:92
  290.6 33.7 %collective-permute-start.3 = (bf16[1920,256]{1,0:T(8,128)(2,1)}, bf16[1920,256]{1,0:T(8,128)(2,1)}, u32[]{:S(2)}, u32[]{:S(2)}) collective-permute-start(bf16[1920,256]{1,0:T(8,128)(2,1)} %pad_maximum_fusion.12), channel_id=1, source_target_pairs={{0,1},{1,0},{2,3},{3,2},{4,5},{5,4},{6,7},{7,6},{8,9},{9,8},{10,11... | collective-permute-start | bytes 2949128 | tf_op jit(solution)/shard_map/ppermute | solution.py:92
  345.3 40.5 %collective-permute-start.22 = (f32[256,768]{1,0:T(8,128)}, f32[256,768]{1,0:T(8,128)}, u32[]{:S(2)}, u32[]{:S(2)}) collective-permute-start(f32[256,768]{1,0:T(8,128)} %fusion.22), channel_id=1, source_target_pairs={{0,2},{1,3},{2,0},{3,1},{4,6},{5,7},{6,4},{7,5},{8,10},{9,11},{10,... | collective-permute-start | bytes 2359304 | tf_op jit(solution)/shard_map/ppermute | solution.py:92
  348.3 54.1 %collective-permute-start.21 = (f32[256,768]{1,0:T(8,128)}, f32[256,768]{1,0:T(8,128)}, u32[]{:S(2)}, u32[]{:S(2)}) collective-permute-start(f32[256,768]{1,0:T(8,128)} %fusion.22), channel_id=1, source_target_pairs={{0,1},{1,0},{2,3},{3,2},{4,5},{5,4},{6,7},{7,6},{8,9},{9,8},{10,11... | collective-permute-start | bytes 2359304 | tf_op jit(solution)/shard_map/ppermute | solution.py:92
  412.5 32.3 %collective-permute-start.34 = (f32[256,512]{1,0:T(8,128)S(1)}, f32[256,512]{1,0:T(8,128)S(1)}, u32[]{:S(2)}, u32[]{:S(2)}) collective-permute-start(f32[256,512]{1,0:T(8,128)S(1)} %maximum_add_fusion.12), channel_id=1, source_target_pairs={{0,2},{1,3},{2,0},{3,1},{4,6},{5,7},{6,4},{7,5},{8,10},{9,11},{10,... | collective-permute-start | bytes 1572872 | tf_op jit(solution)/shard_map/ppermute | solution.py:92
  543.9 48.9 %collective-permute-start.66 = (f16[656,1024]{1,0:T(8,128)(2,1)}, f16[656,1024]{1,0:T(8,128)(2,1)}, u32[]{:S(2)}, u32[]{:S(2)}) collective-permute-start(f16[656,1024]{1,0:T(8,128)(2,1)} %concatenate.340), channel_id=1, source_target_pairs={{0,4},{4,0},{8,12},{12,8},{16,20},{20,16},{24,28},{28,24},{1,5},{5... | collective-permute-start | bytes 4030472 | tf_op jit(solution)/shard_map/ppermute | solution.py:92
  548.1 65.4 %collective-permute-start.62 = (f16[656,1024]{1,0:T(8,128)(2,1)}, f16[656,1024]{1,0:T(8,128)(2,1)}, u32[]{:S(2)}, u32[]{:S(2)}) collective-permute-start(f16[656,1024]{1,0:T(8,128)(2,1)} %concatenate.335), channel_id=1, source_target_pairs={{0,4},{4,0},{8,12},{12,8},{16,20},{20,16},{24,28},{28,24},{1,5},{5... | collective-permute-start | bytes 4030472 | tf_op jit(solution)/shard_map/ppermute | solution.py:92
  585.6 37.1 %collective-permute-start.45 = (f32[160,768]{1,0:T(8,128)}, f32[160,768]{1,0:T(8,128)}, u32[]{:S(2)}, u32[]{:S(2)}) collective-permute-start(f32[160,768]{1,0:T(8,128)} %constant_dynamic-slice_fusion.8), channel_id=1, source_target_pairs={{0,1},{1,0},{2,3},{3,2},{4,5},{5,4},{6,7},{7,6},{8,9},{9,8},{10,11... | collective-permute-start | bytes 1474568 | tf_op jit(solution)/shard_map/ppermute | solution.py:92
  609.5 37.2 %collective-permute-start.68 = (f16[176,1024]{1,0:T(8,128)(2,1)}, f16[176,1024]{1,0:T(8,128)(2,1)}, u32[]{:S(2)}, u32[]{:S(2)}) collective-permute-start(f16[176,1024]{1,0:T(8,128)(2,1)} %concatenate.342), channel_id=1, source_target_pairs={{0,16},{4,20},{8,24},{12,28},{16,0},{20,4},{24,8},{28,12},{1,17},{... | collective-permute-start | bytes 1081352 | tf_op jit(solution)/shard_map/ppermute | solution.py:92
  612.0 38.5 %collective-permute-start.69 = (f16[176,1024]{1,0:T(8,128)(2,1)}, f16[176,1024]{1,0:T(8,128)(2,1)}, u32[]{:S(2)}, u32[]{:S(2)}) collective-permute-start(f16[176,1024]{1,0:T(8,128)(2,1)} %concatenate.343), channel_id=1, source_target_pairs={{0,24},{4,28},{8,16},{12,20},{16,8},{20,12},{24,0},{28,4},{1,25},{... | collective-permute-start | bytes 1081352 | tf_op jit(solution)/shard_map/ppermute | solution.py:92
  613.4 43.8 %collective-permute-start.67 = (f16[176,1024]{1,0:T(8,128)(2,1)}, f16[176,1024]{1,0:T(8,128)(2,1)}, u32[]{:S(2)}, u32[]{:S(2)}) collective-permute-start(f16[176,1024]{1,0:T(8,128)(2,1)} %concatenate.341), channel_id=1, source_target_pairs={{0,8},{4,12},{8,0},{12,4},{16,24},{20,28},{24,16},{28,20},{1,9},{5... | collective-permute-start | bytes 1081352 | tf_op jit(solution)/shard_map/ppermute | solution.py:92
  657.2 62.1 %collective-permute-start.70 = (f16[2512,256]{1,0:T(8,128)(2,1)}, f16[2512,256]{1,0:T(8,128)(2,1)}, u32[]{:S(2)}, u32[]{:S(2)}) collective-permute-start(f16[2512,256]{1,0:T(8,128)(2,1)} %concatenate.345), channel_id=1, source_target_pairs={{0,4},{4,0},{8,12},{12,8},{16,20},{20,16},{24,28},{28,24},{1,5},{5... | collective-permute-start | bytes 3858440 | tf_op jit(solution)/shard_map/ppermute | solution.py:92
  716.6 71.5 %collective-permute-start.58 = (f16[1168,768]{1,0:T(8,128)(2,1)}, f16[1168,768]{1,0:T(8,128)(2,1)}, u32[]{:S(2)}, u32[]{:S(2)}) collective-permute-start(f16[1168,768]{1,0:T(8,128)(2,1)} %concatenate.330), channel_id=1, source_target_pairs={{0,4},{4,0},{8,12},{12,8},{16,20},{20,16},{24,28},{28,24},{1,5},{5... | collective-permute-start | bytes 5382152 | tf_op jit(solution)/shard_map/ppermute | solution.py:92
  717.9 40.1 %collective-permute-start.96 = (f32[42,128]{1,0:T(8,128)S(1)}, f32[42,128]{1,0:T(8,128)S(1)}, u32[]{:S(2)}, u32[]{:S(2)}) collective-permute-start(f32[42,128]{1,0:T(8,128)S(1)} %fusion.370), channel_id=1, source_target_pairs={{0,4},{4,0},{8,12},{12,8},{16,20},{20,16},{24,28},{28,24},{1,5},{5... | collective-permute-start | bytes 64520 | tf_op jit(solution)/shard_map/ppermute | solution.py:92
  722.0 48.9 %collective-permute-start.50 = (f32[160,768]{1,0:T(8,128)}, f32[160,768]{1,0:T(8,128)}, u32[]{:S(2)}, u32[]{:S(2)}) collective-permute-start(f32[160,768]{1,0:T(8,128)} %convert_add_fusion.5), channel_id=1, source_target_pairs={{0,1},{1,0},{2,3},{3,2},{4,5},{5,4},{6,7},{7,6},{8,9},{9,8},{10,11... | collective-permute-start | bytes 1474568 | tf_op jit(solution)/shard_map/ppermute | solution.py:92
  767.4 104.4 %collective-permute-start.72 = (f16[640,256]{1,0:T(8,128)(2,1)}, f16[640,256]{1,0:T(8,128)(2,1)}, u32[]{:S(2)}, u32[]{:S(2)}) collective-permute-start(f16[640,256]{1,0:T(8,128)(2,1)} %concatenate.347), channel_id=1, source_target_pairs={{0,16},{4,20},{8,24},{12,28},{16,0},{20,4},{24,8},{28,12},{1,17},{... | collective-permute-start | bytes 983048 | tf_op jit(solution)/shard_map/ppermute | solution.py:92
  767.4 105.4 %collective-permute-start.73 = (f16[640,256]{1,0:T(8,128)(2,1)}, f16[640,256]{1,0:T(8,128)(2,1)}, u32[]{:S(2)}, u32[]{:S(2)}) collective-permute-start(f16[640,256]{1,0:T(8,128)(2,1)} %concatenate.348), channel_id=1, source_target_pairs={{0,24},{4,28},{8,16},{12,20},{16,8},{20,12},{24,0},{28,4},{1,25},{... | collective-permute-start | bytes 983048 | tf_op jit(solution)/shard_map/ppermute | solution.py:92
  769.8 103.9 %collective-permute-start.71 = (f16[640,256]{1,0:T(8,128)(2,1)}, f16[640,256]{1,0:T(8,128)(2,1)}, u32[]{:S(2)}, u32[]{:S(2)}) collective-permute-start(f16[640,256]{1,0:T(8,128)(2,1)} %concatenate.346), channel_id=1, source_target_pairs={{0,8},{4,12},{8,0},{12,4},{16,24},{20,28},{24,16},{28,20},{1,9},{5... | collective-permute-start | bytes 983048 | tf_op jit(solution)/shard_map/ppermute | solution.py:92
  858.5 87.6 %collective-permute-start.54 = (f16[1168,768]{1,0:T(8,128)(2,1)}, f16[1168,768]{1,0:T(8,128)(2,1)}, u32[]{:S(2)}, u32[]{:S(2)}) collective-permute-start(f16[1168,768]{1,0:T(8,128)(2,1)} %concatenate.325), channel_id=1, source_target_pairs={{0,4},{4,0},{8,12},{12,8},{16,20},{20,16},{24,28},{28,24},{1,5},{5... | collective-permute-start | bytes 5382152 | tf_op jit(solution)/shard_map/ppermute | solution.py:92
  870.6 33.4 %collective-permute-start.91 = (f32[42,128]{1,0:T(8,128)S(1)}, f32[42,128]{1,0:T(8,128)S(1)}, u32[]{:S(2)}, u32[]{:S(2)}) collective-permute-start(f32[42,128]{1,0:T(8,128)S(1)} %fusion.369), channel_id=1, source_target_pairs={{0,4},{4,0},{8,12},{12,8},{16,20},{20,16},{24,28},{28,24},{1,5},{5... | collective-permute-start | bytes 64520 | tf_op jit(solution)/shard_map/ppermute | solution.py:92
  871.8 48.4 %collective-permute-start.60 = (f16[304,768]{1,0:T(8,128)(2,1)S(1)}, f16[304,768]{1,0:T(8,128)(2,1)}, u32[]{:S(2)}, u32[]{:S(2)}) collective-permute-start(f16[304,768]{1,0:T(8,128)(2,1)S(1)} %copy-done.156), channel_id=1, source_target_pairs={{0,16},{4,20},{8,24},{12,28},{16,0},{20,4},{24,8},{28,12},{1,17},{... | collective-permute-start | bytes 1400840 | tf_op jit(solution)/shard_map/ppermute | solution.py:92
  872.8 41.8 %collective-permute-start.78 = (f32[96,184]{1,0:T(8,128)S(1)}, f32[96,184]{1,0:T(8,128)S(1)}, u32[]{:S(2)}, u32[]{:S(2)}) collective-permute-start(f32[96,184]{1,0:T(8,128)S(1)} %bitcast.556), channel_id=1, source_target_pairs={{0,8},{4,12},{8,0},{12,4},{16,24},{20,28},{24,16},{28,20},{1,9},{5... | collective-permute-start | bytes 211976 | tf_op jit(solution)/shard_map/ppermute | solution.py:92
  873.7 43.5 %collective-permute-start.79 = (f32[96,184]{1,0:T(8,128)S(1)}, f32[96,184]{1,0:T(8,128)}, u32[]{:S(2)}, u32[]{:S(2)}) collective-permute-start(f32[96,184]{1,0:T(8,128)S(1)} %bitcast.555), channel_id=1, source_target_pairs={{0,16},{4,20},{8,24},{12,28},{16,0},{20,4},{24,8},{28,12},{1,17},{... | collective-permute-start | bytes 211976 | tf_op jit(solution)/shard_map/ppermute | solution.py:92
  955.9 32.9 %collective-permute-start.56 = (f16[304,768]{1,0:T(8,128)(2,1)}, f16[304,768]{1,0:T(8,128)(2,1)}, u32[]{:S(2)}, u32[]{:S(2)}) collective-permute-start(f16[304,768]{1,0:T(8,128)(2,1)} %concatenate.327), channel_id=1, source_target_pairs={{0,16},{4,20},{8,24},{12,28},{16,0},{20,4},{24,8},{28,12},{1,17},{... | collective-permute-start | bytes 1400840 | tf_op jit(solution)/shard_map/ppermute | solution.py:92
  956.7 34.0 %collective-permute-start.57 = (f16[304,768]{1,0:T(8,128)(2,1)}, f16[304,768]{1,0:T(8,128)(2,1)}, u32[]{:S(2)}, u32[]{:S(2)}) collective-permute-start(f16[304,768]{1,0:T(8,128)(2,1)} %concatenate.328), channel_id=1, source_target_pairs={{0,24},{4,28},{8,16},{12,20},{16,8},{20,12},{24,0},{28,4},{1,25},{... | collective-permute-start | bytes 1400840 | tf_op jit(solution)/shard_map/ppermute | solution.py:92
  959.1 33.5 %collective-permute-start.55 = (f16[304,768]{1,0:T(8,128)(2,1)}, f16[304,768]{1,0:T(8,128)(2,1)}, u32[]{:S(2)}, u32[]{:S(2)}) collective-permute-start(f16[304,768]{1,0:T(8,128)(2,1)} %concatenate.326), channel_id=1, source_target_pairs={{0,8},{4,12},{8,0},{12,4},{16,24},{20,28},{24,16},{28,20},{1,9},{5... | collective-permute-start | bytes 1400840 | tf_op jit(solution)/shard_map/ppermute | solution.py:92
  (392 other events, 4587.7 us)
Sparse Core Ops, SparseCore 0:
  28.9 53.4 all-gather.10
  85.1 63.7 all-gather.14
  151.6 63.6 all-gather.16
  217.9 52.4 all-gather.12
  273.0 53.2 all-gather.18
  328.9 53.2 all-gather.20

commit v2 on v1

v2 whole, which is shorter than its diff:
```python
import functools
import math

import jax
import jax.numpy as jnp
from jax import lax
from jax.experimental import pallas as pl
from jax.experimental.pallas import tpu as pltpu
from jax.sharding import PartitionSpec as P

D = 768
HEAD = 64
FF = 3072
HW = 1024
TOKD = 64
CLASSES = 1000
BUF = 64
TOK = 256
T_STEPS = 1000
COPIES = 1
LAYERS = 2
HB = 2


highest = lax.Precision.HIGHEST
norm_eps = 1e-06
beta_first = 0.9
beta_second = 0.95
adam_eps = 1e-08
learn_rate = 0.02
decay_rate = 0.05
clip_limit = 0.002
dp_axis, tensor_axis = "dp", "tensor"


def layer_norm(inputs, gain_vec, offset_vec):
    average = jnp.mean(inputs, axis=-1, keepdims=True)
    centred = inputs - average
    spread = jnp.mean(centred * centred, axis=-1, keepdims=True)
    return centred * lax.rsqrt(spread + norm_eps) * gain_vec + offset_vec


def modulate(inputs, shift_vec, scale_vec):
    return layer_norm(inputs, 1.0, 0.0) * (1.0 + scale_vec) + shift_vec


def exact_gelu(inputs):
    return jax.nn.gelu(inputs, approximate=False)


def local_back(function, inputs, incoming):
    return jax.vjp(function, inputs)[1](incoming)[0]


def sinusoid(step_ids):
    half_width = HW // 2
    frequency = jnp.exp(-math.log(10000.0) * jnp.arange(half_width, dtype=jnp.float32) / half_width)
    angles = step_ids.astype(jnp.float32)[..., None] * frequency
    return jnp.concatenate([jnp.cos(angles), jnp.sin(angles)], axis=-1)


def cut_rows(packed, counts):
    pieces = []
    begin_at = 0
    for count in counts:
        pieces.append(packed[begin_at : begin_at + count])
        begin_at = begin_at + count
    return pieces


def narrow(inputs):
    return inputs.astype(jnp.bfloat16)


def product(left, right):
    return jnp.dot(left, right, preferred_element_type=jnp.float32)


def product_left(left, right):
    return lax.dot_general(
        left, right, (((0,), (0,)), ((), ())), preferred_element_type=jnp.float32
    )


def product_right(left, right):
    return lax.dot_general(
        left, right, (((1,), (1,)), ((), ())), preferred_element_type=jnp.float32
    )


def column_sum(inputs):
    return jnp.sum(inputs.astype(jnp.float32), axis=0)


def swap(value, axis, step):
    return lax.ppermute(value, axis, [(i, i ^ step) for i in range(lax.axis_size(axis))])


MESH = pl.DeviceIdType.MESH
(
    first_gather,
    last_sums_kernel,
    encoder_forward,
    decoder_forward,
    head_forward,
    back_head,
    back_cond,
    back_decoder,
    back_encoder,
) = (0, 1, 2, 4, 6, 8, 10, 11, 13)
rest_group, mix_group = 100, 101


class RingGather:
    def __init__(self, shares, wholes, local_sem, send_sem, recv_sem):
        rank = lax.axis_index(dp_axis)
        self.rank, self.low, self.high = rank, lax.rem(rank, 2), lax.div(rank, 2)
        self.beside = rank + 1 - 2 * self.low
        self.ahead = 2 * lax.rem(self.high + 1, 4) + self.low
        self.behind = 2 * lax.rem(self.high + 3, 4) + self.low
        self.shares, self.wholes = shares, wholes
        self.send_sem, self.recv_sem = send_sem, recv_sem
        self.items = range(len(shares))
        self.sent = []
        self.own = [
            pltpu.make_async_copy(shares[item], wholes[item].at[rank], local_sem.at[item])
            for item in self.items
        ]

    def copy(self, item, source, place, peer, slot):
        return pltpu.make_async_remote_copy(
            src_ref=source,
            dst_ref=self.wholes[item].at[place],
            send_sem=self.send_sem.at[item, slot],
            recv_sem=self.recv_sem.at[item, slot],
            device_id={dp_axis: peer},
            device_id_type=MESH,
        )

    def send(self, *arguments):
        self.sent.append(self.copy(*arguments))
        self.sent[-1].start()

    def begin(self):
        for item in self.items:
            self.send(item, self.shares[item], self.rank, self.ahead, 0)
            self.send(item, self.shares[item], self.rank, self.beside, 4)
            self.own[item].start()

    def advance(self, step):
        place = 2 * lax.rem(self.high + 4 - step, 4) + self.low
        for item in self.items:
            source = self.wholes[item].at[place]
            self.copy(item, source, place, self.ahead, step - 1).wait_recv()
            if step < 3:
                self.send(item, source, place, self.ahead, step)
            self.send(item, source, place, self.beside, 4 + step)

    def finish(self):
        for step in range(4):
            place = 2 * lax.rem(self.high + 4 - step, 4) + 1 - self.low
            for item in self.items:
                source = self.wholes[item].at[place]
                self.copy(item, source, place, self.beside, 4 + step).wait_recv()
        for sent in self.sent:
            sent.wait_send()
        for kept in self.own:
            kept.wait()


def ring_scratch(count):
    return [
        pltpu.SemaphoreType.DMA((count,)),
        pltpu.SemaphoreType.DMA((count, 8)),
        pltpu.SemaphoreType.DMA((count, 8)),
    ]


def sum_kernel(count, cross_type, *refs):
    partial, shares = refs[0], refs[1 : 1 + count]
    total, wholes = refs[1 + count], refs[2 + count : 2 + 2 * count]
    near, pair, far, send_sem, recv_sem = refs[2 + 2 * count : 7 + 2 * count]
    rank = lax.axis_index(tensor_axis)
    low = lax.rem(rank, 2)
    partner, across = rank + 1 - 2 * low, lax.rem(rank + 2, 4)
    ring = RingGather(shares, wholes, *refs[7 + 2 * count :]) if count else None
    barrier = pltpu.get_barrier_semaphore()
    for peer in (partner, across):
        pl.semaphore_signal(barrier, inc=1, device_id={tensor_axis: peer}, device_id_type=MESH)
    if ring:
        for peer in (ring.beside, ring.behind):
            pl.semaphore_signal(barrier, inc=1, device_id={dp_axis: peer}, device_id_type=MESH)
    pl.semaphore_wait(barrier, 4 if ring else 2)
    half = partial.shape[0] // 2
    mine = pl.ds(pl.multiple_of(low * half, 8), half)
    others = pl.ds(pl.multiple_of((1 - low) * half, 8), half)

    def copy(source, target, peer, slot):
        return pltpu.make_async_remote_copy(
            src_ref=source,
            dst_ref=target,
            send_sem=send_sem.at[slot],
            recv_sem=recv_sem.at[slot],
            device_id={tensor_axis: peer},
            device_id_type=MESH,
        )

    give = copy(partial.at[others], near, partner, 0)
    cross = copy(pair, far, across, 1)
    back = copy(total.at[mine], total.at[mine], partner, 2)
    give.start()
    if ring:
        ring.begin()
    give.wait()
    pair[...] = (partial[mine, :] + near[...]).astype(cross_type)
    cross.start()
    if ring:
        ring.advance(1)
        ring.advance(2)
    cross.wait()
    total[mine, :] = pair[...].astype(jnp.float32) + far[...].astype(jnp.float32)
    back.start()
    if ring:
        ring.advance(3)
    back.wait()
    if ring:
        ring.finish()


def tensor_sum(partial_term, cross_type, kernel, shares=()):
    ring_here = lax.axis_size(dp_axis) == 8
    wholes = [] if ring_here else [lax.all_gather(share, dp_axis) for share in shares]
    shares = shares if ring_here else ()
    if lax.axis_size(tensor_axis) != 4:
        return lax.psum(partial_term, tensor_axis), wholes
    rows, columns = partial_term.shape
    count = len(shares)
    vmem, anywhere = pl.BlockSpec(memory_space=pltpu.VMEM), pl.BlockSpec(memory_space=pl.ANY)
    outs = pl.pallas_call(
        functools.partial(sum_kernel, count, cross_type),
        out_shape=[jax.ShapeDtypeStruct(partial_term.shape, jnp.float32)]
        + [jax.ShapeDtypeStruct((8,) + share.shape, share.dtype) for share in shares],
        in_specs=[vmem] + [anywhere] * count,
        out_specs=[vmem] + [anywhere] * count,
        scratch_shapes=[
            pltpu.VMEM((rows // 2, columns), jnp.float32),
            pltpu.VMEM((rows // 2, columns), cross_type),
            pltpu.VMEM((rows // 2, columns), cross_type),
            pltpu.SemaphoreType.DMA((3,)),
            pltpu.SemaphoreType.DMA((3,)),
        ]
        + (ring_scratch(count) if count else []),
        compiler_params=pltpu.CompilerParams(
            collective_id=kernel, has_side_effects=True, vmem_limit_bytes=16 << 20
        ),
        cost_estimate=pl.CostEstimate(flops=0, bytes_accessed=2_000_000, transcendentals=0),
    )(partial_term, *shares)
    return outs[0], outs[1:] if ring_here else wholes


def branch_sum(partial_term, kernel, shares=()):
    return tensor_sum(partial_term, jnp.bfloat16, kernel, shares)


def spread(block, slots, axis, send_sem, recv_sem):
    rank, size = lax.axis_index(axis), lax.axis_size(axis)
    copies = []
    for step in range(1, size):
        peer = lax.rem(rank + step, size)
        copies.append(
            pltpu.make_async_remote_copy(
                src_ref=block,
                dst_ref=slots.at[rank],
                send_sem=send_sem.at[step - 1],
                recv_sem=recv_sem.at[step - 1],
                device_id={axis: peer},
                device_id_type=MESH,
            )
        )
        copies[-1].start()
    return copies


def greet(barrier, axes):
    count = 0
    for axis in axes:
        rank, size = lax.axis_index(axis), lax.axis_size(axis)
        for step in range(1, size):
            peer = lax.rem(rank + step, size)
            pl.semaphore_signal(barrier, inc=1, device_id={axis: peer}, device_id_type=MESH)
            count += 1
    pl.semaphore_wait(barrier, count)


def small_sum_kernel(value, total, middle, near, far, near_send, near_recv, far_send, far_recv):
    greet(pltpu.get_barrier_semaphore(), (tensor_axis, dp_axis))
    near[lax.axis_index(tensor_axis)] = value[...]
    for copy in spread(value, near, tensor_axis, near_send, near_recv):
        copy.wait()
    middle[...] = functools.reduce(jnp.add, [near[slot] for slot in range(near.shape[0])])
    far[lax.axis_index(dp_axis)] = middle[...]
    for copy in spread(middle, far, dp_axis, far_send, far_recv):
        copy.wait()
    total[...] = functools.reduce(jnp.add, [far[slot] for slot in range(far.shape[0])])


def small_sums(values):
    sizes = [lax.axis_size(tensor_axis), lax.axis_size(dp_axis)]
    if max(sizes) > 8:
        return sum_everywhere(jnp.stack(values), (tensor_axis, dp_axis))
    rows = lax.broadcasted_iota(jnp.int32, (8, 128), 0)
    block = jnp.zeros((8, 128), jnp.float32)
    for row, value in enumerate(values):
        block = jnp.where(rows == row, value, block)
    scratch = [pltpu.VMEM((8, 128), jnp.float32)]
    scratch += [pltpu.VMEM((size, 8, 128), jnp.float32) for size in sizes]
    for size in sizes:
        scratch += [pltpu.SemaphoreType.DMA((size - 1,))] * 2
    total = pl.pallas_call(
        small_sum_kernel,
        out_shape=jax.ShapeDtypeStruct((8, 128), jnp.float32),
        in_specs=[pl.BlockSpec(memory_space=pltpu.VMEM)],
        out_specs=pl.BlockSpec(memory_space=pltpu.VMEM),
        scratch_shapes=scratch,
        compiler_params=pltpu.CompilerParams(
            collective_id=last_sums_kernel, has_side_effects=True
        ),
    )(block)
    return total[:, 0]


def tensor_blocks(piece):
    if lax.axis_size(tensor_axis) != 4:
        return list(lax.all_gather(piece, tensor_axis))
    rank = lax.axis_index(tensor_axis)
    near = swap(piece, tensor_axis, 1)
    far = swap(piece, tensor_axis, 2)
    cross = swap(far, tensor_axis, 1)
    blocks = []
    for index in range(4):
        same_pair = jnp.where(rank == index, piece, near)
        other_pair = jnp.where(rank == index ^ 2, far, cross)
        blocks.append(jnp.where(rank // 2 == index // 2, same_pair, other_pair))
    return blocks


def tensor_columns(piece):
    return jnp.concatenate(tensor_blocks(piece), axis=1)


def sum_everywhere(value, axes):
    for axis in axes:
        step = 1
        while step < lax.axis_size(axis):
            value = value + swap(value, axis, step)
            step = 2 * step
    return value


def pick(blocks, index):
    return lax.dynamic_index_in_dim(blocks, index, 0, keepdims=False)


def bound_level(pairs):
    bounds = [
        left.shape[0]
        * jnp.max(jnp.abs(left.astype(jnp.float32)))
        * jnp.max(jnp.abs(right.astype(jnp.float32)))
        for left, right in pairs
    ]
    return jnp.ceil(jnp.log2(jnp.maximum(functools.reduce(jnp.maximum, bounds), 2.0**-100)))


def coded(values, level):
    rows = values.shape[0]
    padded = jnp.pad(values * jnp.exp2(13.0 - level), ((0, 16), (0, 0)))
    is_value = lax.broadcasted_iota(jnp.int32, padded.shape, 0) < rows
    return jnp.where(is_value, padded, level).astype(jnp.float16)


class Scattered:
    def __init__(self, pairs, first=0):
        self.pairs, self.first = pairs, max(first, 0)
        self.count = 4 - first if first >= 0 else -first
        self.got, self.parts = None, None
        self.level = bound_level(pairs)
        self.product = None

    def grad(self):
        if self.product is None:
            self.product = jnp.concatenate(
                [product_left(left, right) for left, right in self.pairs], axis=0
            )
        return self.product

    def slab(self):
        return self.grad().shape[0] // (2 * self.count)

    def near_message(self):
        grad, slab = self.grad(), self.slab()
        low = lax.axis_index(dp_axis) % 2
        blocks = grad.reshape(self.count, 2 * slab, grad.shape[1])
        give = lax.dynamic_slice_in_dim(blocks, (1 - low) * slab, slab, 1)
        return coded(give.reshape(-1, grad.shape[1]), self.level)

    def send_near(self, message):
        self.got = swap(message, dp_axis, 1)

    def got_level(self):
        return self.got[self.count * self.slab(), 0].astype(jnp.float32)

    def share(self, place):
        grad, slab = self.grad(), self.slab()
        low = lax.axis_index(dp_axis) % 2
        place = jnp.clip(place - self.first, 0, self.count - 1)
        kept = lax.dynamic_slice_in_dim(grad, (2 * place + low) * slab, slab, 0)
        arrived = lax.dynamic_slice_in_dim(self.got, place * slab, slab, 0)
        return kept + arrived.astype(jnp.float32) * jnp.exp2(self.got_level() - 13.0)

    def far_messages(self):
        high = lax.axis_index(dp_axis) // 2
        level = jnp.maximum(self.level, self.got_level()) + 1.0
        return [coded(self.share(high ^ step), level) for step in (1, 2, 3)]

    def send_far(self, messages):
        self.parts = []
        for step, message in zip((1, 2, 3), messages):
            pairs = [
                (2 * source + side, 2 * (source ^ step) + side)
                for source in range(4)
                for side in range(2)
                if self.first <= source ^ step < self.first + self.count
            ]
            self.parts.append(lax.ppermute(message, dp_axis, pairs))

    def total(self):
        if lax.axis_size(dp_axis) != 8:
            return lax.psum_scatter(self.grad(), dp_axis, scatter_dimension=0, tiled=True)
        slab = self.slab()
        total = self.share(lax.axis_index(dp_axis) // 2)
        for part in self.parts:
            level = part[slab, 0].astype(jnp.float32)
            total = total + part[:slab].astype(jnp.float32) * jnp.exp2(level - 13.0)
        return total


class Traffic:
    def __init__(self, plan):
        self.plan, self.groups = plan, {}

    def add(self, name, group):
        self.groups[name] = group
        return group

    def tie(self, value, near, far, arrived):
        near_messages = [group.near_message() for group in near]
        far_messages = [group.far_messages() for group in far]
        parts = [group.parts for group in arrived]
        value, near_messages, far_messages, parts = lax.optimization_barrier(
            (value, near_messages, far_messages, parts)
        )
        for group, message in zip(near, near_messages):
            group.send_near(message)
        for group, messages in zip(far, far_messages):
            group.send_far(messages)
        for group, part in zip(arrived, parts):
            group.parts = part
        return value

    def input_sum(self, partial_term, kernel):
        if lax.axis_size(dp_axis) != 8:
            return tensor_sum(partial_term, jnp.bfloat16, kernel)[0]
        near, far, arrived = [[self.groups[group] for group in part] for part in self.plan[kernel]]
        partial_term = self.tie(partial_term, near, [], [])
        total = tensor_sum(partial_term, jnp.bfloat16, kernel)[0]
        return self.tie(total, [], far, arrived)

    def finish(self, value, names):
        if lax.axis_size(dp_axis) != 8:
            return value
        return self.tie(value, [], [self.groups[name] for name in names], [])


def first_kernel(count, images, *refs):
    notes, class_table, shares = refs[0], refs[1], refs[2 : 2 + count]
    all_notes, classes, wholes = refs[2 + count], refs[3 + count], refs[4 + count : 4 + 2 * count]
    found, note_send, note_recv, class_send, class_recv, own_sem = refs[
        4 + 2 * count : 10 + 2 * count
    ]
    greet(pltpu.get_barrier_semaphore(), (dp_axis,))
    rank = lax.axis_index(dp_axis)
    ring = RingGather(shares, wholes, *refs[10 + 2 * count :])
    note_copies = spread(notes, all_notes, dp_axis, note_send, note_recv)
    all_notes[rank] = notes[...]
    ring.begin()
    for copy in note_copies:
        copy.wait()
    place = lax.broadcasted_iota(jnp.int32, class_table.shape, 1).astype(jnp.float32)
    lane = lax.broadcasted_iota(jnp.int32, found.shape, 1)
    columns = jnp.zeros(found.shape, jnp.float32)
    for image in range(8 * images):
        label = all_notes[image // images, 0:1, image % images : image % images + 1]
        value = jnp.sum(
            jnp.where(place == label, class_table[...], 0.0), axis=1, keepdims=True
        )
        columns = jnp.where(lane == image, value, columns)
    found[...] = columns
    own = pltpu.make_async_copy(found, classes.at[rank], own_sem.at[0])
    own.start()
    class_copies = spread(found, classes, dp_axis, class_send, class_recv)
    for step in (1, 2, 3):
        ring.advance(step)
    ring.finish()
    for copy in class_copies:
        copy.wait()
    own.wait()


def gather_first(notes, class_table, images, shares):
    count = len(shares)
    rows = class_table.shape[0]
    vmem, anywhere = pl.BlockSpec(memory_space=pltpu.VMEM), pl.BlockSpec(memory_space=pl.ANY)
    outs = pl.pallas_call(
        functools.partial(first_kernel, count, images),
        out_shape=[
            jax.ShapeDtypeStruct((8, 8, 128), jnp.float32),
            jax.ShapeDtypeStruct((8, rows, 128), jnp.float32),
        ]
        + [jax.ShapeDtypeStruct((8,) + share.shape, share.dtype) for share in shares],
        in_specs=[vmem, vmem] + [anywhere] * count,
        out_specs=[vmem, vmem] + [anywhere] * count,
        scratch_shapes=[pltpu.VMEM((rows, 128), jnp.float32)]
        + [pltpu.SemaphoreType.DMA((7,))] * 4
        + [pltpu.SemaphoreType.DMA((1,))]
        + ring_scratch(count),
        compiler_params=pltpu.CompilerParams(
            collective_id=first_gather, has_side_effects=True, vmem_limit_bytes=16 << 20
        ),
    )(notes, class_table, *shares)
    return outs[0], outs[1], outs[2:]


def scatter_small(grad):
    if lax.axis_size(dp_axis) != 8:
        return lax.psum_scatter(grad, dp_axis, scatter_dimension=0, tiled=True)
    rank = lax.axis_index(dp_axis)
    low, high = rank % 2, rank // 2
    slab, columns = grad.shape[0] // 8, grad.shape[1]
    blocks = grad.reshape(4, 2 * slab, columns)
    keep = lax.dynamic_slice_in_dim(blocks, low * slab, slab, 1)
    give = lax.dynamic_slice_in_dim(blocks, (1 - low) * slab, slab, 1)
    pairs = keep + swap(give, dp_axis, 1)
    total = pick(pairs, high)
    for step in (1, 2, 3):
        total = total + swap(pick(pairs, high ^ step), dp_axis, 2 * step)
    return total


def take_pieces(vector, starts, counts):
    return jnp.concatenate(
        [lax.dynamic_slice_in_dim(vector, start, count) for start, count in zip(starts, counts)]
    )


def place_pieces(total, pieces, starts):
    full = jnp.zeros((total,), jnp.float32)
    for piece, start in zip(pieces, starts):
        full = lax.dynamic_update_slice_in_dim(full, piece, start, 0)
    return full


def score_block(queries, key_rows, visible):
    scores = jnp.einsum(
        "bqhd,bkhd->bhqk", queries, key_rows, preferred_element_type=jnp.float32
    ) * HEAD ** (-0.5)
    return scores + (visible[:, None, None, :] - 1.0) * 1000000000.0


def attention(queries, key_rows, value_rows, visible):
    scores = score_block(queries, key_rows, visible)
    largest = jnp.max(scores, axis=-1, keepdims=True)
    exponent = jnp.exp(scores - largest)
    normaliser = jnp.sum(exponent, axis=-1, keepdims=True)
    chance = narrow(exponent / normaliser)
    attended = narrow(
        jnp.einsum("bhqk,bkhd->bqhd", chance, value_rows, preferred_element_type=jnp.float32)
    )
    return (attended, largest + jnp.log(normaliser))


def attention_back(queries, key_rows, value_rows, visible, log_total, grad_attended):
    chance = jnp.exp(score_block(queries, key_rows, visible) - log_total)
    grad_values = jnp.einsum(
        "bhqk,bqhd->bkhd", narrow(chance), grad_attended, preferred_element_type=jnp.float32
    )
    grad_chance = jnp.einsum(
        "bqhd,bkhd->bhqk", grad_attended, value_rows, preferred_element_type=jnp.float32
    )
    grad_scores = narrow(
        chance * (grad_chance - jnp.sum(chance * grad_chance, axis=-1, keepdims=True))
    )
    grad_queries = jnp.einsum(
        "bhqk,bkhd->bqhd", grad_scores, key_rows, preferred_element_type=jnp.float32
    ) * HEAD ** (-0.5)
    grad_keys = jnp.einsum(
        "bhqk,bqhd->bkhd", grad_scores, queries, preferred_element_type=jnp.float32
    ) * HEAD ** (-0.5)
    return (grad_queries, grad_keys, grad_values)


def block_forward(
    stream, visible, layer_rows, layer_bias, vectors, kernel, first_shares, last_shares
):
    images = visible.shape[0]
    local_width = D // lax.axis_size(tensor_axis)
    local_ff = FF // lax.axis_size(tensor_axis)
    heads_here = local_width // HEAD
    flat = stream.reshape(-1, D)
    normed = narrow(layer_norm(flat, vectors[0], vectors[1]))
    mixed = narrow(
        product_right(normed, layer_rows[: 3 * local_width]) + layer_bias[: 3 * local_width]
    )
    parts = [
        mixed[:, slot * local_width : (slot + 1) * local_width].reshape(
            images, -1, heads_here, HEAD
        )
        for slot in range(3)
    ]
    attended, log_total = attention(parts[0], parts[1], parts[2], visible)
    attended = attended.reshape(-1, local_width)
    branch, first_wholes = branch_sum(
        product(attended, layer_rows[3 * local_width + local_ff : 4 * local_width + local_ff]),
        kernel,
        first_shares,
    )
    middle = flat + branch + vectors[4]
    second = narrow(layer_norm(middle, vectors[2], vectors[3]))
    inner = (
        product_right(second, layer_rows[3 * local_width : 3 * local_width + local_ff])
        + layer_bias[3 * local_width :]
    )
    active = narrow(exact_gelu(inner))
    branch, last_wholes = branch_sum(
        product(active, layer_rows[4 * local_width + local_ff :]), kernel + 1, last_shares
    )
    result = middle + branch + vectors[5]
    return (
        result.reshape(stream.shape),
        (flat, normed, parts, log_total, attended, middle, second, inner, active),
        first_wholes,
        last_wholes,
    )


def block_back(incoming, visible, layer_rows, vectors, stored, kernel, traffic):
    flat, normed, parts, log_total, attended, middle, second, inner, active = stored
    local_width = D // lax.axis_size(tensor_axis)
    local_ff = FF // lax.axis_size(tensor_axis)
    mix_rows = layer_rows[: 3 * local_width]
    up_rows = layer_rows[3 * local_width : 3 * local_width + local_ff]
    proj_rows = layer_rows[3 * local_width + local_ff : 4 * local_width + local_ff]
    down_rows = layer_rows[4 * local_width + local_ff :]
    flow = incoming.reshape(-1, D)
    grad_branch = narrow(flow)
    grad_active = product_right(grad_branch, down_rows)
    grad_inner = narrow(local_back(exact_gelu, inner, grad_active))
    grad_second = traffic.input_sum(product(grad_inner, up_rows), kernel)
    grad_middle, grad_gain_two, grad_shift_two = jax.vjp(
        layer_norm, middle, vectors[2], vectors[3]
    )[1](grad_second)
    grad_middle = flow + grad_middle
    grad_attn = narrow(grad_middle)
    grad_attended = narrow(product_right(grad_attn, proj_rows)).reshape(parts[0].shape)
    grads_mixed = attention_back(parts[0], parts[1], parts[2], visible, log_total, grad_attended)
    grad_mixed = narrow(
        jnp.concatenate([piece.reshape(-1, local_width) for piece in grads_mixed], axis=1)
    )
    mix = [(grad_mixed, normed)]
    later = [(grad_inner, second), (attended, grad_attn), (active, grad_branch)]
    if kernel == back_encoder and lax.axis_size(dp_axis) == 8:
        owned_rows = [
            traffic.add(mix_group, Scattered(mix, -1)),
            traffic.add(kernel, Scattered(later, 1)),
        ]
    else:
        owned_rows = [traffic.add(kernel, Scattered(mix + later))]
    grad_normed = traffic.input_sum(product(grad_mixed, mix_rows), kernel + 1)
    grad_flat, grad_gain_one, grad_shift_one = jax.vjp(layer_norm, flat, vectors[0], vectors[1])[1](
        grad_normed
    )
    grad_bias = jnp.concatenate([column_sum(grad_mixed), column_sum(grad_inner)])
    grad_vectors = jnp.stack(
        [
            grad_gain_one,
            grad_shift_one,
            grad_gain_two,
            grad_shift_two,
            column_sum(grad_attn),
            column_sum(grad_branch),
        ]
    )
    return ((grad_middle + grad_flat).reshape(incoming.shape), owned_rows, grad_bias, grad_vectors)


def gathered_parts(columns, count):
    width = columns.shape[1] // count
    blocks = [block.astype(jnp.float32) for block in tensor_blocks(narrow(columns))]
    return [
        jnp.concatenate([block[:, slot * width : (slot + 1) * width] for block in blocks], axis=1)
        for slot in range(count)
    ]


def adaptive_vectors(cond_act, segment_rows, segment_bias):
    local_hidden = HW // lax.axis_size(tensor_axis)
    adaptive = (
        product_right(cond_act, segment_rows[: 3 * local_hidden]) + segment_bias[: 3 * local_hidden]
    )
    return gathered_parts(adaptive, 3)


def head_block(hidden_state, vectors, segment_rows, segment_bias, last_bias, kernel):
    local_hidden = HW // lax.axis_size(tensor_axis)
    shift_vec, scale_vec, gate_vec = vectors
    modulated = narrow(modulate(hidden_state, shift_vec, scale_vec))
    inner = (
        product_right(modulated, segment_rows[3 * local_hidden : 4 * local_hidden])
        + segment_bias[3 * local_hidden :]
    )
    active = narrow(jax.nn.silu(inner))
    branch = branch_sum(product(active, segment_rows[4 * local_hidden :]), kernel)[0] + last_bias
    return (
        hidden_state + gate_vec * branch,
        (hidden_state, shift_vec, scale_vec, gate_vec, modulated, inner, active, branch),
    )


def head_block_back(incoming, cond_act, segment_rows, offset, stored, kernel, traffic):
    hidden_state, shift_vec, scale_vec, gate_vec, modulated, inner, active, branch = stored
    local_hidden = HW // lax.axis_size(tensor_axis)
    grad_gate = incoming * branch
    grad_branch = narrow(incoming * gate_vec)
    grad_active = product_right(grad_branch, segment_rows[4 * local_hidden :])
    grad_inner = narrow(local_back(jax.nn.silu, inner, grad_active))
    grad_modulated = traffic.input_sum(
        product(grad_inner, segment_rows[3 * local_hidden : 4 * local_hidden]), kernel
    )
    grad_hidden, grad_shift, grad_scale = jax.vjp(modulate, hidden_state, shift_vec, scale_vec)[1](
        grad_modulated
    )
    grad_adaptive = narrow(
        jnp.concatenate(
            [
                lax.dynamic_slice_in_dim(piece, offset, local_hidden, 1)
                for piece in (grad_shift, grad_scale, grad_gate)
            ],
            axis=1,
        )
    )
    grad_cond = product(grad_adaptive, segment_rows[: 3 * local_hidden])
    owned_rows = traffic.add(
        kernel,
        Scattered([(grad_adaptive, cond_act), (grad_inner, modulated), (active, grad_branch)]),
    )
    grad_bias = jnp.concatenate([column_sum(grad_adaptive), column_sum(grad_inner)])
    return (incoming + grad_hidden, grad_cond, owned_rows, grad_bias, column_sum(grad_branch))


def adam_update(weight, moment_one, moment_two, gradient, factor, step_num):
    gradient = gradient * factor
    moment_one = beta_first * moment_one + (1.0 - beta_first) * gradient
    moment_two = beta_second * moment_two + (1.0 - beta_second) * gradient * gradient
    fixed_one = moment_one / (1.0 - beta_first**step_num)
    fixed_two = moment_two / (1.0 - beta_second**step_num)
    weight = weight - learn_rate * (
        fixed_one / (jnp.sqrt(fixed_two) + adam_eps) + decay_rate * weight
    )
    return (weight, moment_one, moment_two)


def local(
    block_weights,
    head_weights,
    head_rest,
    embed_tables,
    bias_rows,
    first_blocks,
    second_blocks,
    first_head,
    second_head,
    first_rest,
    second_rest,
    first_tables,
    second_tables,
    first_bias,
    second_bias,
    patches,
    noise,
    token_mask,
    labels,
    drop_marks,
    timesteps,
    step_weights,
    step_count,
):
    tensor_size = lax.axis_size(tensor_axis)
    tensor_index = lax.axis_index(tensor_axis)
    local_width = D // tensor_size
    local_ff = FF // tensor_size
    local_hidden = HW // tensor_size
    offset = tensor_index * local_hidden
    column_starts = [slot * D + tensor_index * local_width for slot in range(3)] + [
        3 * D + tensor_index * local_ff
    ]
    column_counts = [local_width] * 3 + [local_ff]
    head_starts = [slot * HW + offset for slot in range(4)]
    dp_size = lax.axis_size(dp_axis)
    dp_index = lax.axis_index(dp_axis)
    images = patches.shape[0]
    all_images = dp_size * images
    mask_float = token_mask.astype(jnp.float32)
    matches = timesteps[..., None] == jnp.arange(T_STEPS)
    row_weight = (
        jnp.sum(jnp.where(matches, step_weights, 0.0), axis=-1) * mask_float[None]
    ).reshape(-1)
    chosen = jnp.where(drop_marks == 1, CLASSES, labels)
    class_at = TOKD + 1
    class_end = class_at + CLASSES + 1
    weight_here = jnp.sum(row_weight)
    table_share = jnp.concatenate(
        [embed_tables[:, :class_at], embed_tables[:, class_end:]], axis=1
    )
    class_share = embed_tables[:, class_at:class_end]
    block_share = narrow(block_weights)
    if dp_size == 8:
        notes = jnp.zeros((8, 128), jnp.float32)
        notes = lax.dynamic_update_slice(notes, chosen.astype(jnp.float32)[None], (0, 0))
        notes = lax.dynamic_update_slice(notes, weight_here[None, None], (1, 0))
        all_notes, classes, (table_cols, first_block) = gather_first(
            notes, class_share, images, [table_share, block_share[0]]
        )
        all_chosen = all_notes[:, 0, :images].reshape(-1)
        weight_total = jnp.sum(all_notes[:, 1, 0])
        class_rows = lax.dynamic_slice_in_dim(
            classes.reshape(-1, classes.shape[-1]), dp_index * images, images, 1
        ).T
    else:
        all_chosen = lax.all_gather(chosen, dp_axis, axis=0, tiled=True).astype(jnp.float32)
        weight_total = lax.psum(weight_here, dp_axis)
        table_cols = lax.all_gather(table_share, dp_axis)
        first_block = lax.all_gather(block_share[0], dp_axis)
    picker = (all_chosen[:, None] == jnp.arange(CLASSES + 1)[None, :]).astype(jnp.float32)
    if dp_size != 8:
        found = lax.dot_general(
            class_share, picker, (((1,), (1,)), ((), ())), precision=highest
        )
        class_rows = lax.dynamic_slice_in_dim(
            lax.all_gather(found, dp_axis, axis=0, tiled=True), dp_index * images, images, 1
        ).T
    table_cols = table_cols.reshape(-1, table_cols.shape[-1])
    first_block = first_block.reshape(-1, D)
    share_rows = block_share[1].shape[0] // 2
    rest_share = narrow(head_rest)
    rest_rows_here = rest_share.shape[0] // 2
    flat_bias = bias_rows.reshape(-1)
    rest_bias = flat_bias[: 6 * HW].reshape(6, HW)
    head_bias = flat_bias[6 * HW : 6 * HW + 5 * HB * HW].reshape(HB, 5 * HW)
    column_bias = flat_bias[6 * HW + 5 * HB * HW :].reshape(LAYERS, 3 * D + FF)
    table_parts = cut_rows(table_cols.T, (TOKD, 1, TOK + BUF, TOK + BUF, 1, 6 * LAYERS, 4))
    layer_vectors = table_parts[5].reshape(LAYERS, 6, D)
    final_norms = table_parts[6]
    patch_flat = patches.reshape(-1, TOKD)
    tokens = product(patch_flat, narrow(table_parts[0])) + table_parts[1][0]
    stream = (
        jnp.concatenate(
            [
                jnp.broadcast_to(class_rows[:, None, :], (images, BUF, D)),
                tokens.reshape(images, TOK, D),
            ],
            axis=1,
        )
        + table_parts[2]
    )
    buffer_ones = jnp.ones((images, BUF), jnp.float32)
    visible_enc = jnp.concatenate([buffer_ones, 1.0 - mask_float], axis=1)
    visible_all = jnp.ones((images, TOK + BUF), jnp.float32)
    hidden_rows = jnp.concatenate([0.0 * buffer_ones, mask_float], axis=1)[..., None]
    layer_bias = [
        take_pieces(column_bias[layer], column_starts, column_counts) for layer in range(LAYERS)
    ]
    encoded, stored_enc, first_half, last_half = block_forward(
        stream,
        visible_enc,
        first_block,
        layer_bias[0],
        layer_vectors[0],
        encoder_forward,
        [block_share[1][:share_rows]],
        [block_share[1][share_rows:]],
    )
    encoded, head_share = lax.optimization_barrier((encoded, narrow(head_weights)))
    head_all = lax.all_gather(head_share, dp_axis, axis=1, tiled=True)
    second_block = jnp.concatenate([first_half[0], last_half[0]], axis=1).reshape(-1, D)
    block_all = [first_block, second_block]
    enc_normed = layer_norm(encoded, final_norms[0], final_norms[1])
    decoder_in = enc_normed * (1.0 - hidden_rows) + table_parts[4][0] * hidden_rows + table_parts[3]
    decoded, stored_dec, first_half, last_half = block_forward(
        decoder_in,
        visible_all,
        second_block,
        layer_bias[1],
        layer_vectors[1],
        decoder_forward,
        [rest_share[:rest_rows_here]],
        [rest_share[rest_rows_here:]],
    )
    rest_rows = jnp.concatenate([first_half[0], last_half[0]], axis=1)
    rest_rows = rest_rows.reshape(-1, rest_rows.shape[-1])
    cond_mine, input_mine, output_mine, time_first, second_mine, final_shift, final_scale = cut_rows(
        rest_rows, (D, TOKD, TOKD, HW, HW, HW, HW)
    )
    cond_weight, input_weight, output_weight, time_second = cut_rows(
        tensor_columns(jnp.concatenate([cond_mine, input_mine, output_mine, second_mine], axis=0)),
        (D, TOKD, TOKD, HW),
    )
    latent = narrow(layer_norm(decoded, final_norms[2], final_norms[3])[:, BUF:].reshape(-1, D))
    condition = product(latent, cond_weight) + rest_bias[0]
    step_rows = timesteps.reshape(COPIES, -1)
    time_feat = narrow(sinusoid(step_rows).reshape(-1, HW))
    time_pre = product(time_feat, time_first) + lax.dynamic_slice_in_dim(
        rest_bias[2], offset, local_hidden
    )
    time_act = tensor_columns(narrow(jax.nn.silu(time_pre)))
    time_embed = product(time_act, time_second) + rest_bias[3]
    cond_vec = (condition[None] + time_embed.reshape(COPIES, -1, HW)).reshape(-1, HW)
    cond_act = narrow(jax.nn.silu(cond_vec))
    phase = step_rows.astype(jnp.float32)[..., None] * (math.pi / (2 * T_STEPS))
    signal_coef = jnp.cos(phase)
    noise_coef = jnp.sin(phase)
    clean = patch_flat.astype(jnp.float32)[None]
    noise_rows = noise.reshape(COPIES, -1, TOKD).astype(jnp.float32)
    noisy_rows = narrow((signal_coef * clean + noise_coef * noise_rows).reshape(-1, TOKD))
    target = (signal_coef * noise_rows - noise_coef * clean).reshape(-1, TOKD)
    hidden_state = product(noisy_rows, input_weight) + rest_bias[1]
    stored_head = []
    segment_biases = [
        take_pieces(head_bias[segment], head_starts, [local_hidden] * 4) for segment in range(HB)
    ]
    head_vectors = [
        adaptive_vectors(cond_act, head_all[segment], segment_biases[segment])
        for segment in range(HB)
    ]
    last_pair = jnp.concatenate(
        [product(cond_act, final_shift), product(cond_act, final_scale)], axis=1
    ) + take_pieces(flat_bias, [4 * HW + offset, 5 * HW + offset], [local_hidden] * 2)
    shift_last, scale_last = gathered_parts(last_pair, 2)
    for segment in range(HB):
        hidden_state, stored = head_block(
            hidden_state,
            head_vectors[segment],
            head_all[segment],
            segment_biases[segment],
            head_bias[segment, 4 * HW :],
            head_forward + segment,
        )
        stored_head.append(stored)
    final_in = narrow(modulate(hidden_state, shift_last, scale_last))
    predicted = product_right(final_in, output_weight)
    sq_error = jnp.mean((predicted - target) ** 2, axis=-1)
    numerator = jnp.sum(row_weight * sq_error)
    grad_pred = narrow(2.0 / (TOKD * weight_total) * row_weight[:, None] * (predicted - target))
    grad_final = product(grad_pred, output_weight)
    grad_hidden, grad_shift_last, grad_scale_last = jax.vjp(
        modulate, hidden_state, shift_last, scale_last
    )[1](grad_final)

    def own_columns(value):
        return lax.dynamic_slice_in_dim(value, offset, local_hidden, 1)

    grad_shift_last = narrow(own_columns(grad_shift_last))
    grad_scale_last = narrow(own_columns(grad_scale_last))
    traffic = Traffic(
        {
            back_head + 1: ([], [], []),
            back_head: ([back_head + 1], [], []),
            back_cond: ([back_head], [back_head + 1], []),
            back_decoder: ([rest_group], [back_head], [back_head + 1]),
            back_decoder + 1: ([back_decoder], [rest_group], [back_head]),
            back_encoder: ([], [back_decoder], [rest_group]),
            back_encoder + 1: ([back_encoder, mix_group], [back_encoder], [back_decoder]),
        }
    )
    cond_split = product_right(grad_shift_last, final_shift) + product_right(
        grad_scale_last, final_scale
    )
    head_grads = []
    head_bias_grads = []
    for segment in reversed(range(HB)):
        grad_hidden, grad_cond, grad_segment, grad_segment_bias, grad_last_bias = head_block_back(
            grad_hidden,
            cond_act,
            head_all[segment],
            offset,
            stored_head[segment],
            back_head + segment,
            traffic,
        )
        cond_split = cond_split + grad_cond
        head_grads.insert(0, grad_segment)
        pieces = [
            grad_segment_bias[slot * local_hidden : (slot + 1) * local_hidden] for slot in range(4)
        ] + [grad_last_bias / tensor_size]
        head_bias_grads.insert(0, place_pieces(5 * HW, pieces, head_starts + [4 * HW]))
    grad_input = narrow(grad_hidden)
    grad_cond_vec = narrow(local_back(jax.nn.silu, cond_vec, traffic.input_sum(cond_split, back_cond)))
    cond_bias_grad = column_sum(grad_cond_vec)
    grad_time_act = product_right(
        grad_cond_vec, lax.dynamic_slice_in_dim(time_second, offset, local_hidden, 0)
    )
    grad_time_pre = narrow(local_back(jax.nn.silu, time_pre, grad_time_act))
    grad_latent = jnp.sum(product(grad_cond_vec, cond_weight.T).reshape(COPIES, -1, D), axis=0)
    grad_cond_mine = own_columns(grad_cond_vec)
    owned_rest = Scattered(
        [
            (jnp.tile(latent, (COPIES, 1)), grad_cond_mine),
            (noisy_rows, own_columns(grad_input)),
            (grad_pred, own_columns(final_in)),
            (time_feat, grad_time_pre),
            (time_act, grad_cond_mine),
            (cond_act, grad_shift_last),
            (cond_act, grad_scale_last),
        ]
    )
    traffic.add(rest_group, owned_rest)
    rest_bias_grad = place_pieces(
        6 * HW,
        [
            cond_bias_grad / tensor_size,
            column_sum(grad_input) / tensor_size,
            column_sum(grad_time_pre),
            cond_bias_grad / tensor_size,
            column_sum(grad_shift_last),
            column_sum(grad_scale_last),
        ],
        [0, HW, 2 * HW + offset, 3 * HW, 4 * HW + offset, 5 * HW + offset],
    )
    grad_top = jnp.concatenate(
        [jnp.zeros((images, BUF, D), jnp.float32), grad_latent.reshape(images, TOK, D)], axis=1
    )
    grad_decoded, grad_gain_dec, grad_shift_dec = jax.vjp(
        layer_norm, decoded, final_norms[2], final_norms[3]
    )[1](grad_top)
    grad_dec_in, grad_rows_dec, grad_bias_dec, grad_vec_dec = block_back(
        grad_decoded, visible_all, block_all[1], layer_vectors[1], stored_dec, back_decoder, traffic
    )
    grad_encoded, grad_gain_enc, grad_shift_enc = jax.vjp(
        layer_norm, encoded, final_norms[0], final_norms[1]
    )[1](grad_dec_in * (1.0 - hidden_rows))
    grad_stream, grad_rows_enc, grad_bias_enc, grad_vec_enc = block_back(
        grad_encoded, visible_enc, block_all[0], layer_vectors[0], stored_enc, back_encoder, traffic
    )
    grad_stream, bias_parts = traffic.finish(
        (grad_stream, [rest_bias_grad] + head_bias_grads),
        [mix_group],
    )
    grad_tokens = narrow(grad_stream[:, BUF:].reshape(-1, D))
    grad_class = lax.dynamic_update_slice_in_dim(
        jnp.zeros((all_images, D), jnp.float32),
        jnp.sum(grad_stream[:, :BUF], axis=1),
        dp_index * images,
        0,
    )
    small_rows = jnp.concatenate(
        [
            column_sum(grad_tokens)[None],
            jnp.sum(grad_dec_in * hidden_rows, axis=(0, 1))[None],
            grad_vec_enc,
            grad_vec_dec,
            jnp.stack([grad_gain_enc, grad_shift_enc, grad_gain_dec, grad_shift_dec]),
            grad_class,
        ],
        axis=0,
    )
    seq_rows = TOK + BUF
    small_at = 2 * seq_rows + TOKD
    table_count = small_at + small_rows.shape[0]
    quarter = -(-table_count // (8 * tensor_size)) * 8
    small_rows = jnp.pad(small_rows, ((0, quarter * tensor_size - table_count), (0, 0)))
    grad_tables = jnp.concatenate(
        [
            jnp.sum(grad_stream, axis=0),
            jnp.sum(grad_dec_in, axis=0),
            product_left(patch_flat, grad_tokens),
            small_rows,
        ],
        axis=0,
    )
    grad_tables = lax.dynamic_slice_in_dim(grad_tables, tensor_index * quarter, quarter, 0)
    owned_cols = tensor_columns(scatter_small(grad_tables.T))
    class_cols = small_at + 6 * LAYERS + 6
    owned_tables = jnp.concatenate(
        [
            owned_cols[:, 2 * seq_rows : small_at + 1],
            jnp.dot(
                owned_cols[:, class_cols : class_cols + all_images], picker, precision=highest
            ),
            owned_cols[:, : 2 * seq_rows],
            owned_cols[:, small_at + 1 : class_cols],
        ],
        axis=1,
    )
    encoder_shares = [group.total() for group in grad_rows_enc]
    if len(encoder_shares) == 2:
        encoder_shares = [jnp.where(dp_index < 2, encoder_shares[0], encoder_shares[1])]
    owned_blocks = jnp.stack(encoder_shares + [grad_rows_dec[0].total()])
    owned_head = jnp.stack([group.total() for group in head_grads])
    owned_rest = owned_rest.total()
    column_grads = []
    for grad_local in (grad_bias_enc, grad_bias_dec):
        pieces = [
            grad_local[slot * local_width : (slot + 1) * local_width] for slot in range(3)
        ] + [grad_local[3 * local_width :]]
        column_grads.append(place_pieces(3 * D + FF, pieces, column_starts))
    lanes = bias_rows.shape[1]
    bias_grad = sum_everywhere(
        jnp.concatenate(bias_parts + column_grads).reshape(-1, lanes), (tensor_axis, dp_axis)
    )
    split_squares = (
        jnp.sum(owned_blocks * owned_blocks)
        + jnp.sum(owned_head * owned_head)
        + jnp.sum(owned_rest * owned_rest)
    )
    shared_squares = jnp.sum(owned_tables * owned_tables) / tensor_size
    every_squares = jnp.sum(bias_grad * bias_grad) / (tensor_size * lax.axis_size(dp_axis))
    last_sums = small_sums(
        [split_squares + shared_squares + every_squares, numerator / tensor_size]
    )
    norm_square = last_sums[0]
    loss_value = last_sums[1] / weight_total
    grad_norm = jnp.sqrt(norm_square)
    factor = jnp.minimum(1.0, clip_limit / (grad_norm + 1e-06))
    step_num = step_count[0].astype(jnp.float32)
    blocks_new, blocks_first, blocks_second = adam_update(
        block_weights, first_blocks, second_blocks, owned_blocks, factor, step_num
    )
    head_new, head_first, head_second = adam_update(
        head_weights, first_head, second_head, owned_head, factor, step_num
    )
    rest_new, rest_first, rest_second = adam_update(
        head_rest, first_rest, second_rest, owned_rest, factor, step_num
    )
    tables_new, tables_first, tables_second = adam_update(
        embed_tables, first_tables, second_tables, owned_tables, factor, step_num
    )
    bias_new, bias_first, bias_second = adam_update(
        bias_rows, first_bias, second_bias, bias_grad, factor, step_num
    )
    return (
        loss_value,
        grad_norm,
        blocks_new,
        blocks_first,
        blocks_second,
        narrow(blocks_new),
        head_new,
        head_first,
        head_second,
        narrow(head_new),
        rest_new,
        rest_first,
        rest_second,
        narrow(rest_new),
        tables_new,
        tables_first,
        tables_second,
        narrow(tables_new),
        bias_new,
        bias_first,
        bias_second,
        narrow(bias_new),
    )


def solution(mesh):
    in_specs = (
        P(None, (dp_axis, tensor_axis), None),
        P(None, (dp_axis, tensor_axis), None),
        P(dp_axis, tensor_axis),
        P(dp_axis, None),
        P(),
        P(None, (dp_axis, tensor_axis), None),
        P(None, (dp_axis, tensor_axis), None),
        P(None, (dp_axis, tensor_axis), None),
        P(None, (dp_axis, tensor_axis), None),
        P(dp_axis, tensor_axis),
        P(dp_axis, tensor_axis),
        P(dp_axis, None),
        P(dp_axis, None),
        P(),
        P(),
        P(dp_axis, None, None),
        P(None, dp_axis, None, None),
        P(dp_axis, None),
        P(dp_axis),
        P(dp_axis),
        P(None, dp_axis, None),
        P(),
        P(),
    )
    out_specs = (
        P(),
        P(),
        P(None, (dp_axis, tensor_axis), None),
        P(None, (dp_axis, tensor_axis), None),
        P(None, (dp_axis, tensor_axis), None),
        P(None, (dp_axis, tensor_axis), None),
        P(None, (dp_axis, tensor_axis), None),
        P(None, (dp_axis, tensor_axis), None),
        P(None, (dp_axis, tensor_axis), None),
        P(None, (dp_axis, tensor_axis), None),
        P(dp_axis, tensor_axis),
        P(dp_axis, tensor_axis),
        P(dp_axis, tensor_axis),
        P(dp_axis, tensor_axis),
        P(dp_axis, None),
        P(dp_axis, None),
        P(dp_axis, None),
        P(dp_axis, None),
        P(),
        P(),
        P(),
        P(),
    )
    return jax.shard_map(local, mesh=mesh, in_specs=in_specs, out_specs=out_specs, check_vma=False)
```

time: 1060 us -> 941 us (0.89)
  waiting for transfers between devices: 504 us -> 108 us
  Pallas kernels: 0 us -> 307 us
  starting transfers between devices: 98.3 us -> 65.4 us
  between operations: 48.8 us -> 74.1 us
  other arithmetic: 185 us -> 165 us
    pallas_call x0 -> x15, Pallas kernels: none -> 307 us  [the longest x13 205 us: tensor_sum(): pl.pallas_call(functools.partial(sum_kernel, count, cross_type), out_shap...]
    ppermute x104 -> x33, waiting for transfers between devices: 290 us -> 79.6 us  [swap(): lax.ppermute(value, axis, [(i, i ^ step) for i in range(lax.axis_size(axi...]
    all_gather x6 -> x1, waiting for transfers between devices: 213 us -> 22.9 us  [local(): head_all = lax.all_gather(head_share, dp_axis, axis=1, tiled=True)]
    ppermute x104 -> x33, starting transfers between devices: 97.8 us -> 33.4 us  [swap(): lax.ppermute(value, axis, [(i, i ^ step) for i in range(lax.axis_size(axi...]
    concatenate x22 -> x4, local copies, waits for them, and re-layouts: 34.3 us -> 1.68 us  [the longest x1 1.32 us: local(): jnp.concatenate([owned_cols[:, 2 * seq_rows:small_at + 1], jnp.dot(owned_...]
    ppermute x0 -> x18, starting transfers between devices: none -> 32.1 us  [send_far(): self.parts.append(lax.ppermute(message, dp_axis, pairs))]
    add x28 -> x2, other arithmetic: 27.5 us -> 1.23 us  [the longest x1 0.97 us: scatter_small(): total = total + swap(pick(pairs, high ^ step), dp_axis, 2 * step)]
    unnamed x626 -> x703, local copies, waits for them, and re-layouts: 22.9 us -> 36.9 us
  transfers between devices with their start and end apart: 110 -> 52, of which waited for: 45 -> 11; matrix products, arithmetic and copies ran while one was open for 29% -> 17% of each run, Pallas kernels for 0% -> 6%
where the time goes in v2:
time: 941 us; the launch traced here: 928 us
  Pallas kernels  307 us (33%)
  other arithmetic  165 us (18%)
  local copies, waits for them, and re-layouts  115 us (12%)
  waiting for transfers between devices  108 us (11%)
  matrix products  93.6 us (10%)
  between operations  74.1 us (8%)
  starting transfers between devices  65.4 us (7%)
    pallas_call x13, Pallas kernels, tensor_sum(): pl.pallas_call(functools.partial(sum_kernel, count, cross_type), out_shap...  205 us
    ppermute x33, waiting for transfers between devices, swap(): lax.ppermute(value, axis, [(i, i ^ step) for i in range(lax.axis_size(axi...  79.6 us
    pallas_call x1, Pallas kernels, gather_first(): pl.pallas_call(functools.partial(first_kernel, count, images), out_shape=...  75.3 us
    unnamed x703, local copies, waits for them, and re-layouts  36.9 us
    dot_general x18, matrix products, product_right(): lax.dot_general(left, right, (((1,), (1,)), ((), ())), preferred_element_...  35.3 us
    ppermute x33, starting transfers between devices, swap(): lax.ppermute(value, axis, [(i, i ^ step) for i in range(lax.axis_size(axi...  33.4 us
    ppermute x18, starting transfers between devices, send_far(): self.parts.append(lax.ppermute(message, dp_axis, pairs))  32.1 us
    dot_general x22, matrix products, product_left(): lax.dot_general(left, right, (((0,), (0,)), ((), ())), preferred_element_...  31.6 us
  transfers between devices with their start and end apart: 52, of which 11 were waited for; matrix products, arithmetic and copies ran while one was open for 17% of the time, Pallas kernels for 6%

profile of v2, /device:TPU:0, one launch (start us, length us, event | category | flops | bytes accessed | tf_op | source)
XLA Modules:
  0.0 927.9 jit_solution(9434811873145577688)
XLA Ops:
  30.4 75.3 %shard_map.393 = (f32[8,8,128]{2,1,0:T(8,128)S(1)}, f32[8,96,128]{2,1,0:T(8,128)S(1)}, f32[8,96,722]{2,1,0:T(8,128)S(1)}, bf16[8,288,768]{2,1,0:T(8,128)(2,1)S(1)}) custom-call(f32[8,128]{1,0:T(8,128)S(1)} %dynamic_update_slice.82.refs_0_, f32[96,1001]{1,0:T(8,128)S(1)} %copy-done.6, f32[96,722]{1,0:T(8,128)S(1)} %copy-done.7, bf16[288,768]{1,0:T(8,128)(2,1)S(1)} %copy-done.5), custom_call_target="tpu_custom_call" | custom-call | tf_op jit(solution)/shard_map/pallas_call | solution.py:523
  108.4 4.3 copy.95
  137.2 29.2 %shard_map.394 = (f32[320,768]{1,0:T(8,128)S(1)}, bf16[8,144,768]{2,1,0:T(8,128)(2,1)S(1)}) custom-call(f32[320,768]{1,0:T(8,128)S(1)} %fusion.156.refs_0_, bf16[144,768]{1,0:T(8,128)(2,1)S(1)} %copy-done.9), custom_call_target="tpu_custom_call" | custom-call | bytes 2000000 | tf_op jit(solution)/shard_map/pallas_call | solution.py:239
  168.6 4.5 abs_reduce_fusion.6
  174.2 24.9 %shard_map.395 = (f32[320,768]{1,0:T(8,128)S(1)}, bf16[8,144,768]{2,1,0:T(8,128)(2,1)S(1)}) custom-call(f32[320,768]{1,0:T(8,128)S(1)} %fusion.53.refs_0_, bf16[144,768]{1,0:T(8,128)(2,1)S(1)} %copy-done.8), custom_call_target="tpu_custom_call" | custom-call | bytes 2000000 | tf_op jit(solution)/shard_map/pallas_call | solution.py:239
  208.6 21.1 %shard_map.396 = (f32[320,768]{1,0:T(8,128)S(1)}, bf16[8,312,256]{2,1,0:T(8,128)(2,1)S(1)}) custom-call(f32[320,768]{1,0:T(8,128)S(1)} %fusion.153.refs_0_, bf16[312,256]{1,0:T(8,128)(2,1)S(1)} %copy-done.11), custom_call_target="tpu_custom_call" | custom-call | bytes 2000000 | tf_op jit(solution)/shard_map/pallas_call | solution.py:239
  232.9 4.5 abs_reduce_fusion.8
  241.7 22.5 %shard_map.397 = (f32[320,768]{1,0:T(8,128)S(1)}, bf16[8,312,256]{2,1,0:T(8,128)(2,1)S(1)}) custom-call(f32[320,768]{1,0:T(8,128)S(1)} %fusion.46.refs_0_, bf16[312,256]{1,0:T(8,128)(2,1)S(1)} %copy-done.10), custom_call_target="tpu_custom_call" | custom-call | bytes 2000000 | tf_op jit(solution)/shard_map/pallas_call | solution.py:239
  283.0 11.9 %collective-permute-done.1 = bf16[1920,256]{1,0:T(8,128)(2,1)} collective-permute-done((bf16[1920,256]{1,0:T(8,128)(2,1)}, bf16[1920,256]{1,0:T(8,128)(2,1)}, u32[]{:S(2)}, u32[]{:S(2)}) %collective-permute-start.1) | collective-permute-done | bytes 983072 | tf_op jit(solution)/shard_map/ppermute | solution.py:96
  317.7 5.8 collective-permute-done.13
  329.7 22.9 %all-gather.2.cloned.1.call-done = bf16[2,1280,1024]{2,1,0:T(8,128)(2,1)} async-done(((bf16[2,160,1024]{2,1,0:T(8,128)(2,1)}), bf16[2,1280,1024]{2,1,0:T(8,128)(2,1)}) %all-gather.2.cloned.1.call-update) | async-done | bytes 5242896 | tf_op jit(solution)/shard_map/all_gather | solution.py:902
  358.9 7.8 collective-permute-done.10
  367.4 5.7 collective-permute-done.7
  380.8 12.1 %shard_map.398 = f32[256,1024]{1,0:T(8,128)S(1)} custom-call(f32[256,1024]{1,0:T(8,128)S(1)} %fusion.119.refs_0_), custom_call_target="tpu_custom_call" | custom-call | bytes 2000000 | tf_op jit(solution)/shard_map/pallas_call | solution.py:239
  396.6 12.1 %shard_map.399 = f32[256,1024]{1,0:T(8,128)S(1)} custom-call(f32[256,1024]{1,0:T(8,128)S(1)} %fusion.122.refs_0_), custom_call_target="tpu_custom_call" | custom-call | bytes 2000000 | tf_op jit(solution)/shard_map/pallas_call | solution.py:239
  417.8 12.1 %shard_map.400 = f32[256,1024]{1,0:T(8,128)S(1)} custom-call(f32[256,1024]{1,0:T(8,128)S(1)} %fusion.120.refs_0_), custom_call_target="tpu_custom_call" | custom-call | bytes 2000000 | tf_op jit(solution)/shard_map/pallas_call | solution.py:239
  456.5 12.1 %shard_map.401 = f32[256,1024]{1,0:T(8,128)S(1)} custom-call(f32[256,1024]{1,0:T(8,128)S(1)} %fusion.117.refs_0_), custom_call_target="tpu_custom_call" | custom-call | bytes 2000000 | tf_op jit(solution)/shard_map/pallas_call | solution.py:239
  505.5 12.2 %shard_map.402 = f32[256,1024]{1,0:T(8,128)S(1)} custom-call(f32[256,1024]{1,0:T(8,128)S(1)} %fusion.16.refs_0_), custom_call_target="tpu_custom_call" | custom-call | bytes 2000000 | tf_op jit(solution)/shard_map/pallas_call | solution.py:239
  529.4 26.4 %collective-permute-done.16 = f16[656,1024]{1,0:T(8,128)(2,1)} collective-permute-done((f16[656,1024]{1,0:T(8,128)(2,1)}, f16[656,1024]{1,0:T(8,128)(2,1)}, u32[]{:S(2)}, u32[]{:S(2)}) %collective-permute-start.16) | collective-permute-done | bytes 1343520 | tf_op jit(solution)/shard_map/ppermute | solution.py:96
  603.5 11.6 %shard_map.403 = f32[320,768]{1,0:T(8,128)S(1)} custom-call(f32[320,768]{1,0:T(8,128)S(1)} %fusion.48.refs_0_), custom_call_target="tpu_custom_call" | custom-call | bytes 2000000 | tf_op jit(solution)/shard_map/pallas_call | solution.py:239
  630.8 3.6 pad_maximum_fusion
  642.0 11.6 %shard_map.404 = f32[320,768]{1,0:T(8,128)S(1)} custom-call(f32[320,768]{1,0:T(8,128)S(1)} %fusion.209.refs_0_), custom_call_target="tpu_custom_call" | custom-call | bytes 2000000 | tf_op jit(solution)/shard_map/pallas_call | solution.py:239
  675.1 11.7 %shard_map.405 = f32[320,768]{1,0:T(8,128)S(1)} custom-call(f32[320,768]{1,0:T(8,128)S(1)} %fusion.55.refs_0_), custom_call_target="tpu_custom_call" | custom-call | bytes 2000000 | tf_op jit(solution)/shard_map/pallas_call | solution.py:239
  736.4 11.6 %shard_map.406 = f32[320,768]{1,0:T(8,128)S(1)} custom-call(f32[320,768]{1,0:T(8,128)S(1)} %fusion.206.refs_0_), custom_call_target="tpu_custom_call" | custom-call | bytes 2000000 | tf_op jit(solution)/shard_map/pallas_call | solution.py:239
  748.6 12.7 %collective-permute-done.28 = f16[304,768]{1,0:T(8,128)(2,1)S(1)} collective-permute-done((f16[304,768]{1,0:T(8,128)(2,1)S(1)}, f16[304,768]{1,0:T(8,128)(2,1)S(1)}, u32[]{:S(2)}, u32[]{:S(2)}) %collective-permute-start.28) | collective-permute-done | bytes 466976 | tf_op jit(solution)/shard_map/ppermute | solution.py:96
  804.9 4.4 collective-permute-start.41
  819.0 5.4 collective-permute-done.41
  828.8 5.8 collective-permute-start.37
  846.6 5.9 collective-permute-start.50
  854.9 5.2 collective-permute-done.38
  875.0 26.5 %shard_map.407 = f32[8,128]{1,0:T(8,128)} custom-call(f32[8,128]{1,0:T(8,128)} %broadcast_select_fusion.value), custom_call_target="tpu_custom_call" | custom-call | tf_op jit(solution)/shard_map/pallas_call | solution.py:319
  912.5 3.6 fusion.218
  (1215 shorter events, 406.7 us)
Async XLA Ops:
  7.2 345.4 %all-gather.2.cloned.1.call-start = ((), (), s32[]{:S(2)}) async-start(), calls=%async_computation | async-start | bytes 5898240 | tf_op jit(solution)/shard_map/all_gather | solution.py:902
  266.9 30.1 %collective-permute-start.4 = (bf16[256,256]{1,0:T(8,128)(2,1)S(1)}, bf16[256,256]{1,0:T(8,128)(2,1)S(1)}, u32[]{:S(2)}, u32[]{:S(2)}) collective-permute-start(bf16[256,256]{1,0:T(8,128)(2,1)S(1)} %get-tuple-element.480), channel_id=1, source_target_pairs={{0,2},{1,3},{2,0},{3,1},{4,6},{5,7},{6,4},{7,5},{8,10},{9,11},{10,... | collective-permute-start | bytes 393224 | tf_op jit(solution)/shard_map/ppermute | solution.py:96
  266.9 37.4 %collective-permute-start.3 = (bf16[256,256]{1,0:T(8,128)(2,1)S(1)}, bf16[256,256]{1,0:T(8,128)(2,1)S(1)}, u32[]{:S(2)}, u32[]{:S(2)}) collective-permute-start(bf16[256,256]{1,0:T(8,128)(2,1)S(1)} %get-tuple-element.480), channel_id=1, source_target_pairs={{0,1},{1,0},{2,3},{3,2},{4,5},{5,4},{6,7},{7,6},{8,9},{9,8},{10,11... | collective-permute-start | bytes 393224 | tf_op jit(solution)/shard_map/ppermute | solution.py:96
  270.2 24.8 %collective-permute-start.1 = (bf16[1920,256]{1,0:T(8,128)(2,1)}, bf16[1920,256]{1,0:T(8,128)(2,1)}, u32[]{:S(2)}, u32[]{:S(2)}) collective-permute-start(bf16[1920,256]{1,0:T(8,128)(2,1)} %pad_maximum_fusion.10), channel_id=1, source_target_pairs={{0,2},{1,3},{2,0},{3,1},{4,6},{5,7},{6,4},{7,5},{8,10},{9,11},{10,... | collective-permute-start | bytes 2949128 | tf_op jit(solution)/shard_map/ppermute | solution.py:96
  272.2 33.5 %collective-permute-start = (bf16[1920,256]{1,0:T(8,128)(2,1)}, bf16[1920,256]{1,0:T(8,128)(2,1)}, u32[]{:S(2)}, u32[]{:S(2)}) collective-permute-start(bf16[1920,256]{1,0:T(8,128)(2,1)} %pad_maximum_fusion.10), channel_id=1, source_target_pairs={{0,1},{1,0},{2,3},{3,2},{4,5},{5,4},{6,7},{7,6},{8,9},{9,8},{10,11... | collective-permute-start | bytes 2949128 | tf_op jit(solution)/shard_map/ppermute | solution.py:96
  494.8 32.7 %collective-permute-start.15 = (f16[656,1024]{1,0:T(8,128)(2,1)}, f16[656,1024]{1,0:T(8,128)(2,1)}, u32[]{:S(2)}, u32[]{:S(2)}) collective-permute-start(f16[656,1024]{1,0:T(8,128)(2,1)} %select_convert_fusion.3), channel_id=1, source_target_pairs={{0,4},{4,0},{8,12},{12,8},{16,20},{20,16},{24,28},{28,24},{1,5},{5... | collective-permute-start | bytes 4030472 | tf_op jit(solution)/shard_map/ppermute | solution.py:96
  517.7 38.1 %collective-permute-start.16 = (f16[656,1024]{1,0:T(8,128)(2,1)}, f16[656,1024]{1,0:T(8,128)(2,1)}, u32[]{:S(2)}, u32[]{:S(2)}) collective-permute-start(f16[656,1024]{1,0:T(8,128)(2,1)} %select_convert_fusion.2), channel_id=1, source_target_pairs={{0,4},{4,0},{8,12},{12,8},{16,20},{20,16},{24,28},{28,24},{1,5},{5... | collective-permute-start | bytes 4030472 | tf_op jit(solution)/shard_map/ppermute | solution.py:96
  581.5 36.9 %collective-permute-start.17 = (f16[176,1024]{1,0:T(8,128)(2,1)}, f16[176,1024]{1,0:T(8,128)(2,1)}, u32[]{:S(2)}, u32[]{:S(2)}) collective-permute-start(f16[176,1024]{1,0:T(8,128)(2,1)} %get-tuple-element.106), channel_id=1, source_target_pairs={{0,8},{4,12},{8,0},{12,4},{16,24},{20,28},{24,16},{28,20},{1,9},{5... | collective-permute-start | bytes 1081352 | tf_op jit(solution)/shard_map/ppermute | solution.py:434
  581.8 36.6 %collective-permute-start.18 = (f16[176,1024]{1,0:T(8,128)(2,1)}, f16[176,1024]{1,0:T(8,128)(2,1)}, u32[]{:S(2)}, u32[]{:S(2)}) collective-permute-start(f16[176,1024]{1,0:T(8,128)(2,1)} %get-tuple-element.107), channel_id=1, source_target_pairs={{0,16},{4,20},{8,24},{12,28},{16,0},{20,4},{24,8},{28,12},{1,17},{... | collective-permute-start | bytes 1081352 | tf_op jit(solution)/shard_map/ppermute | solution.py:434
  584.6 33.8 %collective-permute-start.19 = (f16[176,1024]{1,0:T(8,128)(2,1)}, f16[176,1024]{1,0:T(8,128)(2,1)}, u32[]{:S(2)}, u32[]{:S(2)}) collective-permute-start(f16[176,1024]{1,0:T(8,128)(2,1)} %get-tuple-element.108), channel_id=1, source_target_pairs={{0,24},{4,28},{8,16},{12,20},{16,8},{20,12},{24,0},{28,4},{1,25},{... | collective-permute-start | bytes 1081352 | tf_op jit(solution)/shard_map/ppermute | solution.py:434
  615.2 40.0 %collective-permute-start.20 = (f16[2512,256]{1,0:T(8,128)(2,1)}, f16[2512,256]{1,0:T(8,128)(2,1)}, u32[]{:S(2)}, u32[]{:S(2)}) collective-permute-start(f16[2512,256]{1,0:T(8,128)(2,1)} %select_convert_fusion.4), channel_id=1, source_target_pairs={{0,4},{4,0},{8,12},{12,8},{16,20},{20,16},{24,28},{28,24},{1,5},{5... | collective-permute-start | bytes 3858440 | tf_op jit(solution)/shard_map/ppermute | solution.py:96
  625.7 34.7 %collective-permute-start.21 = (f16[176,1024]{1,0:T(8,128)(2,1)}, f16[176,1024]{1,0:T(8,128)(2,1)}, u32[]{:S(2)}, u32[]{:S(2)}) collective-permute-start(f16[176,1024]{1,0:T(8,128)(2,1)} %get-tuple-element.112), channel_id=1, source_target_pairs={{0,8},{4,12},{8,0},{12,4},{16,24},{20,28},{24,16},{28,20},{1,9},{5... | collective-permute-start | bytes 1081352 | tf_op jit(solution)/shard_map/ppermute | solution.py:434
  625.8 34.6 %collective-permute-start.22 = (f16[176,1024]{1,0:T(8,128)(2,1)}, f16[176,1024]{1,0:T(8,128)(2,1)}, u32[]{:S(2)}, u32[]{:S(2)}) collective-permute-start(f16[176,1024]{1,0:T(8,128)(2,1)} %get-tuple-element.113), channel_id=1, source_target_pairs={{0,16},{4,20},{8,24},{12,28},{16,0},{20,4},{24,8},{28,12},{1,17},{... | collective-permute-start | bytes 1081352 | tf_op jit(solution)/shard_map/ppermute | solution.py:434
  628.8 31.6 %collective-permute-start.23 = (f16[176,1024]{1,0:T(8,128)(2,1)S(1)}, f16[176,1024]{1,0:T(8,128)(2,1)}, u32[]{:S(2)}, u32[]{:S(2)}) collective-permute-start(f16[176,1024]{1,0:T(8,128)(2,1)S(1)} %copy-done.173), channel_id=1, source_target_pairs={{0,24},{4,28},{8,16},{12,20},{16,8},{20,12},{24,0},{28,4},{1,25},{... | collective-permute-start | bytes 1081352 | tf_op jit(solution)/shard_map/ppermute | solution.py:434
  653.6 41.8 %collective-permute-start.24 = (f16[1168,768]{1,0:T(8,128)(2,1)}, f16[1168,768]{1,0:T(8,128)(2,1)}, u32[]{:S(2)}, u32[]{:S(2)}) collective-permute-start(f16[1168,768]{1,0:T(8,128)(2,1)} %select_convert_fusion), channel_id=1, source_target_pairs={{0,4},{4,0},{8,12},{12,8},{16,20},{20,16},{24,28},{28,24},{1,5},{5... | collective-permute-start | bytes 5382152 | tf_op jit(solution)/shard_map/ppermute | solution.py:96
  665.4 35.9 %collective-permute-start.25 = (f16[640,256]{1,0:T(8,128)(2,1)}, f16[640,256]{1,0:T(8,128)(2,1)}, u32[]{:S(2)}, u32[]{:S(2)}) collective-permute-start(f16[640,256]{1,0:T(8,128)(2,1)} %get-tuple-element.117), channel_id=1, source_target_pairs={{0,8},{4,12},{8,0},{12,4},{16,24},{20,28},{24,16},{28,20},{1,9},{5... | collective-permute-start | bytes 983048 | tf_op jit(solution)/shard_map/ppermute | solution.py:434
  666.2 35.0 %collective-permute-start.26 = (f16[640,256]{1,0:T(8,128)(2,1)}, f16[640,256]{1,0:T(8,128)(2,1)}, u32[]{:S(2)}, u32[]{:S(2)}) collective-permute-start(f16[640,256]{1,0:T(8,128)(2,1)} %get-tuple-element.118), channel_id=1, source_target_pairs={{0,16},{4,20},{8,24},{12,28},{16,0},{20,4},{24,8},{28,12},{1,17},{... | collective-permute-start | bytes 983048 | tf_op jit(solution)/shard_map/ppermute | solution.py:434
  668.4 32.8 %collective-permute-start.27 = (f16[640,256]{1,0:T(8,128)(2,1)}, f16[640,256]{1,0:T(8,128)(2,1)}, u32[]{:S(2)}, u32[]{:S(2)}) collective-permute-start(f16[640,256]{1,0:T(8,128)(2,1)} %get-tuple-element.119), channel_id=1, source_target_pairs={{0,24},{4,28},{8,16},{12,20},{16,8},{20,12},{24,0},{28,4},{1,25},{... | collective-permute-start | bytes 983048 | tf_op jit(solution)/shard_map/ppermute | solution.py:434
  719.9 45.8 %collective-permute-start.29 = (f16[880,768]{1,0:T(8,128)(2,1)}, f16[880,768]{1,0:T(8,128)(2,1)}, u32[]{:S(2)}, u32[]{:S(2)}) collective-permute-start(f16[880,768]{1,0:T(8,128)(2,1)} %select_convert_fusion.1), channel_id=1, source_target_pairs={{0,4},{4,0},{8,12},{12,8},{16,20},{20,16},{24,28},{28,24},{1,5},{5... | collective-permute-start | bytes 4055048 | tf_op jit(solution)/shard_map/ppermute | solution.py:96
  730.8 41.4 %collective-permute-start.30 = (f16[304,768]{1,0:T(8,128)(2,1)}, f16[304,768]{1,0:T(8,128)(2,1)}, u32[]{:S(2)}, u32[]{:S(2)}) collective-permute-start(f16[304,768]{1,0:T(8,128)(2,1)} %get-tuple-element.124), channel_id=1, source_target_pairs={{0,8},{4,12},{8,0},{12,4},{16,24},{20,28},{24,16},{28,20},{1,9},{5... | collective-permute-start | bytes 1400840 | tf_op jit(solution)/shard_map/ppermute | solution.py:434
  730.8 41.4 %collective-permute-start.31 = (f16[304,768]{1,0:T(8,128)(2,1)}, f16[304,768]{1,0:T(8,128)(2,1)}, u32[]{:S(2)}, u32[]{:S(2)}) collective-permute-start(f16[304,768]{1,0:T(8,128)(2,1)} %get-tuple-element.125), channel_id=1, source_target_pairs={{0,16},{4,20},{8,24},{12,28},{16,0},{20,4},{24,8},{28,12},{1,17},{... | collective-permute-start | bytes 1400840 | tf_op jit(solution)/shard_map/ppermute | solution.py:434
  733.8 38.4 %collective-permute-start.32 = (f16[304,768]{1,0:T(8,128)(2,1)}, f16[304,768]{1,0:T(8,128)(2,1)}, u32[]{:S(2)}, u32[]{:S(2)}) collective-permute-start(f16[304,768]{1,0:T(8,128)(2,1)} %get-tuple-element.126), channel_id=1, source_target_pairs={{0,24},{4,28},{8,16},{12,20},{16,8},{20,12},{24,0},{28,4},{1,25},{... | collective-permute-start | bytes 1400840 | tf_op jit(solution)/shard_map/ppermute | solution.py:434
  735.2 26.1 %collective-permute-start.28 = (f16[304,768]{1,0:T(8,128)(2,1)S(1)}, f16[304,768]{1,0:T(8,128)(2,1)S(1)}, u32[]{:S(2)}, u32[]{:S(2)}) collective-permute-start(f16[304,768]{1,0:T(8,128)(2,1)S(1)} %copy-done.169), channel_id=1, source_target_pairs={{0,4},{4,0},{8,12},{12,8},{16,20},{20,16},{24,28},{28,24},{1,5},{5... | collective-permute-start | bytes 1400840 | tf_op jit(solution)/shard_map/ppermute | solution.py:96
  788.3 46.3 %collective-permute-start.33 = (f16[304,768]{1,0:T(8,128)(2,1)}, f16[304,768]{1,0:T(8,128)(2,1)}, u32[]{:S(2)}, u32[]{:S(2)}) collective-permute-start(f16[304,768]{1,0:T(8,128)(2,1)} %get-tuple-element.128), channel_id=1, source_target_pairs={{8,0},{12,4},{9,1},{13,5},{10,2},{14,6},{11,3},{15,7}} | collective-permute-start | bytes 1400840 | tf_op jit(solution)/shard_map/ppermute | solution.py:434
  803.4 33.7 %collective-permute-start.34 = (f16[304,768]{1,0:T(8,128)(2,1)S(1)}, f16[304,768]{1,0:T(8,128)(2,1)}, u32[]{:S(2)}, u32[]{:S(2)}) collective-permute-start(f16[304,768]{1,0:T(8,128)(2,1)S(1)} %copy-done.172), channel_id=1, source_target_pairs={{16,0},{20,4},{17,1},{21,5},{18,2},{22,6},{19,3},{23,7}} | collective-permute-start | bytes 1400840 | tf_op jit(solution)/shard_map/ppermute | solution.py:434
  824.4 20.5 %collective-permute-start.35 = (f16[304,768]{1,0:T(8,128)(2,1)}, f16[304,768]{1,0:T(8,128)(2,1)S(1)}, u32[]{:S(2)}, u32[]{:S(2)}) collective-permute-start(f16[304,768]{1,0:T(8,128)(2,1)} %get-tuple-element.130), channel_id=1, source_target_pairs={{24,0},{28,4},{25,1},{29,5},{26,2},{30,6},{27,3},{31,7}} | collective-permute-start | bytes 1400840 | tf_op jit(solution)/shard_map/ppermute | solution.py:434
  825.7 20.9 %collective-permute-start.36 = (f16[304,768]{1,0:T(8,128)(2,1)}, f16[304,768]{1,0:T(8,128)(2,1)S(1)}, u32[]{:S(2)}, u32[]{:S(2)}) collective-permute-start(f16[304,768]{1,0:T(8,128)(2,1)} %get-tuple-element.131), channel_id=1, source_target_pairs={{0,8},{4,12},{16,24},{20,28},{24,16},{28,20},{1,9},{5,13},{17,25},... | collective-permute-start | bytes 1400840 | tf_op jit(solution)/shard_map/ppermute | solution.py:434
  828.8 24.9 %collective-permute-start.37 = (f16[304,768]{1,0:T(8,128)(2,1)S(1)}, f16[304,768]{1,0:T(8,128)(2,1)S(1)}, u32[]{:S(2)}, u32[]{:S(2)}) collective-permute-start(f16[304,768]{1,0:T(8,128)(2,1)S(1)} %copy-done.171), channel_id=1, source_target_pairs={{0,16},{4,20},{8,24},{12,28},{24,8},{28,12},{1,17},{5,21},{9,25},{... | collective-permute-start | bytes 1400840 | tf_op jit(solution)/shard_map/ppermute | solution.py:434
  834.6 25.5 %collective-permute-start.38 = (f16[304,768]{1,0:T(8,128)(2,1)S(1)}, f16[304,768]{1,0:T(8,128)(2,1)S(1)}, u32[]{:S(2)}, u32[]{:S(2)}) collective-permute-start(f16[304,768]{1,0:T(8,128)(2,1)S(1)} %copy-done.170), channel_id=1, source_target_pairs={{0,24},{4,28},{8,16},{12,20},{16,8},{20,12},{1,25},{5,29},{9,17},{... | collective-permute-start | bytes 1400840 | tf_op jit(solution)/shard_map/ppermute | solution.py:434
  844.8 21.9 %collective-permute-start.43 = (f32[96,184]{1,0:T(8,128)S(1)}, f32[96,184]{1,0:T(8,128)S(1)}, u32[]{:S(2)}, u32[]{:S(2)}) collective-permute-start(f32[96,184]{1,0:T(8,128)S(1)} %fusion.171), channel_id=1, source_target_pairs={{0,1},{1,0},{2,3},{3,2},{4,5},{5,4},{6,7},{7,6},{8,9},{9,8},{10,11... | collective-permute-start | bytes 211976 | tf_op jit(solution)/shard_map/ppermute | solution.py:96
  844.9 21.8 %collective-permute-start.45 = (f32[96,184]{1,0:T(8,128)S(1)}, f32[96,184]{1,0:T(8,128)S(1)}, u32[]{:S(2)}, u32[]{:S(2)}) collective-permute-start(f32[96,184]{1,0:T(8,128)S(1)} %collective-permute-done.44), channel_id=1, source_target_pairs={{0,1},{1,0},{2,3},{3,2},{4,5},{5,4},{6,7},{7,6},{8,9},{9,8},{10,11... | collective-permute-start | bytes 211976 | tf_op jit(solution)/shard_map/ppermute | solution.py:96
  846.6 24.9 %collective-permute-start.50 = (f32[212,128]{1,0:T(8,128)}, f32[212,128]{1,0:T(8,128)}, u32[]{:S(2)}, u32[]{:S(2)}) collective-permute-start(f32[212,128]{1,0:T(8,128)} %add.1491), channel_id=1, source_target_pairs={{0,16},{4,20},{8,24},{12,28},{16,0},{20,4},{24,8},{28,12},{1,17},{... | collective-permute-start | bytes 325640 | tf_op jit(solution)/shard_map/ppermute | solution.py:96
  (371 other events, 2916.9 us)
Sparse Core Ops, SparseCore 0:
  267.0 85.5 all-gather.1

commit v3 on v2

--- a/solution.py
+++ b/solution.py
@@ -107,7 +107,8 @@
     back_cond,
     back_decoder,
     back_encoder,
-) = (0, 1, 2, 4, 6, 8, 10, 11, 13)
+    last_exchange,
+) = (0, 1, 2, 4, 6, 8, 10, 11, 13, 15)
 rest_group, mix_group = 100, 101
 
 
@@ -281,8 +282,10 @@
     return copies
 
 
-def greet(barrier, axes):
-    count = 0
+def greet(barrier, axes, others=()):
+    count = len(others)
+    for peer in others:
+        pl.semaphore_signal(barrier, inc=1, device_id=peer, device_id_type=MESH)
     for axis in axes:
         rank, size = lax.axis_index(axis), lax.axis_size(axis)
         for step in range(1, size):
@@ -378,11 +381,16 @@
     return jnp.where(is_value, padded, level).astype(jnp.float16)
 
 
+def decoded(message, rows):
+    level = message[rows : rows + 1].astype(jnp.float32)
+    return message[:rows].astype(jnp.float32) * jnp.exp2(level - 13.0)
+
+
 class Scattered:
     def __init__(self, pairs, first=0):
         self.pairs, self.first = pairs, max(first, 0)
         self.count = 4 - first if first >= 0 else -first
-        self.got, self.parts = None, None
+        self.got, self.parts, self.owned, self.owned_square = None, None, None, None
         self.level = bound_level(pairs)
         self.product = None
 
@@ -407,7 +415,8 @@
         self.got = swap(message, dp_axis, 1)
 
     def got_level(self):
-        return self.got[self.count * self.slab(), 0].astype(jnp.float32)
+        at = self.count * self.slab()
+        return self.got[at : at + 1].astype(jnp.float32)
 
     def share(self, place):
         grad, slab = self.grad(), self.slab()
@@ -433,15 +442,115 @@
             ]
             self.parts.append(lax.ppermute(message, dp_axis, pairs))
 
+    def square(self):
+        if self.owned_square is None:
+            self.owned_square = jnp.sum(self.total() ** 2)
+        return self.owned_square
+
     def total(self):
+        if self.owned is None:
+            self.owned = self.summed()
+        return self.owned
+
+    def summed(self):
         if lax.axis_size(dp_axis) != 8:
             return lax.psum_scatter(self.grad(), dp_axis, scatter_dimension=0, tiled=True)
         slab = self.slab()
         total = self.share(lax.axis_index(dp_axis) // 2)
         for part in self.parts:
-            level = part[slab, 0].astype(jnp.float32)
-            total = total + part[:slab].astype(jnp.float32) * jnp.exp2(level - 13.0)
+            total = total + decoded(part, slab)
         return total
+
+
+def tail_kernel(*refs):
+    give, keep, bias, tables, bias_total = refs[:5]
+    got, pairs, far, own, near, middle, beside_sum, pair_sum, far_sum, send_sem, recv_sem = refs[5:]
+    rank, across = lax.axis_index(dp_axis), lax.axis_index(tensor_axis)
+    low, high = lax.rem(rank, 2), lax.div(rank, 2)
+    beside = {dp_axis: rank + 1 - 2 * low}
+    pair_peers = [{dp_axis: 2 * lax.rem(high + step, 4) + low} for step in (1, 2, 3)]
+    tensor_peers = [{tensor_axis: lax.rem(across + step, 4)} for step in (1, 2, 3)]
+    barrier = pltpu.get_barrier_semaphore()
+    peers = [beside] + pair_peers + tensor_peers
+    for peer in peers:
+        pl.semaphore_signal(barrier, inc=1, device_id=peer, device_id_type=MESH)
+    pl.semaphore_wait(barrier, len(peers))
+    slots = iter(range(14))
+
+    def send(source, target, peer):
+        slot = next(slots)
+        copy = pltpu.make_async_remote_copy(
+            src_ref=source,
+            dst_ref=target,
+            send_sem=send_sem.at[slot],
+            recv_sem=recv_sem.at[slot],
+            device_id=peer,
+            device_id_type=MESH,
+        )
+        copy.start()
+        return copy
+
+    tables_near = send(give, got, beside)
+    bias_near = [send(bias, near.at[across], peer) for peer in tensor_peers]
+    near[across] = bias[...]
+    tables_near.wait()
+    pairs[...] = keep[...] + got[...]
+    tables_far = [
+        send(pairs.at[lax.rem(high + step, 4)], far.at[step - 1], pair_peers[step - 1])
+        for step in (1, 2, 3)
+    ]
+    for copy in bias_near:
+        copy.wait()
+    middle[...] = near[0] + near[1] + near[2] + near[3]
+    send(middle, beside_sum, beside).wait()
+    pair_sum[...] = middle[...] + beside_sum[...]
+    far_sum[high] = pair_sum[...]
+    bias_far = [send(pair_sum, far_sum.at[high], peer) for peer in pair_peers]
+    for copy in tables_far:
+        copy.wait()
+    own[...] = pairs[high] + far[0] + far[1] + far[2]
+    tables[across] = own[...]
+    tables_all = [send(own, tables.at[across], peer) for peer in tensor_peers]
+    for copy in bias_far:
+        copy.wait()
+    bias_total[...] = far_sum[0] + far_sum[1] + far_sum[2] + far_sum[3]
+    for copy in tables_all:
+        copy.wait()
+
+
+def tail_exchange(tables, bias):
+    low = lax.axis_index(dp_axis) % 2
+    slab, columns = tables.shape[0] // 8, tables.shape[1]
+    blocks = tables.reshape(4, 2 * slab, columns)
+    keep = lax.dynamic_slice_in_dim(blocks, low * slab, slab, 1)
+    give = lax.dynamic_slice_in_dim(blocks, (1 - low) * slab, slab, 1)
+    four, one = keep.shape, (slab, columns)
+    vmem = pl.BlockSpec(memory_space=pltpu.VMEM)
+    return pl.pallas_call(
+        tail_kernel,
+        out_shape=[
+            jax.ShapeDtypeStruct(four, jnp.float32),
+            jax.ShapeDtypeStruct(bias.shape, jnp.float32),
+        ],
+        in_specs=[vmem] * 3,
+        out_specs=[vmem] * 2,
+        scratch_shapes=[
+            pltpu.VMEM(four, jnp.float32),
+            pltpu.VMEM(four, jnp.float32),
+            pltpu.VMEM((3,) + one, jnp.float32),
+            pltpu.VMEM(one, jnp.float32),
+            pltpu.VMEM((4,) + bias.shape, jnp.float32),
+            pltpu.VMEM(bias.shape, jnp.float32),
+            pltpu.VMEM(bias.shape, jnp.float32),
+            pltpu.VMEM(bias.shape, jnp.float32),
+            pltpu.VMEM((4,) + bias.shape, jnp.float32),
+            pltpu.SemaphoreType.DMA((14,)),
+            pltpu.SemaphoreType.DMA((14,)),
+        ],
+        compiler_params=pltpu.CompilerParams(
+            collective_id=last_exchange, has_side_effects=True, vmem_limit_bytes=24 << 20
+        ),
+    )(give, keep, bias)
 
 
 class Traffic:
@@ -454,8 +563,12 @@
 
     def tie(self, value, near, far, arrived):
         near_messages = [group.near_message() for group in near]
+        parts = [group.parts for group in arrived]
+        if far:
+            value, gots = lax.optimization_barrier((value, [group.got for group in far]))
+            for group, got in zip(far, gots):
+                group.got = got
         far_messages = [group.far_messages() for group in far]
-        parts = [group.parts for group in arrived]
         value, near_messages, far_messages, parts = lax.optimization_barrier(
             (value, near_messages, far_messages, parts)
         )
@@ -472,29 +585,109 @@
             return tensor_sum(partial_term, jnp.bfloat16, kernel)[0]
         near, far, arrived = [[self.groups[group] for group in part] for part in self.plan[kernel]]
         partial_term = self.tie(partial_term, near, [], [])
+        if kernel == back_encoder + 1:
+            group = self.groups[back_encoder]
+            done = [self.groups[key] for key in (back_head, back_head + 1, rest_group)]
+            totals = [(item.total(), item.square()) for item in done]
+            partial_term, group.got, totals = lax.optimization_barrier(
+                (partial_term, group.got, totals)
+            )
+            for item, (total, square) in zip(done, totals):
+                item.owned, item.owned_square = total, square
         total = tensor_sum(partial_term, jnp.bfloat16, kernel)[0]
-        return self.tie(total, [], far, arrived)
-
-    def finish(self, value, names):
+        total = self.tie(total, [], far, arrived)
+        if kernel == back_encoder + 1:
+            mix = self.groups[mix_group]
+            total, mix.got = lax.optimization_barrier((total, mix.got))
+            total, messages = lax.optimization_barrier((total, self.encoder_messages()))
+            self.encoder_parts = [
+                swap(message, dp_axis, 2 * step) for step, message in zip((1, 2, 3), messages)
+            ]
+        return total
+
+    def arrive(self, value, index):
         if lax.axis_size(dp_axis) != 8:
             return value
-        return self.tie(value, [], [self.groups[name] for name in names], [])
-
-
-def first_kernel(count, images, *refs):
-    notes, class_table, shares = refs[0], refs[1], refs[2 : 2 + count]
-    all_notes, classes, wholes = refs[2 + count], refs[3 + count], refs[4 + count : 4 + 2 * count]
-    found, note_send, note_recv, class_send, class_recv, own_sem = refs[
-        4 + 2 * count : 10 + 2 * count
-    ]
-    greet(pltpu.get_barrier_semaphore(), (dp_axis,))
-    rank = lax.axis_index(dp_axis)
-    ring = RingGather(shares, wholes, *refs[10 + 2 * count :])
+        value, self.encoder_parts[index] = lax.optimization_barrier(
+            (value, self.encoder_parts[index])
+        )
+        return value
+
+    def encoder_share(self, place):
+        mix, rest = self.groups[mix_group], self.groups[back_encoder]
+        return jnp.where(place == 0, mix.share(place), rest.share(place))
+
+    def encoder_messages(self):
+        mix, rest = self.groups[mix_group], self.groups[back_encoder]
+        high = lax.axis_index(dp_axis) // 2
+        level = jnp.maximum(
+            jnp.maximum(mix.level, mix.got_level()), jnp.maximum(rest.level, rest.got_level())
+        )
+        return [
+            coded(self.encoder_share(high ^ step), level + 1.0) for step in (1, 2, 3)
+        ]
+
+    def encoder_total(self, ahead):
+        parts, ahead = lax.optimization_barrier((self.encoder_parts, ahead))
+        slab = self.groups[mix_group].slab()
+        total = self.encoder_share(lax.axis_index(dp_axis) // 2)
+        for part in parts:
+            total = total + decoded(part, slab)
+        return total, ahead
+
+
+def first_kernel(
+    images,
+    notes,
+    class_table,
+    table_share,
+    block_share,
+    all_notes,
+    classes,
+    tables,
+    blocks,
+    found,
+    note_send,
+    note_recv,
+    class_send,
+    class_recv,
+    own_sem,
+    across_send,
+    across_recv,
+    *ring_sems,
+):
+    rank, place_across = lax.axis_index(dp_axis), lax.axis_index(tensor_axis)
+    low = lax.rem(place_across, 2)
+    partner, across = place_across + 1 - 2 * low, lax.rem(place_across + 2, 4)
+    others = [{tensor_axis: partner}, {tensor_axis: across}]
+    greet(pltpu.get_barrier_semaphore(), (dp_axis,), others)
+    table_ring = RingGather([table_share], [tables.at[place_across]], *ring_sems[:3])
+    block_ring = RingGather([block_share], [blocks], *ring_sems[3:])
     note_copies = spread(notes, all_notes, dp_axis, note_send, note_recv)
     all_notes[rank] = notes[...]
-    ring.begin()
+    table_ring.begin()
+    block_ring.begin()
     for copy in note_copies:
         copy.wait()
+    for step in (1, 2, 3):
+        table_ring.advance(step)
+    block_ring.advance(1)
+    table_ring.finish()
+
+    def cross(owner, peer, slot):
+        return pltpu.make_async_remote_copy(
+            src_ref=tables.at[owner],
+            dst_ref=tables.at[owner],
+            send_sem=across_send.at[slot],
+            recv_sem=across_recv.at[slot],
+            device_id={tensor_axis: peer},
+            device_id_type=MESH,
+        )
+
+    near = cross(place_across, partner, 0)
+    far = cross(place_across, across, 1)
+    near.start()
+    far.start()
     place = lax.broadcasted_iota(jnp.int32, class_table.shape, 1).astype(jnp.float32)
     lane = lax.broadcasted_iota(jnp.int32, found.shape, 1)
     columns = jnp.zeros(found.shape, jnp.float32)
@@ -505,55 +698,45 @@
         )
         columns = jnp.where(lane == image, value, columns)
     found[...] = columns
+    block_ring.advance(2)
     own = pltpu.make_async_copy(found, classes.at[rank], own_sem.at[0])
     own.start()
     class_copies = spread(found, classes, dp_axis, class_send, class_recv)
-    for step in (1, 2, 3):
-        ring.advance(step)
-    ring.finish()
+    near.wait()
+    far.wait()
+    forward = cross(across, partner, 2)
+    forward.start()
+    block_ring.advance(3)
+    block_ring.finish()
+    forward.wait()
     for copy in class_copies:
         copy.wait()
     own.wait()
 
 
-def gather_first(notes, class_table, images, shares):
-    count = len(shares)
+def gather_first(notes, class_table, images, table_share, block_share):
     rows = class_table.shape[0]
     vmem, anywhere = pl.BlockSpec(memory_space=pltpu.VMEM), pl.BlockSpec(memory_space=pl.ANY)
-    outs = pl.pallas_call(
-        functools.partial(first_kernel, count, images),
+    return pl.pallas_call(
+        functools.partial(first_kernel, images),
         out_shape=[
             jax.ShapeDtypeStruct((8, 8, 128), jnp.float32),
             jax.ShapeDtypeStruct((8, rows, 128), jnp.float32),
-        ]
-        + [jax.ShapeDtypeStruct((8,) + share.shape, share.dtype) for share in shares],
-        in_specs=[vmem, vmem] + [anywhere] * count,
-        out_specs=[vmem, vmem] + [anywhere] * count,
+            jax.ShapeDtypeStruct((4, 8) + table_share.shape, table_share.dtype),
+            jax.ShapeDtypeStruct((8,) + block_share.shape, block_share.dtype),
+        ],
+        in_specs=[vmem, vmem, anywhere, anywhere],
+        out_specs=[vmem, vmem, anywhere, anywhere],
         scratch_shapes=[pltpu.VMEM((rows, 128), jnp.float32)]
         + [pltpu.SemaphoreType.DMA((7,))] * 4
         + [pltpu.SemaphoreType.DMA((1,))]
-        + ring_scratch(count),
+        + [pltpu.SemaphoreType.DMA((3,))] * 2
+        + ring_scratch(1)
+        + ring_scratch(1),
         compiler_params=pltpu.CompilerParams(
             collective_id=first_gather, has_side_effects=True, vmem_limit_bytes=16 << 20
         ),
-    )(notes, class_table, *shares)
-    return outs[0], outs[1], outs[2:]
-
-
-def scatter_small(grad):
-    if lax.axis_size(dp_axis) != 8:
-        return lax.psum_scatter(grad, dp_axis, scatter_dimension=0, tiled=True)
-    rank = lax.axis_index(dp_axis)
-    low, high = rank % 2, rank // 2
-    slab, columns = grad.shape[0] // 8, grad.shape[1]
-    blocks = grad.reshape(4, 2 * slab, columns)
-    keep = lax.dynamic_slice_in_dim(blocks, low * slab, slab, 1)
-    give = lax.dynamic_slice_in_dim(blocks, (1 - low) * slab, slab, 1)
-    pairs = keep + swap(give, dp_axis, 1)
-    total = pick(pairs, high)
-    for step in (1, 2, 3):
-        total = total + swap(pick(pairs, high ^ step), dp_axis, 2 * step)
-    return total
+    )(notes, class_table, table_share, block_share)
 
 
 def take_pieces(vector, starts, counts):
@@ -832,13 +1015,18 @@
     )
     class_share = embed_tables[:, class_at:class_end]
     block_share = narrow(block_weights)
-    if dp_size == 8:
+    whole_here = dp_size == 8 and tensor_size == 4
+    if whole_here:
+        part = -(-table_share.shape[1] // 32) * 8
+        table_share = jnp.pad(table_share, ((0, 0), (0, 4 * part - table_share.shape[1])))
+        table_share = lax.dynamic_slice_in_dim(table_share, tensor_index * part, part, 1)
         notes = jnp.zeros((8, 128), jnp.float32)
         notes = lax.dynamic_update_slice(notes, chosen.astype(jnp.float32)[None], (0, 0))
         notes = lax.dynamic_update_slice(notes, weight_here[None, None], (1, 0))
-        all_notes, classes, (table_cols, first_block) = gather_first(
-            notes, class_share, images, [table_share, block_share[0]]
-        )
+        all_notes, classes, table_parts, first_block = gather_first(
+            notes, class_share, images, table_share.T, block_share[0]
+        )
+        table_rows = table_parts.transpose(0, 2, 1, 3).reshape(4 * part, -1)
         all_chosen = all_notes[:, 0, :images].reshape(-1)
         weight_total = jnp.sum(all_notes[:, 1, 0])
         class_rows = lax.dynamic_slice_in_dim(
@@ -847,26 +1035,24 @@
     else:
         all_chosen = lax.all_gather(chosen, dp_axis, axis=0, tiled=True).astype(jnp.float32)
         weight_total = lax.psum(weight_here, dp_axis)
-        table_cols = lax.all_gather(table_share, dp_axis)
+        table_rows = lax.all_gather(table_share, dp_axis, axis=0, tiled=True).T
         first_block = lax.all_gather(block_share[0], dp_axis)
     picker = (all_chosen[:, None] == jnp.arange(CLASSES + 1)[None, :]).astype(jnp.float32)
-    if dp_size != 8:
+    if not whole_here:
         found = lax.dot_general(
             class_share, picker, (((1,), (1,)), ((), ())), precision=highest
         )
         class_rows = lax.dynamic_slice_in_dim(
             lax.all_gather(found, dp_axis, axis=0, tiled=True), dp_index * images, images, 1
         ).T
-    table_cols = table_cols.reshape(-1, table_cols.shape[-1])
     first_block = first_block.reshape(-1, D)
     share_rows = block_share[1].shape[0] // 2
     rest_share = narrow(head_rest)
-    rest_rows_here = rest_share.shape[0] // 2
     flat_bias = bias_rows.reshape(-1)
     rest_bias = flat_bias[: 6 * HW].reshape(6, HW)
     head_bias = flat_bias[6 * HW : 6 * HW + 5 * HB * HW].reshape(HB, 5 * HW)
     column_bias = flat_bias[6 * HW + 5 * HB * HW :].reshape(LAYERS, 3 * D + FF)
-    table_parts = cut_rows(table_cols.T, (TOKD, 1, TOK + BUF, TOK + BUF, 1, 6 * LAYERS, 4))
+    table_parts = cut_rows(table_rows, (TOKD, 1, TOK + BUF, TOK + BUF, 1, 6 * LAYERS, 4))
     layer_vectors = table_parts[5].reshape(LAYERS, 6, D)
     final_norms = table_parts[6]
     patch_flat = patches.reshape(-1, TOKD)
@@ -911,11 +1097,10 @@
         layer_bias[1],
         layer_vectors[1],
         decoder_forward,
-        [rest_share[:rest_rows_here]],
-        [rest_share[rest_rows_here:]],
-    )
-    rest_rows = jnp.concatenate([first_half[0], last_half[0]], axis=1)
-    rest_rows = rest_rows.reshape(-1, rest_rows.shape[-1])
+        [rest_share],
+        [],
+    )
+    rest_rows = first_half[0].reshape(-1, rest_share.shape[-1])
     cond_mine, input_mine, output_mine, time_first, second_mine, final_shift, final_scale = cut_rows(
         rest_rows, (D, TOKD, TOKD, HW, HW, HW, HW)
     )
@@ -933,6 +1118,7 @@
     time_act = tensor_columns(narrow(jax.nn.silu(time_pre)))
     time_embed = product(time_act, time_second) + rest_bias[3]
     cond_vec = (condition[None] + time_embed.reshape(COPIES, -1, HW)).reshape(-1, HW)
+    cond_vec, head_all = lax.optimization_barrier((cond_vec, head_all))
     cond_act = narrow(jax.nn.silu(cond_vec))
     phase = step_rows.astype(jnp.float32)[..., None] * (math.pi / (2 * T_STEPS))
     signal_coef = jnp.cos(phase)
@@ -987,7 +1173,7 @@
             back_decoder: ([rest_group], [back_head], [back_head + 1]),
             back_decoder + 1: ([back_decoder], [rest_group], [back_head]),
             back_encoder: ([], [back_decoder], [rest_group]),
-            back_encoder + 1: ([back_encoder, mix_group], [back_encoder], [back_decoder]),
+            back_encoder + 1: ([back_encoder, mix_group], [], [back_decoder]),
         }
     )
     cond_split = product_right(grad_shift_last, final_shift) + product_right(
@@ -1020,7 +1206,7 @@
     grad_time_pre = narrow(local_back(jax.nn.silu, time_pre, grad_time_act))
     grad_latent = jnp.sum(product(grad_cond_vec, cond_weight.T).reshape(COPIES, -1, D), axis=0)
     grad_cond_mine = own_columns(grad_cond_vec)
-    owned_rest = Scattered(
+    rest_scattered = Scattered(
         [
             (jnp.tile(latent, (COPIES, 1)), grad_cond_mine),
             (noisy_rows, own_columns(grad_input)),
@@ -1031,7 +1217,7 @@
             (cond_act, grad_scale_last),
         ]
     )
-    traffic.add(rest_group, owned_rest)
+    traffic.add(rest_group, rest_scattered)
     rest_bias_grad = place_pieces(
         6 * HW,
         [
@@ -1059,10 +1245,8 @@
     grad_stream, grad_rows_enc, grad_bias_enc, grad_vec_enc = block_back(
         grad_encoded, visible_enc, block_all[0], layer_vectors[0], stored_enc, back_encoder, traffic
     )
-    grad_stream, bias_parts = traffic.finish(
-        (grad_stream, [rest_bias_grad] + head_bias_grads),
-        [mix_group],
-    )
+    grad_stream = traffic.arrive(grad_stream, 0)
+    bias_parts = [rest_bias_grad] + head_bias_grads
     grad_tokens = narrow(grad_stream[:, BUF:].reshape(-1, D))
     grad_class = lax.dynamic_update_slice_in_dim(
         jnp.zeros((all_images, D), jnp.float32),
@@ -1096,7 +1280,28 @@
         axis=0,
     )
     grad_tables = lax.dynamic_slice_in_dim(grad_tables, tensor_index * quarter, quarter, 0)
-    owned_cols = tensor_columns(scatter_small(grad_tables.T))
+    column_grads = []
+    for grad_local in (grad_bias_enc, grad_bias_dec):
+        pieces = [
+            grad_local[slot * local_width : (slot + 1) * local_width] for slot in range(3)
+        ] + [grad_local[3 * local_width :]]
+        column_grads.append(place_pieces(3 * D + FF, pieces, column_starts))
+    lanes = bias_rows.shape[1]
+    bias_local = jnp.concatenate(bias_parts + column_grads).reshape(-1, lanes)
+    if dp_size == 8 and tensor_size == 4:
+        bias_count = bias_local.shape[0]
+        bias_local = jnp.pad(bias_local, ((0, -bias_count % 8), (0, 0)))
+        grad_tables = traffic.arrive(grad_tables, 1)
+        owned_cols, bias_grad = tail_exchange(grad_tables.T, bias_local)
+        encoder_owned, (owned_cols, bias_grad) = traffic.encoder_total((owned_cols, bias_grad))
+        owned_cols = jnp.concatenate([owned_cols[index] for index in range(4)], axis=1)
+        bias_grad = bias_grad[:bias_count]
+    else:
+        owned_cols = tensor_columns(
+            lax.psum_scatter(grad_tables.T, dp_axis, scatter_dimension=0, tiled=True)
+        )
+        bias_grad = sum_everywhere(bias_local, (tensor_axis, dp_axis))
+        encoder_owned = grad_rows_enc[0].total()
     class_cols = small_at + 6 * LAYERS + 6
     owned_tables = jnp.concatenate(
         [
@@ -1109,26 +1314,14 @@
         ],
         axis=1,
     )
-    encoder_shares = [group.total() for group in grad_rows_enc]
-    if len(encoder_shares) == 2:
-        encoder_shares = [jnp.where(dp_index < 2, encoder_shares[0], encoder_shares[1])]
-    owned_blocks = jnp.stack(encoder_shares + [grad_rows_dec[0].total()])
+    owned_blocks = jnp.stack([encoder_owned, grad_rows_dec[0].total()])
     owned_head = jnp.stack([group.total() for group in head_grads])
-    owned_rest = owned_rest.total()
-    column_grads = []
-    for grad_local in (grad_bias_enc, grad_bias_dec):
-        pieces = [
-            grad_local[slot * local_width : (slot + 1) * local_width] for slot in range(3)
-        ] + [grad_local[3 * local_width :]]
-        column_grads.append(place_pieces(3 * D + FF, pieces, column_starts))
-    lanes = bias_rows.shape[1]
-    bias_grad = sum_everywhere(
-        jnp.concatenate(bias_parts + column_grads).reshape(-1, lanes), (tensor_axis, dp_axis)
-    )
+    owned_rest = rest_scattered.total()
     split_squares = (
-        jnp.sum(owned_blocks * owned_blocks)
-        + jnp.sum(owned_head * owned_head)
-        + jnp.sum(owned_rest * owned_rest)
+        jnp.sum(encoder_owned * encoder_owned)
+        + grad_rows_dec[0].square()
+        + sum(group.square() for group in head_grads)
+        + rest_scattered.square()
     )
     shared_squares = jnp.sum(owned_tables * owned_tables) / tensor_size
     every_squares = jnp.sum(bias_grad * bias_grad) / (tensor_size * lax.axis_size(dp_axis))

time: 941 us -> 870 us (0.925)
  starting transfers between devices: 65.4 us -> 36 us
  waiting for transfers between devices: 108 us -> 86 us
  local copies, waits for them, and re-layouts: 115 us -> 93.7 us
  other arithmetic: 165 us -> 183 us
  between operations: 74.1 us -> 58.2 us
    slice x25 -> x0, local copies, waits for them, and re-layouts: 25.8 us -> none  [the longest x18 18.5 us: total(): level = part[slab, 0].astype(jnp.float32)]
    ppermute x33 -> x24, starting transfers between devices: 33.4 us -> 18.3 us  [swap(): lax.ppermute(value, axis, [(i, i ^ step) for i in range(lax.axis_size(axi...]
    ppermute x18 -> x12, starting transfers between devices: 32.1 us -> 17.6 us  [send_far(): self.parts.append(lax.ppermute(message, dp_axis, pairs))]
    pallas_call x1 -> x2, Pallas kernels: 75.3 us -> 89.5 us  [the longest x1 61.8 us: gather_first(): pl.pallas_call(functools.partial(first_kernel, images), out_shape=[jax.Sh...]
    pallas_call x1, Pallas kernels: 26.5 us -> 12.8 us  [small_sums(): pl.pallas_call(small_sum_kernel, out_shape=jax.ShapeDtypeStruct((8, 128),...]
    exp2 x0 -> x19, other arithmetic: none -> 13 us  [the longest x15 10.1 us: decoded(): return message[:rows].astype(jnp.float32) * jnp.exp2(level - 13.0)]
    reduce_sum x3 -> x5, other arithmetic: 5.18 us -> 17.2 us  [the longest x4 13.4 us: square(): self.owned_square = jnp.sum(self.total() ** 2)]
    ppermute x33 -> x24, waiting for transfers between devices: 79.6 us -> 69.2 us  [swap(): lax.ppermute(value, axis, [(i, i ^ step) for i in range(lax.axis_size(axi...]
  transfers between devices with their start and end apart: 52 -> 37, of which waited for: 11 -> 8; matrix products, arithmetic and copies ran while one was open for 17% -> 20% of each run, Pallas kernels for 6% -> 11%
where the time goes in v3:
time: 870 us; the launch traced here: 856 us
  Pallas kernels  305 us (35%)
  other arithmetic  183 us (21%)
  matrix products  94.2 us (11%)
  local copies, waits for them, and re-layouts  93.7 us (11%)
  waiting for transfers between devices  86 us (10%)
  between operations  58.2 us (7%)
  starting transfers between devices  36 us (4%)
    pallas_call x13, Pallas kernels, tensor_sum(): pl.pallas_call(functools.partial(sum_kernel, count, cross_type), out_shap...  203 us
    ppermute x24, waiting for transfers between devices, swap(): lax.ppermute(value, axis, [(i, i ^ step) for i in range(lax.axis_size(axi...  69.2 us
    pallas_call x1, Pallas kernels, gather_first(): pl.pallas_call(functools.partial(first_kernel, images), out_shape=[jax.Sh...  61.8 us
    unnamed x685, local copies, waits for them, and re-layouts  36.9 us
    dot_general x18, matrix products, product_right(): lax.dot_general(left, right, (((1,), (1,)), ((), ())), preferred_element_...  35.1 us
    dot_general x22, matrix products, product_left(): lax.dot_general(left, right, (((0,), (0,)), ((), ())), preferred_element_...  29 us
    pallas_call x1, Pallas kernels, tail_exchange(): pl.pallas_call(tail_kernel, out_shape=[jax.ShapeDtypeStruct(four, jnp.flo...  27.7 us
    dot_general x23, matrix products, product(): return jnp.dot(left, right, preferred_element_type=jnp.float32)  22.3 us
  transfers between devices with their start and end apart: 37, of which 8 were waited for; matrix products, arithmetic and copies ran while one was open for 20% of the time, Pallas kernels for 11%

profile of v3, /device:TPU:0, one launch (start us, length us, event | category | flops | bytes accessed | tf_op | source)
XLA Modules:
  0.0 856.5 jit_solution(15174283908785034045)
XLA Ops:
  27.6 61.8 %shard_map.393 = (f32[8,8,128]{2,1,0:T(8,128)S(1)}, f32[8,96,128]{2,1,0:T(8,128)S(1)}, f32[4,8,184,96]{3,2,1,0:T(8,128)S(1)}, bf16[8,288,768]{2,1,0:T(8,128)(2,1)S(1)}) custom-call(f32[8,128]{1,0:T(8,128)S(1)} %dynamic_update_slice.82.notes, f32[96,1001]{1,0:T(8,128)S(1)} %copy-done.6, f32[184,96]{1,0:T(8,128)S(1)} %fusion.211.table_share, ...), custom_call_target="tpu_custom_call" | custom-call | tf_op jit(solution)/shard_map/pallas_call | solution.py:720
  93.4 4.2 reshape.1245
  123.4 27.3 %shard_map.394 = (f32[320,768]{1,0:T(8,128)S(1)}, bf16[8,144,768]{2,1,0:T(8,128)(2,1)S(1)}) custom-call(f32[320,768]{1,0:T(8,128)S(1)} %fusion.195.refs_0_, bf16[144,768]{1,0:T(8,128)(2,1)S(1)} %copy-done.9), custom_call_target="tpu_custom_call" | custom-call | bytes 2000000 | tf_op jit(solution)/shard_map/pallas_call | solution.py:240
  153.8 4.6 abs_reduce_fusion.6
  159.5 27.5 %shard_map.395 = (f32[320,768]{1,0:T(8,128)S(1)}, bf16[8,144,768]{2,1,0:T(8,128)(2,1)S(1)}) custom-call(f32[320,768]{1,0:T(8,128)S(1)} %fusion.73.refs_0_, bf16[144,768]{1,0:T(8,128)(2,1)S(1)} %copy-done.8), custom_call_target="tpu_custom_call" | custom-call | bytes 2000000 | tf_op jit(solution)/shard_map/pallas_call | solution.py:240
  200.0 29.2 %shard_map.396 = (f32[320,768]{1,0:T(8,128)S(1)}, bf16[8,624,256]{2,1,0:T(8,128)(2,1)S(1)}) custom-call(f32[320,768]{1,0:T(8,128)S(1)} %fusion.192.refs_0_, bf16[624,256]{1,0:T(8,128)(2,1)S(1)} %copy-done.7), custom_call_target="tpu_custom_call" | custom-call | bytes 2000000 | tf_op jit(solution)/shard_map/pallas_call | solution.py:240
  234.9 3.2 abs_reduce_fusion.10
  244.7 5.7 abs_reduce_fusion.8
  253.0 11.7 %shard_map.397 = f32[320,768]{1,0:T(8,128)S(1)} custom-call(f32[320,768]{1,0:T(8,128)S(1)} %fusion.66.refs_0_), custom_call_target="tpu_custom_call" | custom-call | bytes 2000000 | tf_op jit(solution)/shard_map/pallas_call | solution.py:240
  305.7 16.7 %all-gather.2.cloned.1.call-done = bf16[2,1280,1024]{2,1,0:T(8,128)(2,1)} async-done(((bf16[2,160,1024]{2,1,0:T(8,128)(2,1)}), bf16[2,1280,1024]{2,1,0:T(8,128)(2,1)}) %all-gather.2.cloned.1.call-update) | async-done | bytes 5242896 | tf_op jit(solution)/shard_map/all_gather | solution.py:1088
  340.3 4.6 collective-permute-done.7
  344.9 6.1 collective-permute-done.10
  360.3 12.1 %shard_map.398 = f32[256,1024]{1,0:T(8,128)S(1)} custom-call(f32[256,1024]{1,0:T(8,128)S(1)} %fusion.136.refs_0_), custom_call_target="tpu_custom_call" | custom-call | bytes 2000000 | tf_op jit(solution)/shard_map/pallas_call | solution.py:240
  376.1 12.1 %shard_map.399 = f32[256,1024]{1,0:T(8,128)S(1)} custom-call(f32[256,1024]{1,0:T(8,128)S(1)} %fusion.129.refs_0_), custom_call_target="tpu_custom_call" | custom-call | bytes 2000000 | tf_op jit(solution)/shard_map/pallas_call | solution.py:240
  397.0 12.1 %shard_map.400 = f32[256,1024]{1,0:T(8,128)S(1)} custom-call(f32[256,1024]{1,0:T(8,128)S(1)} %fusion.131.refs_0_), custom_call_target="tpu_custom_call" | custom-call | bytes 2000000 | tf_op jit(solution)/shard_map/pallas_call | solution.py:240
  430.4 12.1 %shard_map.401 = f32[256,1024]{1,0:T(8,128)S(1)} custom-call(f32[256,1024]{1,0:T(8,128)S(1)} %fusion.138.refs_0_), custom_call_target="tpu_custom_call" | custom-call | bytes 2000000 | tf_op jit(solution)/shard_map/pallas_call | solution.py:240
  472.8 12.1 %shard_map.402 = f32[256,1024]{1,0:T(8,128)S(1)} custom-call(f32[256,1024]{1,0:T(8,128)S(1)} %fusion.23.refs_0_), custom_call_target="tpu_custom_call" | custom-call | bytes 2000000 | tf_op jit(solution)/shard_map/pallas_call | solution.py:240
  492.5 6.0 collective-permute-done.15
  532.1 11.7 %shard_map.403 = f32[320,768]{1,0:T(8,128)S(1)} custom-call(f32[320,768]{1,0:T(8,128)S(1)} %fusion.68.refs_0_), custom_call_target="tpu_custom_call" | custom-call | bytes 2000000 | tf_op jit(solution)/shard_map/pallas_call | solution.py:240
  581.4 11.6 %shard_map.404 = f32[320,768]{1,0:T(8,128)S(1)} custom-call(f32[320,768]{1,0:T(8,128)S(1)} %fusion.251.refs_0_), custom_call_target="tpu_custom_call" | custom-call | bytes 2000000 | tf_op jit(solution)/shard_map/pallas_call | solution.py:240
  620.5 11.7 %shard_map.405 = f32[320,768]{1,0:T(8,128)S(1)} custom-call(f32[320,768]{1,0:T(8,128)S(1)} %fusion.75.refs_0_), custom_call_target="tpu_custom_call" | custom-call | bytes 2000000 | tf_op jit(solution)/shard_map/pallas_call | solution.py:240
  635.7 3.3 multiply_reduce_fusion.28
  679.6 33.7 %collective-permute-done.28 = f16[880,768]{1,0:T(8,128)(2,1)} collective-permute-done((f16[880,768]{1,0:T(8,128)(2,1)}, f16[880,768]{1,0:T(8,128)(2,1)}, u32[]{:S(2)}, u32[]{:S(2)}) %collective-permute-start.28) | collective-permute-done | bytes 1351712 | tf_op jit(solution)/shard_map/ppermute | solution.py:96
  713.3 11.7 %shard_map.406 = f32[320,768]{1,0:T(8,128)S(1)} custom-call(f32[320,768]{1,0:T(8,128)S(1)} %fusion.248.refs_0_), custom_call_target="tpu_custom_call" | custom-call | bytes 2000000 | tf_op jit(solution)/shard_map/pallas_call | solution.py:240
  741.9 3.7 multiply_reduce_fusion.23
  747.6 11.5 %collective-permute-done.33 = f16[304,768]{1,0:T(8,128)(2,1)} collective-permute-done((f16[304,768]{1,0:T(8,128)(2,1)}, f16[304,768]{1,0:T(8,128)(2,1)}, u32[]{:S(2)}, u32[]{:S(2)}) %collective-permute-start.33) | collective-permute-done | bytes 466976 | tf_op jit(solution)/shard_map/ppermute | solution.py:96
  764.4 6.8 collective-permute-done.34
  772.6 27.7 %shard_map.407 = (f32[4,96,184]{2,1,0:T(8,128)S(1)}, f32[216,128]{1,0:T(8,128)S(1)}) custom-call(f32[4,96,184]{2,1,0:T(8,128)S(1)} %get-tuple-element.436.refs_0_, f32[4,96,184]{2,1,0:T(8,128)S(1)} %get-tuple-element.435.refs_1_, f32[216,128]{1,0:T(8,128)S(1)} %pad.110.refs_2_), custom_call_target="tpu_custom_call" | custom-call | tf_op jit(solution)/shard_map/pallas_call | solution.py:529
  808.8 3.8 multiply_reduce_fusion.24
  815.3 12.8 %shard_map.408 = f32[8,128]{1,0:T(8,128)} custom-call(f32[8,128]{1,0:T(8,128)} %broadcast_select_fusion.value), custom_call_target="tpu_custom_call" | custom-call | tf_op jit(solution)/shard_map/pallas_call | solution.py:322
  832.2 3.5 fusion.255
  843.4 3.6 fusion.261
  (1152 shorter events, 372.0 us)
Async XLA Ops:
  7.2 315.2 %all-gather.2.cloned.1.call-start = ((), (), s32[]{:S(2)}) async-start(), calls=%async_computation | async-start | bytes 5898240 | tf_op jit(solution)/shard_map/all_gather | solution.py:1088
  230.6 56.7 %collective-permute-start.4 = (bf16[256,256]{1,0:T(8,128)(2,1)}, bf16[256,256]{1,0:T(8,128)(2,1)}, u32[]{:S(2)}, u32[]{:S(2)}) collective-permute-start(bf16[256,256]{1,0:T(8,128)(2,1)} %get-tuple-element.538), channel_id=1, source_target_pairs={{0,2},{1,3},{2,0},{3,1},{4,6},{5,7},{6,4},{7,5},{8,10},{9,11},{10,... | collective-permute-start | bytes 393224 | tf_op jit(solution)/shard_map/ppermute | solution.py:96
  230.6 62.3 %collective-permute-start.3 = (bf16[256,256]{1,0:T(8,128)(2,1)}, bf16[256,256]{1,0:T(8,128)(2,1)}, u32[]{:S(2)}, u32[]{:S(2)}) collective-permute-start(bf16[256,256]{1,0:T(8,128)(2,1)} %get-tuple-element.538), channel_id=1, source_target_pairs={{0,1},{1,0},{2,3},{3,2},{4,5},{5,4},{6,7},{7,6},{8,9},{9,8},{10,11... | collective-permute-start | bytes 393224 | tf_op jit(solution)/shard_map/ppermute | solution.py:96
  232.6 48.1 %collective-permute-start.1 = (bf16[1920,256]{1,0:T(8,128)(2,1)}, bf16[1920,256]{1,0:T(8,128)(2,1)}, u32[]{:S(2)}, u32[]{:S(2)}) collective-permute-start(bf16[1920,256]{1,0:T(8,128)(2,1)} %pad_maximum_fusion.7), channel_id=1, source_target_pairs={{0,2},{1,3},{2,0},{3,1},{4,6},{5,7},{6,4},{7,5},{8,10},{9,11},{10,... | collective-permute-start | bytes 2949128 | tf_op jit(solution)/shard_map/ppermute | solution.py:96
  234.6 61.5 %collective-permute-start = (bf16[1920,256]{1,0:T(8,128)(2,1)}, bf16[1920,256]{1,0:T(8,128)(2,1)}, u32[]{:S(2)}, u32[]{:S(2)}) collective-permute-start(bf16[1920,256]{1,0:T(8,128)(2,1)} %pad_maximum_fusion.7), channel_id=1, source_target_pairs={{0,1},{1,0},{2,3},{3,2},{4,5},{5,4},{6,7},{7,6},{8,9},{9,8},{10,11... | collective-permute-start | bytes 2949128 | tf_op jit(solution)/shard_map/ppermute | solution.py:96
  280.7 15.4 %collective-permute-start.2 = (bf16[1920,256]{1,0:T(8,128)(2,1)}, bf16[1920,256]{1,0:T(8,128)(2,1)}, u32[]{:S(2)}, u32[]{:S(2)}) collective-permute-start(bf16[1920,256]{1,0:T(8,128)(2,1)} %collective-permute-done.1), channel_id=1, source_target_pairs={{0,1},{1,0},{2,3},{3,2},{4,5},{5,4},{6,7},{7,6},{8,9},{9,8},{10,11... | collective-permute-start | bytes 2949128 | tf_op jit(solution)/shard_map/ppermute | solution.py:96
  332.5 12.4 %collective-permute-start.7 = (bf16[256,768]{1,0:T(8,128)(2,1)}, bf16[256,768]{1,0:T(8,128)(2,1)}, u32[]{:S(2)}, u32[]{:S(2)}) collective-permute-start(bf16[256,768]{1,0:T(8,128)(2,1)} %fusion.47), channel_id=1, source_target_pairs={{0,2},{1,3},{2,0},{3,1},{4,6},{5,7},{6,4},{7,5},{8,10},{9,11},{10,... | collective-permute-start | bytes 1179656 | tf_op jit(solution)/shard_map/ppermute | solution.py:96
  333.1 17.9 %collective-permute-start.10 = (bf16[256,768]{1,0:T(8,128)(2,1)}, bf16[256,768]{1,0:T(8,128)(2,1)}, u32[]{:S(2)}, u32[]{:S(2)}) collective-permute-start(bf16[256,768]{1,0:T(8,128)(2,1)} %fusion.44), channel_id=1, source_target_pairs={{0,2},{1,3},{2,0},{3,1},{4,6},{5,7},{6,4},{7,5},{8,10},{9,11},{10,... | collective-permute-start | bytes 1179656 | tf_op jit(solution)/shard_map/ppermute | solution.py:96
  334.9 16.1 %collective-permute-start.14 = (bf16[256,512]{1,0:T(8,128)(2,1)}, bf16[256,512]{1,0:T(8,128)(2,1)}, u32[]{:S(2)}, u32[]{:S(2)}) collective-permute-start(bf16[256,512]{1,0:T(8,128)(2,1)} %collective-permute-done.13), channel_id=1, source_target_pairs={{0,1},{1,0},{2,3},{3,2},{4,5},{5,4},{6,7},{7,6},{8,9},{9,8},{10,11... | collective-permute-start | bytes 786440 | tf_op jit(solution)/shard_map/ppermute | solution.py:96
  339.0 15.6 %collective-permute-start.6 = (bf16[256,768]{1,0:T(8,128)(2,1)}, bf16[256,768]{1,0:T(8,128)(2,1)S(1)}, u32[]{:S(2)}, u32[]{:S(2)}) collective-permute-start(bf16[256,768]{1,0:T(8,128)(2,1)} %fusion.47), channel_id=1, source_target_pairs={{0,1},{1,0},{2,3},{3,2},{4,5},{5,4},{6,7},{7,6},{8,9},{9,8},{10,11... | collective-permute-start | bytes 1179656 | tf_op jit(solution)/shard_map/ppermute | solution.py:96
  339.7 12.8 %collective-permute-start.9 = (bf16[256,768]{1,0:T(8,128)(2,1)}, bf16[256,768]{1,0:T(8,128)(2,1)S(1)}, u32[]{:S(2)}, u32[]{:S(2)}) collective-permute-start(bf16[256,768]{1,0:T(8,128)(2,1)} %fusion.44), channel_id=1, source_target_pairs={{0,1},{1,0},{2,3},{3,2},{4,5},{5,4},{6,7},{7,6},{8,9},{9,8},{10,11... | collective-permute-start | bytes 1179656 | tf_op jit(solution)/shard_map/ppermute | solution.py:96
  465.8 32.7 %collective-permute-start.15 = (f16[656,1024]{1,0:T(8,128)(2,1)}, f16[656,1024]{1,0:T(8,128)(2,1)}, u32[]{:S(2)}, u32[]{:S(2)}) collective-permute-start(f16[656,1024]{1,0:T(8,128)(2,1)} %select_convert_fusion.3), channel_id=1, source_target_pairs={{0,4},{4,0},{8,12},{12,8},{16,20},{20,16},{24,28},{28,24},{1,5},{5... | collective-permute-start | bytes 4030472 | tf_op jit(solution)/shard_map/ppermute | solution.py:96
  484.9 62.4 %collective-permute-start.16 = (f16[656,1024]{1,0:T(8,128)(2,1)}, f16[656,1024]{1,0:T(8,128)(2,1)}, u32[]{:S(2)}, u32[]{:S(2)}) collective-permute-start(f16[656,1024]{1,0:T(8,128)(2,1)} %select_convert_fusion.2), channel_id=1, source_target_pairs={{0,4},{4,0},{8,12},{12,8},{16,20},{20,16},{24,28},{28,24},{1,5},{5... | collective-permute-start | bytes 4030472 | tf_op jit(solution)/shard_map/ppermute | solution.py:96
  514.6 42.3 %collective-permute-start.17 = (f16[176,1024]{1,0:T(8,128)(2,1)}, f16[176,1024]{1,0:T(8,128)(2,1)S(1)}, u32[]{:S(2)}, u32[]{:S(2)}) collective-permute-start(f16[176,1024]{1,0:T(8,128)(2,1)} %get-tuple-element.133), channel_id=1, source_target_pairs={{0,8},{4,12},{8,0},{12,4},{16,24},{20,28},{24,16},{28,20},{1,9},{5... | collective-permute-start | bytes 1081352 | tf_op jit(solution)/shard_map/ppermute | solution.py:443
  514.8 42.2 %collective-permute-start.18 = (f16[176,1024]{1,0:T(8,128)(2,1)}, f16[176,1024]{1,0:T(8,128)(2,1)}, u32[]{:S(2)}, u32[]{:S(2)}) collective-permute-start(f16[176,1024]{1,0:T(8,128)(2,1)} %get-tuple-element.134), channel_id=1, source_target_pairs={{0,16},{4,20},{8,24},{12,28},{16,0},{20,4},{24,8},{28,12},{1,17},{... | collective-permute-start | bytes 1081352 | tf_op jit(solution)/shard_map/ppermute | solution.py:443
  517.6 39.3 %collective-permute-start.19 = (f16[176,1024]{1,0:T(8,128)(2,1)}, f16[176,1024]{1,0:T(8,128)(2,1)}, u32[]{:S(2)}, u32[]{:S(2)}) collective-permute-start(f16[176,1024]{1,0:T(8,128)(2,1)} %get-tuple-element.135), channel_id=1, source_target_pairs={{0,24},{4,28},{8,16},{12,20},{16,8},{20,12},{24,0},{28,4},{1,25},{... | collective-permute-start | bytes 1081352 | tf_op jit(solution)/shard_map/ppermute | solution.py:443
  548.0 52.0 %collective-permute-start.20 = (f16[2512,256]{1,0:T(8,128)(2,1)}, f16[2512,256]{1,0:T(8,128)(2,1)}, u32[]{:S(2)}, u32[]{:S(2)}) collective-permute-start(f16[2512,256]{1,0:T(8,128)(2,1)} %select_convert_fusion.4), channel_id=1, source_target_pairs={{0,4},{4,0},{8,12},{12,8},{16,20},{20,16},{24,28},{28,24},{1,5},{5... | collective-permute-start | bytes 3858440 | tf_op jit(solution)/shard_map/ppermute | solution.py:96
  566.2 38.4 %collective-permute-start.21 = (f16[176,1024]{1,0:T(8,128)(2,1)}, f16[176,1024]{1,0:T(8,128)(2,1)}, u32[]{:S(2)}, u32[]{:S(2)}) collective-permute-start(f16[176,1024]{1,0:T(8,128)(2,1)} %get-tuple-element.141), channel_id=1, source_target_pairs={{0,8},{4,12},{8,0},{12,4},{16,24},{20,28},{24,16},{28,20},{1,9},{5... | collective-permute-start | bytes 1081352 | tf_op jit(solution)/shard_map/ppermute | solution.py:443
  566.2 38.4 %collective-permute-start.22 = (f16[176,1024]{1,0:T(8,128)(2,1)}, f16[176,1024]{1,0:T(8,128)(2,1)}, u32[]{:S(2)}, u32[]{:S(2)}) collective-permute-start(f16[176,1024]{1,0:T(8,128)(2,1)} %get-tuple-element.142), channel_id=1, source_target_pairs={{0,16},{4,20},{8,24},{12,28},{16,0},{20,4},{24,8},{28,12},{1,17},{... | collective-permute-start | bytes 1081352 | tf_op jit(solution)/shard_map/ppermute | solution.py:443
  569.2 35.3 %collective-permute-start.23 = (f16[176,1024]{1,0:T(8,128)(2,1)}, f16[176,1024]{1,0:T(8,128)(2,1)}, u32[]{:S(2)}, u32[]{:S(2)}) collective-permute-start(f16[176,1024]{1,0:T(8,128)(2,1)} %get-tuple-element.143), channel_id=1, source_target_pairs={{0,24},{4,28},{8,16},{12,20},{16,8},{20,12},{24,0},{28,4},{1,25},{... | collective-permute-start | bytes 1081352 | tf_op jit(solution)/shard_map/ppermute | solution.py:443
  593.0 50.5 %collective-permute-start.24 = (f16[1168,768]{1,0:T(8,128)(2,1)}, f16[1168,768]{1,0:T(8,128)(2,1)}, u32[]{:S(2)}, u32[]{:S(2)}) collective-permute-start(f16[1168,768]{1,0:T(8,128)(2,1)} %select_convert_fusion), channel_id=1, source_target_pairs={{0,4},{4,0},{8,12},{12,8},{16,20},{20,16},{24,28},{28,24},{1,5},{5... | collective-permute-start | bytes 5382152 | tf_op jit(solution)/shard_map/ppermute | solution.py:96
  610.2 38.0 %collective-permute-start.25 = (f16[640,256]{1,0:T(8,128)(2,1)}, f16[640,256]{1,0:T(8,128)(2,1)}, u32[]{:S(2)}, u32[]{:S(2)}) collective-permute-start(f16[640,256]{1,0:T(8,128)(2,1)} %get-tuple-element.148), channel_id=1, source_target_pairs={{0,8},{4,12},{8,0},{12,4},{16,24},{20,28},{24,16},{28,20},{1,9},{5... | collective-permute-start | bytes 983048 | tf_op jit(solution)/shard_map/ppermute | solution.py:443
  610.3 37.9 %collective-permute-start.26 = (f16[640,256]{1,0:T(8,128)(2,1)}, f16[640,256]{1,0:T(8,128)(2,1)}, u32[]{:S(2)}, u32[]{:S(2)}) collective-permute-start(f16[640,256]{1,0:T(8,128)(2,1)} %get-tuple-element.149), channel_id=1, source_target_pairs={{0,16},{4,20},{8,24},{12,28},{16,0},{20,4},{24,8},{28,12},{1,17},{... | collective-permute-start | bytes 983048 | tf_op jit(solution)/shard_map/ppermute | solution.py:443
  613.3 34.9 %collective-permute-start.27 = (f16[640,256]{1,0:T(8,128)(2,1)}, f16[640,256]{1,0:T(8,128)(2,1)}, u32[]{:S(2)}, u32[]{:S(2)}) collective-permute-start(f16[640,256]{1,0:T(8,128)(2,1)} %get-tuple-element.150), channel_id=1, source_target_pairs={{0,24},{4,28},{8,16},{12,20},{16,8},{20,12},{24,0},{28,4},{1,25},{... | collective-permute-start | bytes 983048 | tf_op jit(solution)/shard_map/ppermute | solution.py:443
  657.4 67.6 %collective-permute-start.29 = (f16[304,768]{1,0:T(8,128)(2,1)}, f16[304,768]{1,0:T(8,128)(2,1)}, u32[]{:S(2)}, u32[]{:S(2)}) collective-permute-start(f16[304,768]{1,0:T(8,128)(2,1)} %get-tuple-element.164), channel_id=1, source_target_pairs={{0,8},{4,12},{8,0},{12,4},{16,24},{20,28},{24,16},{28,20},{1,9},{5... | collective-permute-start | bytes 1400840 | tf_op jit(solution)/shard_map/ppermute | solution.py:443
  657.5 67.6 %collective-permute-start.30 = (f16[304,768]{1,0:T(8,128)(2,1)}, f16[304,768]{1,0:T(8,128)(2,1)}, u32[]{:S(2)}, u32[]{:S(2)}) collective-permute-start(f16[304,768]{1,0:T(8,128)(2,1)} %get-tuple-element.165), channel_id=1, source_target_pairs={{0,16},{4,20},{8,24},{12,28},{16,0},{20,4},{24,8},{28,12},{1,17},{... | collective-permute-start | bytes 1400840 | tf_op jit(solution)/shard_map/ppermute | solution.py:443
  660.5 64.6 %collective-permute-start.31 = (f16[304,768]{1,0:T(8,128)(2,1)}, f16[304,768]{1,0:T(8,128)(2,1)}, u32[]{:S(2)}, u32[]{:S(2)}) collective-permute-start(f16[304,768]{1,0:T(8,128)(2,1)} %get-tuple-element.166), channel_id=1, source_target_pairs={{0,24},{4,28},{8,16},{12,20},{16,8},{20,12},{24,0},{28,4},{1,25},{... | collective-permute-start | bytes 1400840 | tf_op jit(solution)/shard_map/ppermute | solution.py:443
  671.9 53.1 %collective-permute-start.32 = (f16[304,768]{1,0:T(8,128)(2,1)}, f16[304,768]{1,0:T(8,128)(2,1)S(1)}, u32[]{:S(2)}, u32[]{:S(2)}) collective-permute-start(f16[304,768]{1,0:T(8,128)(2,1)} %select_convert_fusion.8), channel_id=1, source_target_pairs={{0,4},{4,0},{8,12},{12,8},{16,20},{20,16},{24,28},{28,24},{1,5},{5... | collective-permute-start | bytes 1400840 | tf_op jit(solution)/shard_map/ppermute | solution.py:96
  672.5 40.8 %collective-permute-start.28 = (f16[880,768]{1,0:T(8,128)(2,1)}, f16[880,768]{1,0:T(8,128)(2,1)}, u32[]{:S(2)}, u32[]{:S(2)}) collective-permute-start(f16[880,768]{1,0:T(8,128)(2,1)} %select_convert_fusion.1), channel_id=1, source_target_pairs={{0,4},{4,0},{8,12},{12,8},{16,20},{20,16},{24,28},{28,24},{1,5},{5... | collective-permute-start | bytes 4055048 | tf_op jit(solution)/shard_map/ppermute | solution.py:96
  736.2 22.9 %collective-permute-start.33 = (f16[304,768]{1,0:T(8,128)(2,1)}, f16[304,768]{1,0:T(8,128)(2,1)}, u32[]{:S(2)}, u32[]{:S(2)}) collective-permute-start(f16[304,768]{1,0:T(8,128)(2,1)} %get-tuple-element.173), channel_id=1, source_target_pairs={{0,8},{4,12},{8,0},{12,4},{16,24},{20,28},{24,16},{28,20},{1,9},{5... | collective-permute-start | bytes 1400840 | tf_op jit(solution)/shard_map/ppermute | solution.py:96
  736.2 34.9 %collective-permute-start.34 = (f16[304,768]{1,0:T(8,128)(2,1)}, f16[304,768]{1,0:T(8,128)(2,1)}, u32[]{:S(2)}, u32[]{:S(2)}) collective-permute-start(f16[304,768]{1,0:T(8,128)(2,1)} %get-tuple-element.176), channel_id=1, source_target_pairs={{0,16},{4,20},{8,24},{12,28},{16,0},{20,4},{24,8},{28,12},{1,17},{... | collective-permute-start | bytes 1400840 | tf_op jit(solution)/shard_map/ppermute | solution.py:96
  739.3 60.9 %collective-permute-start.35 = (f16[304,768]{1,0:T(8,128)(2,1)}, f16[304,768]{1,0:T(8,128)(2,1)}, u32[]{:S(2)}, u32[]{:S(2)}) collective-permute-start(f16[304,768]{1,0:T(8,128)(2,1)} %get-tuple-element.178), channel_id=1, source_target_pairs={{0,24},{4,28},{8,16},{12,20},{16,8},{20,12},{24,0},{28,4},{1,25},{... | collective-permute-start | bytes 1400840 | tf_op jit(solution)/shard_map/ppermute | solution.py:96
  (345 other events, 2425.2 us)
Sparse Core Ops, SparseCore 0:
  235.0 87.3 all-gather.1

commit v4 on v3

--- a/solution.py
+++ b/solution.py
@@ -119,7 +119,14 @@
         self.beside = rank + 1 - 2 * self.low
         self.ahead = 2 * lax.rem(self.high + 1, 4) + self.low
         self.behind = 2 * lax.rem(self.high + 3, 4) + self.low
-        self.shares, self.wholes = shares, wholes
+        self.shares, self.wholes = [], []
+        for share, whole in zip(shares, wholes):
+            rows = share.shape[0]
+            cut = -(-rows // 32) * 16
+            for start, size in ((0, cut), (cut, rows - cut)):
+                self.shares.append(share.at[pl.ds(start, size)])
+                self.wholes.append(whole.at[:, pl.ds(start, size)])
+        shares, wholes = self.shares, self.wholes
         self.send_sem, self.recv_sem = send_sem, recv_sem
         self.items = range(len(shares))
         self.sent = []
@@ -169,7 +176,8 @@
             kept.wait()
 
 
-def ring_scratch(count):
+def ring_scratch(arrays):
+    count = 2 * arrays
     return [
         pltpu.SemaphoreType.DMA((count,)),
         pltpu.SemaphoreType.DMA((count, 8)),
@@ -387,8 +395,8 @@
 
 
 class Scattered:
-    def __init__(self, pairs, first=0):
-        self.pairs, self.first = pairs, max(first, 0)
+    def __init__(self, pairs, first=0, split=False):
+        self.pairs, self.first, self.split = pairs, max(first, 0), split
         self.count = 4 - first if first >= 0 else -first
         self.got, self.parts, self.owned, self.owned_square = None, None, None, None
         self.level = bound_level(pairs)
@@ -409,21 +417,30 @@
         low = lax.axis_index(dp_axis) % 2
         blocks = grad.reshape(self.count, 2 * slab, grad.shape[1])
         give = lax.dynamic_slice_in_dim(blocks, (1 - low) * slab, slab, 1)
+        if self.split:
+            return [coded(give[place], self.level) for place in range(self.count)]
         return coded(give.reshape(-1, grad.shape[1]), self.level)
 
     def send_near(self, message):
-        self.got = swap(message, dp_axis, 1)
+        parts = [swap(part, dp_axis, 1) for part in (message if self.split else [message])]
+        self.got = parts if self.split else parts[0]
 
     def got_level(self):
-        at = self.count * self.slab()
-        return self.got[at : at + 1].astype(jnp.float32)
+        slab = self.slab()
+        got, at = (self.got[0], slab) if self.split else (self.got, self.count * slab)
+        return got[at : at + 1].astype(jnp.float32)
 
     def share(self, place):
         grad, slab = self.grad(), self.slab()
         low = lax.axis_index(dp_axis) % 2
         place = jnp.clip(place - self.first, 0, self.count - 1)
         kept = lax.dynamic_slice_in_dim(grad, (2 * place + low) * slab, slab, 0)
-        arrived = lax.dynamic_slice_in_dim(self.got, place * slab, slab, 0)
+        if self.split:
+            arrived = self.got[0][:slab]
+            for index in range(1, self.count):
+                arrived = jnp.where(place == index, self.got[index][:slab], arrived)
+        else:
+            arrived = lax.dynamic_slice_in_dim(self.got, place * slab, slab, 0)
         return kept + arrived.astype(jnp.float32) * jnp.exp2(self.got_level() - 13.0)
 
     def far_messages(self):
@@ -475,7 +492,7 @@
     for peer in peers:
         pl.semaphore_signal(barrier, inc=1, device_id=peer, device_id_type=MESH)
     pl.semaphore_wait(barrier, len(peers))
-    slots = iter(range(14))
+    slots = iter(range(17))
 
     def send(source, target, peer):
         slot = next(slots)
@@ -504,8 +521,10 @@
     middle[...] = near[0] + near[1] + near[2] + near[3]
     send(middle, beside_sum, beside).wait()
     pair_sum[...] = middle[...] + beside_sum[...]
-    far_sum[high] = pair_sum[...]
-    bias_far = [send(pair_sum, far_sum.at[high], peer) for peer in pair_peers]
+    rows = bias_total.shape[0] // 4
+    mine = pl.ds(pl.multiple_of(across * rows, 8), rows)
+    far_sum[high] = pair_sum[mine, :]
+    bias_far = [send(pair_sum.at[mine], far_sum.at[high], peer) for peer in pair_peers]
     for copy in tables_far:
         copy.wait()
     own[...] = pairs[high] + far[0] + far[1] + far[2]
@@ -513,8 +532,9 @@
     tables_all = [send(own, tables.at[across], peer) for peer in tensor_peers]
     for copy in bias_far:
         copy.wait()
-    bias_total[...] = far_sum[0] + far_sum[1] + far_sum[2] + far_sum[3]
-    for copy in tables_all:
+    bias_total[mine, :] = far_sum[0] + far_sum[1] + far_sum[2] + far_sum[3]
+    bias_all = [send(bias_total.at[mine], bias_total.at[mine], peer) for peer in tensor_peers]
+    for copy in tables_all + bias_all:
         copy.wait()
 
 
@@ -543,9 +563,9 @@
             pltpu.VMEM(bias.shape, jnp.float32),
             pltpu.VMEM(bias.shape, jnp.float32),
             pltpu.VMEM(bias.shape, jnp.float32),
-            pltpu.VMEM((4,) + bias.shape, jnp.float32),
-            pltpu.SemaphoreType.DMA((14,)),
-            pltpu.SemaphoreType.DMA((14,)),
+            pltpu.VMEM((4, bias.shape[0] // 4, bias.shape[1]), jnp.float32),
+            pltpu.SemaphoreType.DMA((17,)),
+            pltpu.SemaphoreType.DMA((17,)),
         ],
         compiler_params=pltpu.CompilerParams(
             collective_id=last_exchange, has_side_effects=True, vmem_limit_bytes=24 << 20
@@ -589,8 +609,8 @@
             group = self.groups[back_encoder]
             done = [self.groups[key] for key in (back_head, back_head + 1, rest_group)]
             totals = [(item.total(), item.square()) for item in done]
-            partial_term, group.got, totals = lax.optimization_barrier(
-                (partial_term, group.got, totals)
+            partial_term, group.got[1], totals = lax.optimization_barrier(
+                (partial_term, group.got[1], totals)
             )
             for item, (total, square) in zip(done, totals):
                 item.owned, item.owned_square = total, square
@@ -598,7 +618,8 @@
         total = self.tie(total, [], far, arrived)
         if kernel == back_encoder + 1:
             mix = self.groups[mix_group]
-            total, mix.got = lax.optimization_barrier((total, mix.got))
+            rest = self.groups[back_encoder]
+            total, mix.got, rest.got[2] = lax.optimization_barrier((total, mix.got, rest.got[2]))
             total, messages = lax.optimization_barrier((total, self.encoder_messages()))
             self.encoder_parts = [
                 swap(message, dp_axis, 2 * step) for step, message in zip((1, 2, 3), messages)
@@ -854,17 +875,21 @@
     grad_middle = flow + grad_middle
     grad_attn = narrow(grad_middle)
     grad_attended = narrow(product_right(grad_attn, proj_rows)).reshape(parts[0].shape)
+    later = [(grad_inner, second), (attended, grad_attn), (active, grad_branch)]
+    apart = kernel == back_encoder and lax.axis_size(dp_axis) == 8
+    if apart:
+        owned_rows = [traffic.add(kernel, Scattered(later, 1, True))]
+        grad_attended = traffic.tie(grad_attended, owned_rows, [], [])
     grads_mixed = attention_back(parts[0], parts[1], parts[2], visible, log_total, grad_attended)
     grad_mixed = narrow(
         jnp.concatenate([piece.reshape(-1, local_width) for piece in grads_mixed], axis=1)
     )
     mix = [(grad_mixed, normed)]
-    later = [(grad_inner, second), (attended, grad_attn), (active, grad_branch)]
-    if kernel == back_encoder and lax.axis_size(dp_axis) == 8:
-        owned_rows = [
-            traffic.add(mix_group, Scattered(mix, -1)),
-            traffic.add(kernel, Scattered(later, 1)),
-        ]
+    if apart:
+        grad_mixed, owned_rows[0].got[0] = lax.optimization_barrier(
+            (grad_mixed, owned_rows[0].got[0])
+        )
+        traffic.add(mix_group, Scattered(mix, -1))
     else:
         owned_rows = [traffic.add(kernel, Scattered(mix + later))]
     grad_normed = traffic.input_sum(product(grad_mixed, mix_rows), kernel + 1)
@@ -1110,6 +1135,9 @@
     )
     latent = narrow(layer_norm(decoded, final_norms[2], final_norms[3])[:, BUF:].reshape(-1, D))
     condition = product(latent, cond_weight) + rest_bias[0]
+    decoded, timesteps, noise, clean = lax.optimization_barrier(
+        (decoded, timesteps, noise, patch_flat)
+    )
     step_rows = timesteps.reshape(COPIES, -1)
     time_feat = narrow(sinusoid(step_rows).reshape(-1, HW))
     time_pre = product(time_feat, time_first) + lax.dynamic_slice_in_dim(
@@ -1123,7 +1151,7 @@
     phase = step_rows.astype(jnp.float32)[..., None] * (math.pi / (2 * T_STEPS))
     signal_coef = jnp.cos(phase)
     noise_coef = jnp.sin(phase)
-    clean = patch_flat.astype(jnp.float32)[None]
+    clean = clean.astype(jnp.float32)[None]
     noise_rows = noise.reshape(COPIES, -1, TOKD).astype(jnp.float32)
     noisy_rows = narrow((signal_coef * clean + noise_coef * noise_rows).reshape(-1, TOKD))
     target = (signal_coef * noise_rows - noise_coef * clean).reshape(-1, TOKD)
@@ -1173,7 +1201,7 @@
             back_decoder: ([rest_group], [back_head], [back_head + 1]),
             back_decoder + 1: ([back_decoder], [rest_group], [back_head]),
             back_encoder: ([], [back_decoder], [rest_group]),
-            back_encoder + 1: ([back_encoder, mix_group], [], [back_decoder]),
+            back_encoder + 1: ([mix_group], [], [back_decoder]),
         }
     )
     cond_split = product_right(grad_shift_last, final_shift) + product_right(
@@ -1290,7 +1318,7 @@
     bias_local = jnp.concatenate(bias_parts + column_grads).reshape(-1, lanes)
     if dp_size == 8 and tensor_size == 4:
         bias_count = bias_local.shape[0]
-        bias_local = jnp.pad(bias_local, ((0, -bias_count % 8), (0, 0)))
+        bias_local = jnp.pad(bias_local, ((0, -bias_count % 32), (0, 0)))
         grad_tables = traffic.arrive(grad_tables, 1)
         owned_cols, bias_grad = tail_exchange(grad_tables.T, bias_local)
         encoder_owned, (owned_cols, bias_grad) = traffic.encoder_total((owned_cols, bias_grad))

time: 870 us -> 841 us (0.967)
  waiting for transfers between devices: 86 us -> 72.6 us
  Pallas kernels: 305 us -> 295 us
    ppermute x24 -> x26, waiting for transfers between devices: 69.2 us -> 64.4 us  [swap(): lax.ppermute(value, axis, [(i, i ^ step) for i in range(lax.axis_size(axi...]
    ppermute x24 -> x26, starting transfers between devices: 18.3 us -> 20 us  [swap(): lax.ppermute(value, axis, [(i, i ^ step) for i in range(lax.axis_size(axi...]
    unnamed x685 -> x659, local copies, waits for them, and re-layouts: 36.9 us -> 37.6 us
  transfers between devices with their start and end apart: 37 -> 39, of which waited for: 8 -> 11; matrix products, arithmetic and copies ran while one was open for 20% -> 20% of each run, Pallas kernels for 11% -> 12%
where the time goes in v4:
time: 841 us; the launch traced here: 829 us
  Pallas kernels  295 us (35%)
  other arithmetic  179 us (21%)
  local copies, waits for them, and re-layouts  95.1 us (11%)
  matrix products  91.2 us (11%)
  waiting for transfers between devices  72.6 us (9%)
  between operations  58.3 us (7%)
  starting transfers between devices  37.7 us (4%)
    pallas_call x13, Pallas kernels, tensor_sum(): pl.pallas_call(functools.partial(sum_kernel, count, cross_type), out_shap...  197 us
    ppermute x26, waiting for transfers between devices, swap(): lax.ppermute(value, axis, [(i, i ^ step) for i in range(lax.axis_size(axi...  64.4 us
    pallas_call x1, Pallas kernels, gather_first(): pl.pallas_call(functools.partial(first_kernel, images), out_shape=[jax.Sh...  61.7 us
    unnamed x659, local copies, waits for them, and re-layouts  37.6 us
    dot_general x18, matrix products, product_right(): lax.dot_general(left, right, (((1,), (1,)), ((), ())), preferred_element_...  32.6 us
    dot_general x22, matrix products, product_left(): lax.dot_general(left, right, (((0,), (0,)), ((), ())), preferred_element_...  30.9 us
    pallas_call x1, Pallas kernels, tail_exchange(): pl.pallas_call(tail_kernel, out_shape=[jax.ShapeDtypeStruct(four, jnp.flo...  24.6 us
    dot_general x23, matrix products, product(): return jnp.dot(left, right, preferred_element_type=jnp.float32)  20.5 us
  transfers between devices with their start and end apart: 39, of which 11 were waited for; matrix products, arithmetic and copies ran while one was open for 20% of the time, Pallas kernels for 12%

profile of v4, /device:TPU:0, one launch (start us, length us, event | category | flops | bytes accessed | tf_op | source)
XLA Modules:
  0.0 828.9 jit_solution(14990186150898118168)
XLA Ops:
  25.1 61.7 %shard_map.393 = (f32[8,8,128]{2,1,0:T(8,128)S(1)}, f32[8,96,128]{2,1,0:T(8,128)S(1)}, f32[4,8,184,96]{3,2,1,0:T(8,128)S(1)}, bf16[8,288,768]{2,1,0:T(8,128)(2,1)S(1)}) custom-call(f32[8,128]{1,0:T(8,128)S(1)} %dynamic_update_slice.82.notes, f32[96,1001]{1,0:T(8,128)S(1)} %copy-done.6, f32[184,96]{1,0:T(8,128)S(1)} %fusion.215.table_share, ...), custom_call_target="tpu_custom_call" | custom-call | tf_op jit(solution)/shard_map/pallas_call | solution.py:741
  90.7 4.2 reshape.1199
  120.7 22.5 %shard_map.394 = (f32[320,768]{1,0:T(8,128)S(1)}, bf16[8,144,768]{2,1,0:T(8,128)(2,1)S(1)}) custom-call(f32[320,768]{1,0:T(8,128)S(1)} %fusion.196.refs_0_, bf16[144,768]{1,0:T(8,128)(2,1)S(1)} %copy-done.9), custom_call_target="tpu_custom_call" | custom-call | bytes 2000000 | tf_op jit(solution)/shard_map/pallas_call | solution.py:248
  145.4 4.6 abs_reduce_fusion.6
  151.1 23.4 %shard_map.395 = (f32[320,768]{1,0:T(8,128)S(1)}, bf16[8,144,768]{2,1,0:T(8,128)(2,1)S(1)}) custom-call(f32[320,768]{1,0:T(8,128)S(1)} %fusion.73.refs_0_, bf16[144,768]{1,0:T(8,128)(2,1)S(1)} %copy-done.8), custom_call_target="tpu_custom_call" | custom-call | bytes 2000000 | tf_op jit(solution)/shard_map/pallas_call | solution.py:248
  184.4 28.8 %shard_map.396 = (f32[320,768]{1,0:T(8,128)S(1)}, bf16[8,624,256]{2,1,0:T(8,128)(2,1)S(1)}) custom-call(f32[320,768]{1,0:T(8,128)S(1)} %fusion.193.refs_0_, bf16[624,256]{1,0:T(8,128)(2,1)S(1)} %copy-done.7), custom_call_target="tpu_custom_call" | custom-call | bytes 2000000 | tf_op jit(solution)/shard_map/pallas_call | solution.py:248
  222.7 4.6 abs_reduce_fusion.8
  228.7 15.0 %shard_map.397 = f32[320,768]{1,0:T(8,128)S(1)} custom-call(f32[320,768]{1,0:T(8,128)S(1)} %fusion.66.refs_0_), custom_call_target="tpu_custom_call" | custom-call | bytes 2000000 | tf_op jit(solution)/shard_map/pallas_call | solution.py:248
  294.2 8.1 all-gather.2.cloned.1.call-done
  316.1 8.1 collective-permute-done.7
  324.2 6.0 collective-permute-done.10
  338.6 12.1 %shard_map.398 = f32[256,1024]{1,0:T(8,128)S(1)} custom-call(f32[256,1024]{1,0:T(8,128)S(1)} %fusion.137.refs_0_), custom_call_target="tpu_custom_call" | custom-call | bytes 2000000 | tf_op jit(solution)/shard_map/pallas_call | solution.py:248
  354.5 12.1 %shard_map.399 = f32[256,1024]{1,0:T(8,128)S(1)} custom-call(f32[256,1024]{1,0:T(8,128)S(1)} %fusion.130.refs_0_), custom_call_target="tpu_custom_call" | custom-call | bytes 2000000 | tf_op jit(solution)/shard_map/pallas_call | solution.py:248
  375.3 12.1 %shard_map.400 = f32[256,1024]{1,0:T(8,128)S(1)} custom-call(f32[256,1024]{1,0:T(8,128)S(1)} %fusion.132.refs_0_), custom_call_target="tpu_custom_call" | custom-call | bytes 2000000 | tf_op jit(solution)/shard_map/pallas_call | solution.py:248
  409.0 12.1 %shard_map.401 = f32[256,1024]{1,0:T(8,128)S(1)} custom-call(f32[256,1024]{1,0:T(8,128)S(1)} %fusion.139.refs_0_), custom_call_target="tpu_custom_call" | custom-call | bytes 2000000 | tf_op jit(solution)/shard_map/pallas_call | solution.py:248
  451.1 12.1 %shard_map.402 = f32[256,1024]{1,0:T(8,128)S(1)} custom-call(f32[256,1024]{1,0:T(8,128)S(1)} %fusion.23.refs_0_), custom_call_target="tpu_custom_call" | custom-call | bytes 2000000 | tf_op jit(solution)/shard_map/pallas_call | solution.py:248
  472.0 5.4 collective-permute-done.15
  511.0 11.7 %shard_map.403 = f32[320,768]{1,0:T(8,128)S(1)} custom-call(f32[320,768]{1,0:T(8,128)S(1)} %fusion.68.refs_0_), custom_call_target="tpu_custom_call" | custom-call | bytes 2000000 | tf_op jit(solution)/shard_map/pallas_call | solution.py:248
  544.8 3.4 collective-permute-start.22
  560.0 11.6 %shard_map.404 = f32[320,768]{1,0:T(8,128)S(1)} custom-call(f32[320,768]{1,0:T(8,128)S(1)} %fusion.251.refs_0_), custom_call_target="tpu_custom_call" | custom-call | bytes 2000000 | tf_op jit(solution)/shard_map/pallas_call | solution.py:248
  600.4 11.7 %shard_map.405 = f32[320,768]{1,0:T(8,128)S(1)} custom-call(f32[320,768]{1,0:T(8,128)S(1)} %fusion.75.refs_0_), custom_call_target="tpu_custom_call" | custom-call | bytes 2000000 | tf_op jit(solution)/shard_map/pallas_call | solution.py:248
  663.7 9.0 %collective-permute-done.29 = f16[304,768]{1,0:T(8,128)(2,1)S(1)} collective-permute-done((f16[304,768]{1,0:T(8,128)(2,1)}, f16[304,768]{1,0:T(8,128)(2,1)S(1)}, u32[]{:S(2)}, u32[]{:S(2)}) %collective-permute-start.29) | collective-permute-done | bytes 466976 | tf_op jit(solution)/shard_map/ppermute | solution.py:96
  673.5 11.6 %shard_map.406 = f32[320,768]{1,0:T(8,128)S(1)} custom-call(f32[320,768]{1,0:T(8,128)S(1)} %fusion.326.refs_0_), custom_call_target="tpu_custom_call" | custom-call | bytes 2000000 | tf_op jit(solution)/shard_map/pallas_call | solution.py:248
  689.4 3.6 multiply_reduce_fusion.25
  693.1 6.4 collective-permute-done.33
  714.6 15.3 %collective-permute-done.35 = f16[304,768]{1,0:T(8,128)(2,1)S(1)} collective-permute-done((f16[304,768]{1,0:T(8,128)(2,1)S(1)}, f16[304,768]{1,0:T(8,128)(2,1)S(1)}, u32[]{:S(2)}, u32[]{:S(2)}) %collective-permute-start.35) | collective-permute-done | bytes 466976 | tf_op jit(solution)/shard_map/ppermute | solution.py:96
  735.7 10.9 %collective-permute-done.36 = f16[304,768]{1,0:T(8,128)(2,1)} collective-permute-done((f16[304,768]{1,0:T(8,128)(2,1)}, f16[304,768]{1,0:T(8,128)(2,1)}, u32[]{:S(2)}, u32[]{:S(2)}) %collective-permute-start.36) | collective-permute-done | bytes 466976 | tf_op jit(solution)/shard_map/ppermute | solution.py:96
  748.1 24.6 %shard_map.407 = (f32[4,96,184]{2,1,0:T(8,128)S(1)}, f32[224,128]{1,0:T(8,128)S(1)}) custom-call(f32[4,96,184]{2,1,0:T(8,128)S(1)} %get-tuple-element.455.refs_0_, f32[4,96,184]{2,1,0:T(8,128)S(1)} %get-tuple-element.454.refs_1_, f32[224,128]{1,0:T(8,128)S(1)} %pad.117.refs_2_), custom_call_target="tpu_custom_call" | custom-call | tf_op jit(solution)/shard_map/pallas_call | solution.py:549
  782.3 4.0 multiply_reduce_fusion.26
  789.0 11.3 %shard_map.408 = f32[8,128]{1,0:T(8,128)} custom-call(f32[8,128]{1,0:T(8,128)} %broadcast_select_fusion.value), custom_call_target="tpu_custom_call" | custom-call | tf_op jit(solution)/shard_map/pallas_call | solution.py:330
  804.4 3.6 fusion.255
  815.7 3.6 fusion.261
  (1136 shorter events, 375.1 us)
Async XLA Ops:
  7.2 295.2 %all-gather.2.cloned.1.call-start = ((), (), s32[]{:S(2)}) async-start(), calls=%async_computation | async-start | bytes 5898240 | tf_op jit(solution)/shard_map/all_gather | solution.py:1113
  215.3 53.4 %collective-permute-start.1 = (bf16[1920,256]{1,0:T(8,128)(2,1)}, bf16[1920,256]{1,0:T(8,128)(2,1)}, u32[]{:S(2)}, u32[]{:S(2)}) collective-permute-start(bf16[1920,256]{1,0:T(8,128)(2,1)} %pad_maximum_fusion.7), channel_id=1, source_target_pairs={{0,2},{1,3},{2,0},{3,1},{4,6},{5,7},{6,4},{7,5},{8,10},{9,11},{10,... | collective-permute-start | bytes 2949128 | tf_op jit(solution)/shard_map/ppermute | solution.py:96
  216.9 67.6 %collective-permute-start = (bf16[1920,256]{1,0:T(8,128)(2,1)}, bf16[1920,256]{1,0:T(8,128)(2,1)}, u32[]{:S(2)}, u32[]{:S(2)}) collective-permute-start(bf16[1920,256]{1,0:T(8,128)(2,1)} %pad_maximum_fusion.7), channel_id=1, source_target_pairs={{0,1},{1,0},{2,3},{3,2},{4,5},{5,4},{6,7},{7,6},{8,9},{9,8},{10,11... | collective-permute-start | bytes 2949128 | tf_op jit(solution)/shard_map/ppermute | solution.py:96
  249.8 27.4 %collective-permute-start.4 = (bf16[256,256]{1,0:T(8,128)(2,1)}, bf16[256,256]{1,0:T(8,128)(2,1)}, u32[]{:S(2)}, u32[]{:S(2)}) collective-permute-start(bf16[256,256]{1,0:T(8,128)(2,1)} %get-tuple-element.562), channel_id=1, source_target_pairs={{0,2},{1,3},{2,0},{3,1},{4,6},{5,7},{6,4},{7,5},{8,10},{9,11},{10,... | collective-permute-start | bytes 393224 | tf_op jit(solution)/shard_map/ppermute | solution.py:96
  251.5 29.6 %collective-permute-start.3 = (bf16[256,256]{1,0:T(8,128)(2,1)}, bf16[256,256]{1,0:T(8,128)(2,1)}, u32[]{:S(2)}, u32[]{:S(2)}) collective-permute-start(bf16[256,256]{1,0:T(8,128)(2,1)} %get-tuple-element.562), channel_id=1, source_target_pairs={{0,1},{1,0},{2,3},{3,2},{4,5},{5,4},{6,7},{7,6},{8,9},{9,8},{10,11... | collective-permute-start | bytes 393224 | tf_op jit(solution)/shard_map/ppermute | solution.py:96
  268.7 15.8 %collective-permute-start.2 = (bf16[1920,256]{1,0:T(8,128)(2,1)}, bf16[1920,256]{1,0:T(8,128)(2,1)}, u32[]{:S(2)}, u32[]{:S(2)}) collective-permute-start(bf16[1920,256]{1,0:T(8,128)(2,1)} %collective-permute-done.1), channel_id=1, source_target_pairs={{0,1},{1,0},{2,3},{3,2},{4,5},{5,4},{6,7},{7,6},{8,9},{9,8},{10,11... | collective-permute-start | bytes 2949128 | tf_op jit(solution)/shard_map/ppermute | solution.py:96
  312.4 17.8 %collective-permute-start.10 = (bf16[256,768]{1,0:T(8,128)(2,1)S(1)}, bf16[256,768]{1,0:T(8,128)(2,1)S(1)}, u32[]{:S(2)}, u32[]{:S(2)}) collective-permute-start(bf16[256,768]{1,0:T(8,128)(2,1)S(1)} %fusion.44), channel_id=1, source_target_pairs={{0,2},{1,3},{2,0},{3,1},{4,6},{5,7},{6,4},{7,5},{8,10},{9,11},{10,... | collective-permute-start | bytes 1179656 | tf_op jit(solution)/shard_map/ppermute | solution.py:96
  314.2 16.0 %collective-permute-start.14 = (bf16[256,512]{1,0:T(8,128)(2,1)}, bf16[256,512]{1,0:T(8,128)(2,1)}, u32[]{:S(2)}, u32[]{:S(2)}) collective-permute-start(bf16[256,512]{1,0:T(8,128)(2,1)} %collective-permute-done.13), channel_id=1, source_target_pairs={{0,1},{1,0},{2,3},{3,2},{4,5},{5,4},{6,7},{7,6},{8,9},{9,8},{10,11... | collective-permute-start | bytes 786440 | tf_op jit(solution)/shard_map/ppermute | solution.py:96
  314.8 18.5 %collective-permute-start.6 = (bf16[256,768]{1,0:T(8,128)(2,1)}, bf16[256,768]{1,0:T(8,128)(2,1)}, u32[]{:S(2)}, u32[]{:S(2)}) collective-permute-start(bf16[256,768]{1,0:T(8,128)(2,1)} %fusion.47), channel_id=1, source_target_pairs={{0,1},{1,0},{2,3},{3,2},{4,5},{5,4},{6,7},{7,6},{8,9},{9,8},{10,11... | collective-permute-start | bytes 1179656 | tf_op jit(solution)/shard_map/ppermute | solution.py:96
  315.9 16.0 %collective-permute-start.9 = (bf16[256,768]{1,0:T(8,128)(2,1)S(1)}, bf16[256,768]{1,0:T(8,128)(2,1)S(1)}, u32[]{:S(2)}, u32[]{:S(2)}) collective-permute-start(bf16[256,768]{1,0:T(8,128)(2,1)S(1)} %fusion.44), channel_id=1, source_target_pairs={{0,1},{1,0},{2,3},{3,2},{4,5},{5,4},{6,7},{7,6},{8,9},{9,8},{10,11... | collective-permute-start | bytes 1179656 | tf_op jit(solution)/shard_map/ppermute | solution.py:96
  444.7 32.7 %collective-permute-start.15 = (f16[656,1024]{1,0:T(8,128)(2,1)}, f16[656,1024]{1,0:T(8,128)(2,1)}, u32[]{:S(2)}, u32[]{:S(2)}) collective-permute-start(f16[656,1024]{1,0:T(8,128)(2,1)} %select_convert_fusion.2), channel_id=1, source_target_pairs={{0,4},{4,0},{8,12},{12,8},{16,20},{20,16},{24,28},{28,24},{1,5},{5... | collective-permute-start | bytes 4030472 | tf_op jit(solution)/shard_map/ppermute | solution.py:96
  463.2 63.0 %collective-permute-start.16 = (f16[656,1024]{1,0:T(8,128)(2,1)}, f16[656,1024]{1,0:T(8,128)(2,1)}, u32[]{:S(2)}, u32[]{:S(2)}) collective-permute-start(f16[656,1024]{1,0:T(8,128)(2,1)} %select_convert_fusion.1), channel_id=1, source_target_pairs={{0,4},{4,0},{8,12},{12,8},{16,20},{20,16},{24,28},{28,24},{1,5},{5... | collective-permute-start | bytes 4030472 | tf_op jit(solution)/shard_map/ppermute | solution.py:96
  493.5 42.8 %collective-permute-start.17 = (f16[176,1024]{1,0:T(8,128)(2,1)}, f16[176,1024]{1,0:T(8,128)(2,1)}, u32[]{:S(2)}, u32[]{:S(2)}) collective-permute-start(f16[176,1024]{1,0:T(8,128)(2,1)} %get-tuple-element.147), channel_id=1, source_target_pairs={{0,8},{4,12},{8,0},{12,4},{16,24},{20,28},{24,16},{28,20},{1,9},{5... | collective-permute-start | bytes 1081352 | tf_op jit(solution)/shard_map/ppermute | solution.py:460
  493.7 42.6 %collective-permute-start.18 = (f16[176,1024]{1,0:T(8,128)(2,1)}, f16[176,1024]{1,0:T(8,128)(2,1)}, u32[]{:S(2)}, u32[]{:S(2)}) collective-permute-start(f16[176,1024]{1,0:T(8,128)(2,1)} %get-tuple-element.148), channel_id=1, source_target_pairs={{0,16},{4,20},{8,24},{12,28},{16,0},{20,4},{24,8},{28,12},{1,17},{... | collective-permute-start | bytes 1081352 | tf_op jit(solution)/shard_map/ppermute | solution.py:460
  496.5 39.7 %collective-permute-start.19 = (f16[176,1024]{1,0:T(8,128)(2,1)}, f16[176,1024]{1,0:T(8,128)(2,1)}, u32[]{:S(2)}, u32[]{:S(2)}) collective-permute-start(f16[176,1024]{1,0:T(8,128)(2,1)} %get-tuple-element.149), channel_id=1, source_target_pairs={{0,24},{4,28},{8,16},{12,20},{16,8},{20,12},{24,0},{28,4},{1,25},{... | collective-permute-start | bytes 1081352 | tf_op jit(solution)/shard_map/ppermute | solution.py:460
  526.9 53.1 %collective-permute-start.20 = (f16[2512,256]{1,0:T(8,128)(2,1)}, f16[2512,256]{1,0:T(8,128)(2,1)}, u32[]{:S(2)}, u32[]{:S(2)}) collective-permute-start(f16[2512,256]{1,0:T(8,128)(2,1)} %select_convert_fusion.3), channel_id=1, source_target_pairs={{0,4},{4,0},{8,12},{12,8},{16,20},{20,16},{24,28},{28,24},{1,5},{5... | collective-permute-start | bytes 3858440 | tf_op jit(solution)/shard_map/ppermute | solution.py:96
  544.8 39.7 %collective-permute-start.21 = (f16[176,1024]{1,0:T(8,128)(2,1)}, f16[176,1024]{1,0:T(8,128)(2,1)}, u32[]{:S(2)}, u32[]{:S(2)}) collective-permute-start(f16[176,1024]{1,0:T(8,128)(2,1)} %get-tuple-element.155), channel_id=1, source_target_pairs={{0,8},{4,12},{8,0},{12,4},{16,24},{20,28},{24,16},{28,20},{1,9},{5... | collective-permute-start | bytes 1081352 | tf_op jit(solution)/shard_map/ppermute | solution.py:460
  544.8 39.7 %collective-permute-start.22 = (f16[176,1024]{1,0:T(8,128)(2,1)}, f16[176,1024]{1,0:T(8,128)(2,1)}, u32[]{:S(2)}, u32[]{:S(2)}) collective-permute-start(f16[176,1024]{1,0:T(8,128)(2,1)} %get-tuple-element.156), channel_id=1, source_target_pairs={{0,16},{4,20},{8,24},{12,28},{16,0},{20,4},{24,8},{28,12},{1,17},{... | collective-permute-start | bytes 1081352 | tf_op jit(solution)/shard_map/ppermute | solution.py:460
  548.3 36.2 %collective-permute-start.23 = (f16[176,1024]{1,0:T(8,128)(2,1)}, f16[176,1024]{1,0:T(8,128)(2,1)}, u32[]{:S(2)}, u32[]{:S(2)}) collective-permute-start(f16[176,1024]{1,0:T(8,128)(2,1)} %get-tuple-element.157), channel_id=1, source_target_pairs={{0,24},{4,28},{8,16},{12,20},{16,8},{20,12},{24,0},{28,4},{1,25},{... | collective-permute-start | bytes 1081352 | tf_op jit(solution)/shard_map/ppermute | solution.py:460
  571.7 51.6 %collective-permute-start.24 = (f16[1168,768]{1,0:T(8,128)(2,1)}, f16[1168,768]{1,0:T(8,128)(2,1)}, u32[]{:S(2)}, u32[]{:S(2)}) collective-permute-start(f16[1168,768]{1,0:T(8,128)(2,1)} %select_convert_fusion), channel_id=1, source_target_pairs={{0,4},{4,0},{8,12},{12,8},{16,20},{20,16},{24,28},{28,24},{1,5},{5... | collective-permute-start | bytes 5382152 | tf_op jit(solution)/shard_map/ppermute | solution.py:96
  590.1 37.8 %collective-permute-start.25 = (f16[640,256]{1,0:T(8,128)(2,1)}, f16[640,256]{1,0:T(8,128)(2,1)}, u32[]{:S(2)}, u32[]{:S(2)}) collective-permute-start(f16[640,256]{1,0:T(8,128)(2,1)} %get-tuple-element.162), channel_id=1, source_target_pairs={{0,8},{4,12},{8,0},{12,4},{16,24},{20,28},{24,16},{28,20},{1,9},{5... | collective-permute-start | bytes 983048 | tf_op jit(solution)/shard_map/ppermute | solution.py:460
  590.2 37.7 %collective-permute-start.26 = (f16[640,256]{1,0:T(8,128)(2,1)}, f16[640,256]{1,0:T(8,128)(2,1)}, u32[]{:S(2)}, u32[]{:S(2)}) collective-permute-start(f16[640,256]{1,0:T(8,128)(2,1)} %get-tuple-element.163), channel_id=1, source_target_pairs={{0,16},{4,20},{8,24},{12,28},{16,0},{20,4},{24,8},{28,12},{1,17},{... | collective-permute-start | bytes 983048 | tf_op jit(solution)/shard_map/ppermute | solution.py:460
  593.2 34.7 %collective-permute-start.27 = (f16[640,256]{1,0:T(8,128)(2,1)}, f16[640,256]{1,0:T(8,128)(2,1)}, u32[]{:S(2)}, u32[]{:S(2)}) collective-permute-start(f16[640,256]{1,0:T(8,128)(2,1)} %get-tuple-element.164), channel_id=1, source_target_pairs={{0,24},{4,28},{8,16},{12,20},{16,8},{20,12},{24,0},{28,4},{1,25},{... | collective-permute-start | bytes 983048 | tf_op jit(solution)/shard_map/ppermute | solution.py:460
  643.9 41.5 %collective-permute-start.30 = (f16[304,768]{1,0:T(8,128)(2,1)}, f16[304,768]{1,0:T(8,128)(2,1)}, u32[]{:S(2)}, u32[]{:S(2)}) collective-permute-start(f16[304,768]{1,0:T(8,128)(2,1)} %get-tuple-element.181), channel_id=1, source_target_pairs={{0,8},{4,12},{8,0},{12,4},{16,24},{20,28},{24,16},{28,20},{1,9},{5... | collective-permute-start | bytes 1400840 | tf_op jit(solution)/shard_map/ppermute | solution.py:460
  643.9 41.5 %collective-permute-start.31 = (f16[304,768]{1,0:T(8,128)(2,1)}, f16[304,768]{1,0:T(8,128)(2,1)}, u32[]{:S(2)}, u32[]{:S(2)}) collective-permute-start(f16[304,768]{1,0:T(8,128)(2,1)} %get-tuple-element.182), channel_id=1, source_target_pairs={{0,16},{4,20},{8,24},{12,28},{16,0},{20,4},{24,8},{28,12},{1,17},{... | collective-permute-start | bytes 1400840 | tf_op jit(solution)/shard_map/ppermute | solution.py:460
  646.9 38.5 %collective-permute-start.32 = (f16[304,768]{1,0:T(8,128)(2,1)}, f16[304,768]{1,0:T(8,128)(2,1)}, u32[]{:S(2)}, u32[]{:S(2)}) collective-permute-start(f16[304,768]{1,0:T(8,128)(2,1)} %get-tuple-element.183), channel_id=1, source_target_pairs={{0,24},{4,28},{8,16},{12,20},{16,8},{20,12},{24,0},{28,4},{1,25},{... | collective-permute-start | bytes 1400840 | tf_op jit(solution)/shard_map/ppermute | solution.py:460
  648.9 13.8 %collective-permute-start.28 = (f16[304,768]{1,0:T(8,128)(2,1)}, f16[304,768]{1,0:T(8,128)(2,1)S(1)}, u32[]{:S(2)}, u32[]{:S(2)}) collective-permute-start(f16[304,768]{1,0:T(8,128)(2,1)} %get-tuple-element.167), channel_id=1, source_target_pairs={{0,4},{4,0},{8,12},{12,8},{16,20},{20,16},{24,28},{28,24},{1,5},{5... | collective-permute-start | bytes 1400840 | tf_op jit(solution)/shard_map/ppermute | solution.py:96
  648.9 23.8 %collective-permute-start.29 = (f16[304,768]{1,0:T(8,128)(2,1)}, f16[304,768]{1,0:T(8,128)(2,1)S(1)}, u32[]{:S(2)}, u32[]{:S(2)}) collective-permute-start(f16[304,768]{1,0:T(8,128)(2,1)} %get-tuple-element.170), channel_id=1, source_target_pairs={{0,4},{4,0},{8,12},{12,8},{16,20},{20,16},{24,28},{28,24},{1,5},{5... | collective-permute-start | bytes 1400840 | tf_op jit(solution)/shard_map/ppermute | solution.py:96
  662.7 30.4 %collective-permute-start.34 = (f16[304,768]{1,0:T(8,128)(2,1)}, f16[304,768]{1,0:T(8,128)(2,1)}, u32[]{:S(2)}, u32[]{:S(2)}) collective-permute-start(f16[304,768]{1,0:T(8,128)(2,1)} %get-tuple-element.186), channel_id=1, source_target_pairs={{0,4},{4,0},{8,12},{12,8},{16,20},{20,16},{24,28},{28,24},{1,5},{5... | collective-permute-start | bytes 1400840 | tf_op jit(solution)/shard_map/ppermute | solution.py:96
  709.2 20.6 %collective-permute-start.35 = (f16[304,768]{1,0:T(8,128)(2,1)S(1)}, f16[304,768]{1,0:T(8,128)(2,1)S(1)}, u32[]{:S(2)}, u32[]{:S(2)}) collective-permute-start(f16[304,768]{1,0:T(8,128)(2,1)S(1)} %get-tuple-element.193), channel_id=1, source_target_pairs={{0,8},{4,12},{8,0},{12,4},{16,24},{20,28},{24,16},{28,20},{1,9},{5... | collective-permute-start | bytes 1400840 | tf_op jit(solution)/shard_map/ppermute | solution.py:96
  711.8 34.9 %collective-permute-start.36 = (f16[304,768]{1,0:T(8,128)(2,1)}, f16[304,768]{1,0:T(8,128)(2,1)}, u32[]{:S(2)}, u32[]{:S(2)}) collective-permute-start(f16[304,768]{1,0:T(8,128)(2,1)} %get-tuple-element.196), channel_id=1, source_target_pairs={{0,16},{4,20},{8,24},{12,28},{16,0},{20,4},{24,8},{28,12},{1,17},{... | collective-permute-start | bytes 1400840 | tf_op jit(solution)/shard_map/ppermute | solution.py:96
  712.7 60.0 %collective-permute-start.37 = (f16[304,768]{1,0:T(8,128)(2,1)}, f16[304,768]{1,0:T(8,128)(2,1)}, u32[]{:S(2)}, u32[]{:S(2)}) collective-permute-start(f16[304,768]{1,0:T(8,128)(2,1)} %get-tuple-element.198), channel_id=1, source_target_pairs={{0,24},{4,28},{8,16},{12,20},{16,8},{20,12},{24,0},{28,4},{1,25},{... | collective-permute-start | bytes 1400840 | tf_op jit(solution)/shard_map/ppermute | solution.py:96
  (335 other events, 2183.9 us)
Sparse Core Ops, SparseCore 0:
  217.1 85.2 all-gather.1

commit v5 on v4

--- a/solution.py
+++ b/solution.py
@@ -620,7 +620,10 @@
             mix = self.groups[mix_group]
             rest = self.groups[back_encoder]
             total, mix.got, rest.got[2] = lax.optimization_barrier((total, mix.got, rest.got[2]))
-            total, messages = lax.optimization_barrier((total, self.encoder_messages()))
+            decoder = self.groups[back_decoder]
+            total, messages, decoder.parts = lax.optimization_barrier(
+                (total, self.encoder_messages(), decoder.parts)
+            )
             self.encoder_parts = [
                 swap(message, dp_axis, 2 * step) for step, message in zip((1, 2, 3), messages)
             ]

time: 841 us -> 836 us (level)
  waiting for transfers between devices: 72.6 us -> 63 us
    ppermute x26, waiting for transfers between devices: 64.4 us -> 55 us  [swap(): lax.ppermute(value, axis, [(i, i ^ step) for i in range(lax.axis_size(axi...]
    unnamed x659 -> x655, local copies, waits for them, and re-layouts: 37.6 us -> 39.4 us
  transfers between devices with their start and end apart: 39 -> 39, of which waited for: 11 -> 11; matrix products, arithmetic and copies ran while one was open for 20% -> 21% of each run, Pallas kernels for 12% -> 12%
where the time goes in v5:
time: 836 us; the launch traced here: 824 us
  Pallas kernels  295 us (35%)
  other arithmetic  180 us (22%)
  local copies, waits for them, and re-layouts  99.1 us (12%)
  matrix products  91.1 us (11%)
  waiting for transfers between devices  63 us (8%)
  between operations  58.4 us (7%)
  starting transfers between devices  37.8 us (5%)
    pallas_call x13, Pallas kernels, tensor_sum(): pl.pallas_call(functools.partial(sum_kernel, count, cross_type), out_shap...  197 us
    pallas_call x1, Pallas kernels, gather_first(): pl.pallas_call(functools.partial(first_kernel, images), out_shape=[jax.Sh...  61.7 us
    ppermute x26, waiting for transfers between devices, swap(): lax.ppermute(value, axis, [(i, i ^ step) for i in range(lax.axis_size(axi...  55 us
    unnamed x655, local copies, waits for them, and re-layouts  39.4 us
    dot_general x18, matrix products, product_right(): lax.dot_general(left, right, (((1,), (1,)), ((), ())), preferred_element_...  32.6 us
    dot_general x22, matrix products, product_left(): lax.dot_general(left, right, (((0,), (0,)), ((), ())), preferred_element_...  30.8 us
    pallas_call x1, Pallas kernels, tail_exchange(): pl.pallas_call(tail_kernel, out_shape=[jax.ShapeDtypeStruct(four, jnp.flo...  24.6 us
    dot_general x23, matrix products, product(): return jnp.dot(left, right, preferred_element_type=jnp.float32)  20.5 us
  transfers between devices with their start and end apart: 39, of which 11 were waited for; matrix products, arithmetic and copies ran while one was open for 21% of the time, Pallas kernels for 12%

profile of v5, /device:TPU:0, one launch (start us, length us, event | category | flops | bytes accessed | tf_op | source)
XLA Modules:
  0.0 823.8 jit_solution(17555614830756285373)
XLA Ops:
  25.1 61.7 %shard_map.393 = (f32[8,8,128]{2,1,0:T(8,128)S(1)}, f32[8,96,128]{2,1,0:T(8,128)S(1)}, f32[4,8,184,96]{3,2,1,0:T(8,128)S(1)}, bf16[8,288,768]{2,1,0:T(8,128)(2,1)S(1)}) custom-call(f32[8,128]{1,0:T(8,128)S(1)} %dynamic_update_slice.82.notes, f32[96,1001]{1,0:T(8,128)S(1)} %copy-done.6, f32[184,96]{1,0:T(8,128)S(1)} %fusion.215.table_share, ...), custom_call_target="tpu_custom_call" | custom-call | tf_op jit(solution)/shard_map/pallas_call | solution.py:744
  90.6 4.2 reshape.1199
  120.6 22.5 %shard_map.394 = (f32[320,768]{1,0:T(8,128)S(1)}, bf16[8,144,768]{2,1,0:T(8,128)(2,1)S(1)}) custom-call(f32[320,768]{1,0:T(8,128)S(1)} %fusion.196.refs_0_, bf16[144,768]{1,0:T(8,128)(2,1)S(1)} %copy-done.9), custom_call_target="tpu_custom_call" | custom-call | bytes 2000000 | tf_op jit(solution)/shard_map/pallas_call | solution.py:248
  145.3 4.5 abs_reduce_fusion.6
  151.0 23.4 %shard_map.395 = (f32[320,768]{1,0:T(8,128)S(1)}, bf16[8,144,768]{2,1,0:T(8,128)(2,1)S(1)}) custom-call(f32[320,768]{1,0:T(8,128)S(1)} %fusion.73.refs_0_, bf16[144,768]{1,0:T(8,128)(2,1)S(1)} %copy-done.8), custom_call_target="tpu_custom_call" | custom-call | bytes 2000000 | tf_op jit(solution)/shard_map/pallas_call | solution.py:248
  184.3 28.8 %shard_map.396 = (f32[320,768]{1,0:T(8,128)S(1)}, bf16[8,624,256]{2,1,0:T(8,128)(2,1)S(1)}) custom-call(f32[320,768]{1,0:T(8,128)S(1)} %fusion.193.refs_0_, bf16[624,256]{1,0:T(8,128)(2,1)S(1)} %copy-done.7), custom_call_target="tpu_custom_call" | custom-call | bytes 2000000 | tf_op jit(solution)/shard_map/pallas_call | solution.py:248
  222.6 4.5 abs_reduce_fusion.8
  228.5 15.1 %shard_map.397 = f32[320,768]{1,0:T(8,128)S(1)} custom-call(f32[320,768]{1,0:T(8,128)S(1)} %fusion.66.refs_0_), custom_call_target="tpu_custom_call" | custom-call | bytes 2000000 | tf_op jit(solution)/shard_map/pallas_call | solution.py:248
  294.4 7.9 all-gather.2.cloned.1.call-done
  316.0 8.1 collective-permute-done.7
  324.2 6.0 collective-permute-done.10
  338.6 12.1 %shard_map.398 = f32[256,1024]{1,0:T(8,128)S(1)} custom-call(f32[256,1024]{1,0:T(8,128)S(1)} %fusion.137.refs_0_), custom_call_target="tpu_custom_call" | custom-call | bytes 2000000 | tf_op jit(solution)/shard_map/pallas_call | solution.py:248
  354.5 12.1 %shard_map.399 = f32[256,1024]{1,0:T(8,128)S(1)} custom-call(f32[256,1024]{1,0:T(8,128)S(1)} %fusion.130.refs_0_), custom_call_target="tpu_custom_call" | custom-call | bytes 2000000 | tf_op jit(solution)/shard_map/pallas_call | solution.py:248
  375.4 12.1 %shard_map.400 = f32[256,1024]{1,0:T(8,128)S(1)} custom-call(f32[256,1024]{1,0:T(8,128)S(1)} %fusion.132.refs_0_), custom_call_target="tpu_custom_call" | custom-call | bytes 2000000 | tf_op jit(solution)/shard_map/pallas_call | solution.py:248
  409.1 12.1 %shard_map.401 = f32[256,1024]{1,0:T(8,128)S(1)} custom-call(f32[256,1024]{1,0:T(8,128)S(1)} %fusion.139.refs_0_), custom_call_target="tpu_custom_call" | custom-call | bytes 2000000 | tf_op jit(solution)/shard_map/pallas_call | solution.py:248
  451.1 12.1 %shard_map.402 = f32[256,1024]{1,0:T(8,128)S(1)} custom-call(f32[256,1024]{1,0:T(8,128)S(1)} %fusion.23.refs_0_), custom_call_target="tpu_custom_call" | custom-call | bytes 2000000 | tf_op jit(solution)/shard_map/pallas_call | solution.py:248
  472.1 5.2 collective-permute-done.15
  511.1 11.7 %shard_map.403 = f32[320,768]{1,0:T(8,128)S(1)} custom-call(f32[320,768]{1,0:T(8,128)S(1)} %fusion.68.refs_0_), custom_call_target="tpu_custom_call" | custom-call | bytes 2000000 | tf_op jit(solution)/shard_map/pallas_call | solution.py:248
  546.0 3.4 collective-permute-start.22
  561.1 11.6 %shard_map.404 = f32[320,768]{1,0:T(8,128)S(1)} custom-call(f32[320,768]{1,0:T(8,128)S(1)} %fusion.251.refs_0_), custom_call_target="tpu_custom_call" | custom-call | bytes 2000000 | tf_op jit(solution)/shard_map/pallas_call | solution.py:248
  577.7 3.3 multiply_reduce_fusion.29
  600.9 11.7 %shard_map.405 = f32[320,768]{1,0:T(8,128)S(1)} custom-call(f32[320,768]{1,0:T(8,128)S(1)} %fusion.75.refs_0_), custom_call_target="tpu_custom_call" | custom-call | bytes 2000000 | tf_op jit(solution)/shard_map/pallas_call | solution.py:248
  664.2 9.1 %collective-permute-done.29 = f16[304,768]{1,0:T(8,128)(2,1)S(1)} collective-permute-done((f16[304,768]{1,0:T(8,128)(2,1)}, f16[304,768]{1,0:T(8,128)(2,1)S(1)}, u32[]{:S(2)}, u32[]{:S(2)}) %collective-permute-start.29) | collective-permute-done | bytes 466976 | tf_op jit(solution)/shard_map/ppermute | solution.py:96
  674.0 11.6 %shard_map.406 = f32[320,768]{1,0:T(8,128)S(1)} custom-call(f32[320,768]{1,0:T(8,128)S(1)} %fusion.326.refs_0_), custom_call_target="tpu_custom_call" | custom-call | bytes 2000000 | tf_op jit(solution)/shard_map/pallas_call | solution.py:248
  709.1 3.6 multiply_reduce_fusion.25
  713.1 12.9 %collective-permute-done.35 = f16[304,768]{1,0:T(8,128)(2,1)S(1)} collective-permute-done((f16[304,768]{1,0:T(8,128)(2,1)S(1)}, f16[304,768]{1,0:T(8,128)(2,1)S(1)}, u32[]{:S(2)}, u32[]{:S(2)}) %collective-permute-start.35) | collective-permute-done | bytes 466976 | tf_op jit(solution)/shard_map/ppermute | solution.py:96
  731.9 9.7 %collective-permute-done.36 = f16[304,768]{1,0:T(8,128)(2,1)} collective-permute-done((f16[304,768]{1,0:T(8,128)(2,1)}, f16[304,768]{1,0:T(8,128)(2,1)}, u32[]{:S(2)}, u32[]{:S(2)}) %collective-permute-start.36) | collective-permute-done | bytes 466976 | tf_op jit(solution)/shard_map/ppermute | solution.py:96
  743.0 24.6 %shard_map.407 = (f32[4,96,184]{2,1,0:T(8,128)S(1)}, f32[224,128]{1,0:T(8,128)S(1)}) custom-call(f32[4,96,184]{2,1,0:T(8,128)S(1)} %get-tuple-element.461.refs_0_, f32[4,96,184]{2,1,0:T(8,128)S(1)} %get-tuple-element.460.refs_1_, f32[224,128]{1,0:T(8,128)S(1)} %pad.117.refs_2_), custom_call_target="tpu_custom_call" | custom-call | tf_op jit(solution)/shard_map/pallas_call | solution.py:549
  777.2 4.0 multiply_reduce_fusion.26
  783.9 11.3 %shard_map.408 = f32[8,128]{1,0:T(8,128)} custom-call(f32[8,128]{1,0:T(8,128)} %broadcast_select_fusion.value), custom_call_target="tpu_custom_call" | custom-call | tf_op jit(solution)/shard_map/pallas_call | solution.py:330
  799.4 3.6 fusion.255
  810.7 3.6 fusion.261
  (1132 shorter events, 376.9 us)
Async XLA Ops:
  7.2 295.1 %all-gather.2.cloned.1.call-start = ((), (), s32[]{:S(2)}) async-start(), calls=%async_computation | async-start | bytes 5898240 | tf_op jit(solution)/shard_map/all_gather | solution.py:1116
  215.2 53.4 %collective-permute-start.1 = (bf16[1920,256]{1,0:T(8,128)(2,1)}, bf16[1920,256]{1,0:T(8,128)(2,1)}, u32[]{:S(2)}, u32[]{:S(2)}) collective-permute-start(bf16[1920,256]{1,0:T(8,128)(2,1)} %pad_maximum_fusion.7), channel_id=1, source_target_pairs={{0,2},{1,3},{2,0},{3,1},{4,6},{5,7},{6,4},{7,5},{8,10},{9,11},{10,... | collective-permute-start | bytes 2949128 | tf_op jit(solution)/shard_map/ppermute | solution.py:96
  216.9 67.8 %collective-permute-start = (bf16[1920,256]{1,0:T(8,128)(2,1)}, bf16[1920,256]{1,0:T(8,128)(2,1)}, u32[]{:S(2)}, u32[]{:S(2)}) collective-permute-start(bf16[1920,256]{1,0:T(8,128)(2,1)} %pad_maximum_fusion.7), channel_id=1, source_target_pairs={{0,1},{1,0},{2,3},{3,2},{4,5},{5,4},{6,7},{7,6},{8,9},{9,8},{10,11... | collective-permute-start | bytes 2949128 | tf_op jit(solution)/shard_map/ppermute | solution.py:96
  249.7 27.6 %collective-permute-start.4 = (bf16[256,256]{1,0:T(8,128)(2,1)}, bf16[256,256]{1,0:T(8,128)(2,1)}, u32[]{:S(2)}, u32[]{:S(2)}) collective-permute-start(bf16[256,256]{1,0:T(8,128)(2,1)} %get-tuple-element.568), channel_id=1, source_target_pairs={{0,2},{1,3},{2,0},{3,1},{4,6},{5,7},{6,4},{7,5},{8,10},{9,11},{10,... | collective-permute-start | bytes 393224 | tf_op jit(solution)/shard_map/ppermute | solution.py:96
  251.5 29.9 %collective-permute-start.3 = (bf16[256,256]{1,0:T(8,128)(2,1)}, bf16[256,256]{1,0:T(8,128)(2,1)}, u32[]{:S(2)}, u32[]{:S(2)}) collective-permute-start(bf16[256,256]{1,0:T(8,128)(2,1)} %get-tuple-element.568), channel_id=1, source_target_pairs={{0,1},{1,0},{2,3},{3,2},{4,5},{5,4},{6,7},{7,6},{8,9},{9,8},{10,11... | collective-permute-start | bytes 393224 | tf_op jit(solution)/shard_map/ppermute | solution.py:96
  268.6 16.0 %collective-permute-start.2 = (bf16[1920,256]{1,0:T(8,128)(2,1)}, bf16[1920,256]{1,0:T(8,128)(2,1)}, u32[]{:S(2)}, u32[]{:S(2)}) collective-permute-start(bf16[1920,256]{1,0:T(8,128)(2,1)} %collective-permute-done.1), channel_id=1, source_target_pairs={{0,1},{1,0},{2,3},{3,2},{4,5},{5,4},{6,7},{7,6},{8,9},{9,8},{10,11... | collective-permute-start | bytes 2949128 | tf_op jit(solution)/shard_map/ppermute | solution.py:96
  312.4 17.8 %collective-permute-start.10 = (bf16[256,768]{1,0:T(8,128)(2,1)S(1)}, bf16[256,768]{1,0:T(8,128)(2,1)S(1)}, u32[]{:S(2)}, u32[]{:S(2)}) collective-permute-start(bf16[256,768]{1,0:T(8,128)(2,1)S(1)} %fusion.44), channel_id=1, source_target_pairs={{0,2},{1,3},{2,0},{3,1},{4,6},{5,7},{6,4},{7,5},{8,10},{9,11},{10,... | collective-permute-start | bytes 1179656 | tf_op jit(solution)/shard_map/ppermute | solution.py:96
  314.2 16.0 %collective-permute-start.14 = (bf16[256,512]{1,0:T(8,128)(2,1)}, bf16[256,512]{1,0:T(8,128)(2,1)}, u32[]{:S(2)}, u32[]{:S(2)}) collective-permute-start(bf16[256,512]{1,0:T(8,128)(2,1)} %collective-permute-done.13), channel_id=1, source_target_pairs={{0,1},{1,0},{2,3},{3,2},{4,5},{5,4},{6,7},{7,6},{8,9},{9,8},{10,11... | collective-permute-start | bytes 786440 | tf_op jit(solution)/shard_map/ppermute | solution.py:96
  314.7 18.5 %collective-permute-start.6 = (bf16[256,768]{1,0:T(8,128)(2,1)}, bf16[256,768]{1,0:T(8,128)(2,1)}, u32[]{:S(2)}, u32[]{:S(2)}) collective-permute-start(bf16[256,768]{1,0:T(8,128)(2,1)} %fusion.47), channel_id=1, source_target_pairs={{0,1},{1,0},{2,3},{3,2},{4,5},{5,4},{6,7},{7,6},{8,9},{9,8},{10,11... | collective-permute-start | bytes 1179656 | tf_op jit(solution)/shard_map/ppermute | solution.py:96
  315.8 16.0 %collective-permute-start.9 = (bf16[256,768]{1,0:T(8,128)(2,1)S(1)}, bf16[256,768]{1,0:T(8,128)(2,1)S(1)}, u32[]{:S(2)}, u32[]{:S(2)}) collective-permute-start(bf16[256,768]{1,0:T(8,128)(2,1)S(1)} %fusion.44), channel_id=1, source_target_pairs={{0,1},{1,0},{2,3},{3,2},{4,5},{5,4},{6,7},{7,6},{8,9},{9,8},{10,11... | collective-permute-start | bytes 1179656 | tf_op jit(solution)/shard_map/ppermute | solution.py:96
  444.7 32.7 %collective-permute-start.15 = (f16[656,1024]{1,0:T(8,128)(2,1)}, f16[656,1024]{1,0:T(8,128)(2,1)}, u32[]{:S(2)}, u32[]{:S(2)}) collective-permute-start(f16[656,1024]{1,0:T(8,128)(2,1)} %select_convert_fusion.2), channel_id=1, source_target_pairs={{0,4},{4,0},{8,12},{12,8},{16,20},{20,16},{24,28},{28,24},{1,5},{5... | collective-permute-start | bytes 4030472 | tf_op jit(solution)/shard_map/ppermute | solution.py:96
  463.2 63.6 %collective-permute-start.16 = (f16[656,1024]{1,0:T(8,128)(2,1)}, f16[656,1024]{1,0:T(8,128)(2,1)}, u32[]{:S(2)}, u32[]{:S(2)}) collective-permute-start(f16[656,1024]{1,0:T(8,128)(2,1)} %select_convert_fusion.1), channel_id=1, source_target_pairs={{0,4},{4,0},{8,12},{12,8},{16,20},{20,16},{24,28},{28,24},{1,5},{5... | collective-permute-start | bytes 4030472 | tf_op jit(solution)/shard_map/ppermute | solution.py:96
  493.5 43.9 %collective-permute-start.17 = (f16[176,1024]{1,0:T(8,128)(2,1)}, f16[176,1024]{1,0:T(8,128)(2,1)}, u32[]{:S(2)}, u32[]{:S(2)}) collective-permute-start(f16[176,1024]{1,0:T(8,128)(2,1)} %get-tuple-element.150), channel_id=1, source_target_pairs={{0,8},{4,12},{8,0},{12,4},{16,24},{20,28},{24,16},{28,20},{1,9},{5... | collective-permute-start | bytes 1081352 | tf_op jit(solution)/shard_map/ppermute | solution.py:460
  493.7 43.7 %collective-permute-start.18 = (f16[176,1024]{1,0:T(8,128)(2,1)}, f16[176,1024]{1,0:T(8,128)(2,1)}, u32[]{:S(2)}, u32[]{:S(2)}) collective-permute-start(f16[176,1024]{1,0:T(8,128)(2,1)} %get-tuple-element.151), channel_id=1, source_target_pairs={{0,16},{4,20},{8,24},{12,28},{16,0},{20,4},{24,8},{28,12},{1,17},{... | collective-permute-start | bytes 1081352 | tf_op jit(solution)/shard_map/ppermute | solution.py:460
  496.5 40.9 %collective-permute-start.19 = (f16[176,1024]{1,0:T(8,128)(2,1)}, f16[176,1024]{1,0:T(8,128)(2,1)}, u32[]{:S(2)}, u32[]{:S(2)}) collective-permute-start(f16[176,1024]{1,0:T(8,128)(2,1)} %get-tuple-element.152), channel_id=1, source_target_pairs={{0,24},{4,28},{8,16},{12,20},{16,8},{20,12},{24,0},{28,4},{1,25},{... | collective-permute-start | bytes 1081352 | tf_op jit(solution)/shard_map/ppermute | solution.py:460
  527.6 53.5 %collective-permute-start.20 = (f16[2512,256]{1,0:T(8,128)(2,1)}, f16[2512,256]{1,0:T(8,128)(2,1)}, u32[]{:S(2)}, u32[]{:S(2)}) collective-permute-start(f16[2512,256]{1,0:T(8,128)(2,1)} %select_convert_fusion.3), channel_id=1, source_target_pairs={{0,4},{4,0},{8,12},{12,8},{16,20},{20,16},{24,28},{28,24},{1,5},{5... | collective-permute-start | bytes 3858440 | tf_op jit(solution)/shard_map/ppermute | solution.py:96
  545.9 39.1 %collective-permute-start.21 = (f16[176,1024]{1,0:T(8,128)(2,1)}, f16[176,1024]{1,0:T(8,128)(2,1)}, u32[]{:S(2)}, u32[]{:S(2)}) collective-permute-start(f16[176,1024]{1,0:T(8,128)(2,1)} %get-tuple-element.158), channel_id=1, source_target_pairs={{0,8},{4,12},{8,0},{12,4},{16,24},{20,28},{24,16},{28,20},{1,9},{5... | collective-permute-start | bytes 1081352 | tf_op jit(solution)/shard_map/ppermute | solution.py:460
  546.0 39.1 %collective-permute-start.22 = (f16[176,1024]{1,0:T(8,128)(2,1)}, f16[176,1024]{1,0:T(8,128)(2,1)}, u32[]{:S(2)}, u32[]{:S(2)}) collective-permute-start(f16[176,1024]{1,0:T(8,128)(2,1)} %get-tuple-element.159), channel_id=1, source_target_pairs={{0,16},{4,20},{8,24},{12,28},{16,0},{20,4},{24,8},{28,12},{1,17},{... | collective-permute-start | bytes 1081352 | tf_op jit(solution)/shard_map/ppermute | solution.py:460
  549.4 35.6 %collective-permute-start.23 = (f16[176,1024]{1,0:T(8,128)(2,1)}, f16[176,1024]{1,0:T(8,128)(2,1)}, u32[]{:S(2)}, u32[]{:S(2)}) collective-permute-start(f16[176,1024]{1,0:T(8,128)(2,1)} %get-tuple-element.160), channel_id=1, source_target_pairs={{0,24},{4,28},{8,16},{12,20},{16,8},{20,12},{24,0},{28,4},{1,25},{... | collective-permute-start | bytes 1081352 | tf_op jit(solution)/shard_map/ppermute | solution.py:460
  572.7 51.1 %collective-permute-start.24 = (f16[1168,768]{1,0:T(8,128)(2,1)}, f16[1168,768]{1,0:T(8,128)(2,1)}, u32[]{:S(2)}, u32[]{:S(2)}) collective-permute-start(f16[1168,768]{1,0:T(8,128)(2,1)} %select_convert_fusion), channel_id=1, source_target_pairs={{0,4},{4,0},{8,12},{12,8},{16,20},{20,16},{24,28},{28,24},{1,5},{5... | collective-permute-start | bytes 5382152 | tf_op jit(solution)/shard_map/ppermute | solution.py:96
  590.7 37.8 %collective-permute-start.25 = (f16[640,256]{1,0:T(8,128)(2,1)}, f16[640,256]{1,0:T(8,128)(2,1)}, u32[]{:S(2)}, u32[]{:S(2)}) collective-permute-start(f16[640,256]{1,0:T(8,128)(2,1)} %get-tuple-element.165), channel_id=1, source_target_pairs={{0,8},{4,12},{8,0},{12,4},{16,24},{20,28},{24,16},{28,20},{1,9},{5... | collective-permute-start | bytes 983048 | tf_op jit(solution)/shard_map/ppermute | solution.py:460
  590.7 37.7 %collective-permute-start.26 = (f16[640,256]{1,0:T(8,128)(2,1)}, f16[640,256]{1,0:T(8,128)(2,1)}, u32[]{:S(2)}, u32[]{:S(2)}) collective-permute-start(f16[640,256]{1,0:T(8,128)(2,1)} %get-tuple-element.166), channel_id=1, source_target_pairs={{0,16},{4,20},{8,24},{12,28},{16,0},{20,4},{24,8},{28,12},{1,17},{... | collective-permute-start | bytes 983048 | tf_op jit(solution)/shard_map/ppermute | solution.py:460
  593.7 34.7 %collective-permute-start.27 = (f16[640,256]{1,0:T(8,128)(2,1)}, f16[640,256]{1,0:T(8,128)(2,1)}, u32[]{:S(2)}, u32[]{:S(2)}) collective-permute-start(f16[640,256]{1,0:T(8,128)(2,1)} %get-tuple-element.167), channel_id=1, source_target_pairs={{0,24},{4,28},{8,16},{12,20},{16,8},{20,12},{24,0},{28,4},{1,25},{... | collective-permute-start | bytes 983048 | tf_op jit(solution)/shard_map/ppermute | solution.py:460
  644.4 41.3 %collective-permute-start.30 = (f16[304,768]{1,0:T(8,128)(2,1)}, f16[304,768]{1,0:T(8,128)(2,1)}, u32[]{:S(2)}, u32[]{:S(2)}) collective-permute-start(f16[304,768]{1,0:T(8,128)(2,1)} %get-tuple-element.184), channel_id=1, source_target_pairs={{0,8},{4,12},{8,0},{12,4},{16,24},{20,28},{24,16},{28,20},{1,9},{5... | collective-permute-start | bytes 1400840 | tf_op jit(solution)/shard_map/ppermute | solution.py:460
  644.4 41.3 %collective-permute-start.31 = (f16[304,768]{1,0:T(8,128)(2,1)}, f16[304,768]{1,0:T(8,128)(2,1)}, u32[]{:S(2)}, u32[]{:S(2)}) collective-permute-start(f16[304,768]{1,0:T(8,128)(2,1)} %get-tuple-element.185), channel_id=1, source_target_pairs={{0,16},{4,20},{8,24},{12,28},{16,0},{20,4},{24,8},{28,12},{1,17},{... | collective-permute-start | bytes 1400840 | tf_op jit(solution)/shard_map/ppermute | solution.py:460
  647.4 38.2 %collective-permute-start.32 = (f16[304,768]{1,0:T(8,128)(2,1)}, f16[304,768]{1,0:T(8,128)(2,1)}, u32[]{:S(2)}, u32[]{:S(2)}) collective-permute-start(f16[304,768]{1,0:T(8,128)(2,1)} %get-tuple-element.186), channel_id=1, source_target_pairs={{0,24},{4,28},{8,16},{12,20},{16,8},{20,12},{24,0},{28,4},{1,25},{... | collective-permute-start | bytes 1400840 | tf_op jit(solution)/shard_map/ppermute | solution.py:460
  649.4 23.8 %collective-permute-start.29 = (f16[304,768]{1,0:T(8,128)(2,1)}, f16[304,768]{1,0:T(8,128)(2,1)S(1)}, u32[]{:S(2)}, u32[]{:S(2)}) collective-permute-start(f16[304,768]{1,0:T(8,128)(2,1)} %get-tuple-element.173), channel_id=1, source_target_pairs={{0,4},{4,0},{8,12},{12,8},{16,20},{20,16},{24,28},{28,24},{1,5},{5... | collective-permute-start | bytes 1400840 | tf_op jit(solution)/shard_map/ppermute | solution.py:96
  663.2 27.8 %collective-permute-start.34 = (f16[304,768]{1,0:T(8,128)(2,1)}, f16[304,768]{1,0:T(8,128)(2,1)}, u32[]{:S(2)}, u32[]{:S(2)}) collective-permute-start(f16[304,768]{1,0:T(8,128)(2,1)} %get-tuple-element.189), channel_id=1, source_target_pairs={{0,4},{4,0},{8,12},{12,8},{16,20},{20,16},{24,28},{28,24},{1,5},{5... | collective-permute-start | bytes 1400840 | tf_op jit(solution)/shard_map/ppermute | solution.py:96
  673.2 18.6 %collective-permute-start.33 = (f16[304,768]{1,0:T(8,128)(2,1)}, f16[304,768]{1,0:T(8,128)(2,1)}, u32[]{:S(2)}, u32[]{:S(2)}) collective-permute-start(f16[304,768]{1,0:T(8,128)(2,1)} %select_convert_fusion.7), channel_id=1, source_target_pairs={{0,4},{4,0},{8,12},{12,8},{16,20},{20,16},{24,28},{28,24},{1,5},{5... | collective-permute-start | bytes 1400840 | tf_op jit(solution)/shard_map/ppermute | solution.py:96
  703.9 22.1 %collective-permute-start.35 = (f16[304,768]{1,0:T(8,128)(2,1)S(1)}, f16[304,768]{1,0:T(8,128)(2,1)S(1)}, u32[]{:S(2)}, u32[]{:S(2)}) collective-permute-start(f16[304,768]{1,0:T(8,128)(2,1)S(1)} %get-tuple-element.199), channel_id=1, source_target_pairs={{0,8},{4,12},{8,0},{12,4},{16,24},{20,28},{24,16},{28,20},{1,9},{5... | collective-permute-start | bytes 1400840 | tf_op jit(solution)/shard_map/ppermute | solution.py:96
  706.7 34.9 %collective-permute-start.36 = (f16[304,768]{1,0:T(8,128)(2,1)}, f16[304,768]{1,0:T(8,128)(2,1)}, u32[]{:S(2)}, u32[]{:S(2)}) collective-permute-start(f16[304,768]{1,0:T(8,128)(2,1)} %get-tuple-element.202), channel_id=1, source_target_pairs={{0,16},{4,20},{8,24},{12,28},{16,0},{20,4},{24,8},{28,12},{1,17},{... | collective-permute-start | bytes 1400840 | tf_op jit(solution)/shard_map/ppermute | solution.py:96
  707.6 60.0 %collective-permute-start.37 = (f16[304,768]{1,0:T(8,128)(2,1)}, f16[304,768]{1,0:T(8,128)(2,1)}, u32[]{:S(2)}, u32[]{:S(2)}) collective-permute-start(f16[304,768]{1,0:T(8,128)(2,1)} %get-tuple-element.204), channel_id=1, source_target_pairs={{0,24},{4,28},{8,16},{12,20},{16,8},{20,12},{24,0},{28,4},{1,25},{... | collective-permute-start | bytes 1400840 | tf_op jit(solution)/shard_map/ppermute | solution.py:96
  (333 other events, 2139.0 us)
Sparse Core Ops, SparseCore 0:
  217.0 85.2 all-gather.1

commit v6 on v5

--- a/solution.py
+++ b/solution.py
@@ -1322,7 +1322,6 @@
     if dp_size == 8 and tensor_size == 4:
         bias_count = bias_local.shape[0]
         bias_local = jnp.pad(bias_local, ((0, -bias_count % 32), (0, 0)))
-        grad_tables = traffic.arrive(grad_tables, 1)
         owned_cols, bias_grad = tail_exchange(grad_tables.T, bias_local)
         encoder_owned, (owned_cols, bias_grad) = traffic.encoder_total((owned_cols, bias_grad))
         owned_cols = jnp.concatenate([owned_cols[index] for index in range(4)], axis=1)

time: 836 us -> 832 us (level)
  waiting for transfers between devices: 63 us -> 53.3 us
    ppermute x26, waiting for transfers between devices: 55 us -> 45.4 us  [swap(): lax.ppermute(value, axis, [(i, i ^ step) for i in range(lax.axis_size(axi...]
  transfers between devices with their start and end apart: 39 -> 39, of which waited for: 11 -> 10; matrix products, arithmetic and copies ran while one was open for 21% -> 21% of each run, Pallas kernels for 12% -> 13%
where the time goes in v6:
time: 832 us; the launch traced here: 820 us
  Pallas kernels  300 us (36%)
  other arithmetic  180 us (22%)
  local copies, waits for them, and re-layouts  99.1 us (12%)
  matrix products  91.1 us (11%)
  between operations  58.4 us (7%)
  waiting for transfers between devices  53.3 us (6%)
  starting transfers between devices  37.8 us (5%)
    pallas_call x13, Pallas kernels, tensor_sum(): pl.pallas_call(functools.partial(sum_kernel, count, cross_type), out_shap...  197 us
    pallas_call x1, Pallas kernels, gather_first(): pl.pallas_call(functools.partial(first_kernel, images), out_shape=[jax.Sh...  61.7 us
    ppermute x26, waiting for transfers between devices, swap(): lax.ppermute(value, axis, [(i, i ^ step) for i in range(lax.axis_size(axi...  45.4 us
    unnamed x655, local copies, waits for them, and re-layouts  39.4 us
    dot_general x18, matrix products, product_right(): lax.dot_general(left, right, (((1,), (1,)), ((), ())), preferred_element_...  32.6 us
    dot_general x22, matrix products, product_left(): lax.dot_general(left, right, (((0,), (0,)), ((), ())), preferred_element_...  30.8 us
    pallas_call x1, Pallas kernels, tail_exchange(): pl.pallas_call(tail_kernel, out_shape=[jax.ShapeDtypeStruct(four, jnp.flo...  30.6 us
    dot_general x23, matrix products, product(): return jnp.dot(left, right, preferred_element_type=jnp.float32)  20.5 us
  transfers between devices with their start and end apart: 39, of which 10 were waited for; matrix products, arithmetic and copies ran while one was open for 21% of the time, Pallas kernels for 13%

profile of v6, /device:TPU:0, one launch (start us, length us, event | category | flops | bytes accessed | tf_op | source)
XLA Modules:
  0.0 819.9 jit_solution(10998663717688162450)
XLA Ops:
  25.1 61.7 %shard_map.393 = (f32[8,8,128]{2,1,0:T(8,128)S(1)}, f32[8,96,128]{2,1,0:T(8,128)S(1)}, f32[4,8,184,96]{3,2,1,0:T(8,128)S(1)}, bf16[8,288,768]{2,1,0:T(8,128)(2,1)S(1)}) custom-call(f32[8,128]{1,0:T(8,128)S(1)} %dynamic_update_slice.82.notes, f32[96,1001]{1,0:T(8,128)S(1)} %copy-done.6, f32[184,96]{1,0:T(8,128)S(1)} %fusion.216.table_share, ...), custom_call_target="tpu_custom_call" | custom-call | tf_op jit(solution)/shard_map/pallas_call | solution.py:744
  90.6 4.2 reshape.1199
  120.6 22.5 %shard_map.394 = (f32[320,768]{1,0:T(8,128)S(1)}, bf16[8,144,768]{2,1,0:T(8,128)(2,1)S(1)}) custom-call(f32[320,768]{1,0:T(8,128)S(1)} %fusion.197.refs_0_, bf16[144,768]{1,0:T(8,128)(2,1)S(1)} %copy-done.9), custom_call_target="tpu_custom_call" | custom-call | bytes 2000000 | tf_op jit(solution)/shard_map/pallas_call | solution.py:248
  145.3 4.5 abs_reduce_fusion.6
  151.0 23.4 %shard_map.395 = (f32[320,768]{1,0:T(8,128)S(1)}, bf16[8,144,768]{2,1,0:T(8,128)(2,1)S(1)}) custom-call(f32[320,768]{1,0:T(8,128)S(1)} %fusion.73.refs_0_, bf16[144,768]{1,0:T(8,128)(2,1)S(1)} %copy-done.8), custom_call_target="tpu_custom_call" | custom-call | bytes 2000000 | tf_op jit(solution)/shard_map/pallas_call | solution.py:248
  184.3 28.8 %shard_map.396 = (f32[320,768]{1,0:T(8,128)S(1)}, bf16[8,624,256]{2,1,0:T(8,128)(2,1)S(1)}) custom-call(f32[320,768]{1,0:T(8,128)S(1)} %fusion.194.refs_0_, bf16[624,256]{1,0:T(8,128)(2,1)S(1)} %copy-done.7), custom_call_target="tpu_custom_call" | custom-call | bytes 2000000 | tf_op jit(solution)/shard_map/pallas_call | solution.py:248
  222.6 4.5 abs_reduce_fusion.8
  228.5 15.1 %shard_map.397 = f32[320,768]{1,0:T(8,128)S(1)} custom-call(f32[320,768]{1,0:T(8,128)S(1)} %fusion.66.refs_0_), custom_call_target="tpu_custom_call" | custom-call | bytes 2000000 | tf_op jit(solution)/shard_map/pallas_call | solution.py:248
  294.4 7.9 all-gather.2.cloned.1.call-done
  316.0 8.1 collective-permute-done.7
  324.2 6.0 collective-permute-done.10
  338.6 12.1 %shard_map.398 = f32[256,1024]{1,0:T(8,128)S(1)} custom-call(f32[256,1024]{1,0:T(8,128)S(1)} %fusion.138.refs_0_), custom_call_target="tpu_custom_call" | custom-call | bytes 2000000 | tf_op jit(solution)/shard_map/pallas_call | solution.py:248
  354.5 12.1 %shard_map.399 = f32[256,1024]{1,0:T(8,128)S(1)} custom-call(f32[256,1024]{1,0:T(8,128)S(1)} %fusion.131.refs_0_), custom_call_target="tpu_custom_call" | custom-call | bytes 2000000 | tf_op jit(solution)/shard_map/pallas_call | solution.py:248
  375.4 12.1 %shard_map.400 = f32[256,1024]{1,0:T(8,128)S(1)} custom-call(f32[256,1024]{1,0:T(8,128)S(1)} %fusion.133.refs_0_), custom_call_target="tpu_custom_call" | custom-call | bytes 2000000 | tf_op jit(solution)/shard_map/pallas_call | solution.py:248
  409.1 12.1 %shard_map.401 = f32[256,1024]{1,0:T(8,128)S(1)} custom-call(f32[256,1024]{1,0:T(8,128)S(1)} %fusion.140.refs_0_), custom_call_target="tpu_custom_call" | custom-call | bytes 2000000 | tf_op jit(solution)/shard_map/pallas_call | solution.py:248
  451.1 12.1 %shard_map.402 = f32[256,1024]{1,0:T(8,128)S(1)} custom-call(f32[256,1024]{1,0:T(8,128)S(1)} %fusion.23.refs_0_), custom_call_target="tpu_custom_call" | custom-call | bytes 2000000 | tf_op jit(solution)/shard_map/pallas_call | solution.py:248
  472.1 5.2 collective-permute-done.15
  511.1 11.7 %shard_map.403 = f32[320,768]{1,0:T(8,128)S(1)} custom-call(f32[320,768]{1,0:T(8,128)S(1)} %fusion.68.refs_0_), custom_call_target="tpu_custom_call" | custom-call | bytes 2000000 | tf_op jit(solution)/shard_map/pallas_call | solution.py:248
  546.0 3.4 collective-permute-start.22
  561.1 11.6 %shard_map.404 = f32[320,768]{1,0:T(8,128)S(1)} custom-call(f32[320,768]{1,0:T(8,128)S(1)} %fusion.252.refs_0_), custom_call_target="tpu_custom_call" | custom-call | bytes 2000000 | tf_op jit(solution)/shard_map/pallas_call | solution.py:248
  577.7 3.3 multiply_reduce_fusion.29
  600.9 11.7 %shard_map.405 = f32[320,768]{1,0:T(8,128)S(1)} custom-call(f32[320,768]{1,0:T(8,128)S(1)} %fusion.75.refs_0_), custom_call_target="tpu_custom_call" | custom-call | bytes 2000000 | tf_op jit(solution)/shard_map/pallas_call | solution.py:248
  616.1 3.3 multiply_reduce_fusion.30
  664.2 9.1 %collective-permute-done.29 = f16[304,768]{1,0:T(8,128)(2,1)S(1)} collective-permute-done((f16[304,768]{1,0:T(8,128)(2,1)}, f16[304,768]{1,0:T(8,128)(2,1)S(1)}, u32[]{:S(2)}, u32[]{:S(2)}) %collective-permute-start.29) | collective-permute-done | bytes 466976 | tf_op jit(solution)/shard_map/ppermute | solution.py:96
  674.0 11.6 %shard_map.406 = f32[320,768]{1,0:T(8,128)S(1)} custom-call(f32[320,768]{1,0:T(8,128)S(1)} %fusion.327.refs_0_), custom_call_target="tpu_custom_call" | custom-call | bytes 2000000 | tf_op jit(solution)/shard_map/pallas_call | solution.py:248
  709.1 3.6 multiply_reduce_fusion.25
  713.1 12.9 %collective-permute-done.35 = f16[304,768]{1,0:T(8,128)(2,1)S(1)} collective-permute-done((f16[304,768]{1,0:T(8,128)(2,1)S(1)}, f16[304,768]{1,0:T(8,128)(2,1)S(1)}, u32[]{:S(2)}, u32[]{:S(2)}) %collective-permute-start.35) | collective-permute-done | bytes 466976 | tf_op jit(solution)/shard_map/ppermute | solution.py:96
  733.3 30.6 %shard_map.407 = (f32[4,96,184]{2,1,0:T(8,128)S(1)}, f32[224,128]{1,0:T(8,128)S(1)}) custom-call(f32[4,96,184]{2,1,0:T(8,128)S(1)} %get-tuple-element.457.refs_0_, f32[4,96,184]{2,1,0:T(8,128)S(1)} %get-tuple-element.456.refs_1_, f32[224,128]{1,0:T(8,128)S(1)} %pad.117.refs_2_), custom_call_target="tpu_custom_call" | custom-call | tf_op jit(solution)/shard_map/pallas_call | solution.py:549
  773.5 4.0 multiply_reduce_fusion.26
  780.2 11.1 %shard_map.408 = f32[8,128]{1,0:T(8,128)} custom-call(f32[8,128]{1,0:T(8,128)} %broadcast_select_fusion.value), custom_call_target="tpu_custom_call" | custom-call | tf_op jit(solution)/shard_map/pallas_call | solution.py:330
  795.5 3.6 fusion.256
  806.7 3.6 fusion.262
  (1132 shorter events, 373.6 us)
Async XLA Ops:
  7.2 295.1 %all-gather.2.cloned.1.call-start = ((), (), s32[]{:S(2)}) async-start(), calls=%async_computation | async-start | bytes 5898240 | tf_op jit(solution)/shard_map/all_gather | solution.py:1116
  215.2 53.4 %collective-permute-start.1 = (bf16[1920,256]{1,0:T(8,128)(2,1)}, bf16[1920,256]{1,0:T(8,128)(2,1)}, u32[]{:S(2)}, u32[]{:S(2)}) collective-permute-start(bf16[1920,256]{1,0:T(8,128)(2,1)} %pad_maximum_fusion.7), channel_id=1, source_target_pairs={{0,2},{1,3},{2,0},{3,1},{4,6},{5,7},{6,4},{7,5},{8,10},{9,11},{10,... | collective-permute-start | bytes 2949128 | tf_op jit(solution)/shard_map/ppermute | solution.py:96
  216.9 67.8 %collective-permute-start = (bf16[1920,256]{1,0:T(8,128)(2,1)}, bf16[1920,256]{1,0:T(8,128)(2,1)}, u32[]{:S(2)}, u32[]{:S(2)}) collective-permute-start(bf16[1920,256]{1,0:T(8,128)(2,1)} %pad_maximum_fusion.7), channel_id=1, source_target_pairs={{0,1},{1,0},{2,3},{3,2},{4,5},{5,4},{6,7},{7,6},{8,9},{9,8},{10,11... | collective-permute-start | bytes 2949128 | tf_op jit(solution)/shard_map/ppermute | solution.py:96
  249.7 27.6 %collective-permute-start.4 = (bf16[256,256]{1,0:T(8,128)(2,1)}, bf16[256,256]{1,0:T(8,128)(2,1)}, u32[]{:S(2)}, u32[]{:S(2)}) collective-permute-start(bf16[256,256]{1,0:T(8,128)(2,1)} %get-tuple-element.564), channel_id=1, source_target_pairs={{0,2},{1,3},{2,0},{3,1},{4,6},{5,7},{6,4},{7,5},{8,10},{9,11},{10,... | collective-permute-start | bytes 393224 | tf_op jit(solution)/shard_map/ppermute | solution.py:96
  251.5 29.9 %collective-permute-start.3 = (bf16[256,256]{1,0:T(8,128)(2,1)}, bf16[256,256]{1,0:T(8,128)(2,1)}, u32[]{:S(2)}, u32[]{:S(2)}) collective-permute-start(bf16[256,256]{1,0:T(8,128)(2,1)} %get-tuple-element.564), channel_id=1, source_target_pairs={{0,1},{1,0},{2,3},{3,2},{4,5},{5,4},{6,7},{7,6},{8,9},{9,8},{10,11... | collective-permute-start | bytes 393224 | tf_op jit(solution)/shard_map/ppermute | solution.py:96
  268.6 16.0 %collective-permute-start.2 = (bf16[1920,256]{1,0:T(8,128)(2,1)}, bf16[1920,256]{1,0:T(8,128)(2,1)}, u32[]{:S(2)}, u32[]{:S(2)}) collective-permute-start(bf16[1920,256]{1,0:T(8,128)(2,1)} %collective-permute-done.1), channel_id=1, source_target_pairs={{0,1},{1,0},{2,3},{3,2},{4,5},{5,4},{6,7},{7,6},{8,9},{9,8},{10,11... | collective-permute-start | bytes 2949128 | tf_op jit(solution)/shard_map/ppermute | solution.py:96
  312.4 17.8 %collective-permute-start.10 = (bf16[256,768]{1,0:T(8,128)(2,1)S(1)}, bf16[256,768]{1,0:T(8,128)(2,1)S(1)}, u32[]{:S(2)}, u32[]{:S(2)}) collective-permute-start(bf16[256,768]{1,0:T(8,128)(2,1)S(1)} %fusion.44), channel_id=1, source_target_pairs={{0,2},{1,3},{2,0},{3,1},{4,6},{5,7},{6,4},{7,5},{8,10},{9,11},{10,... | collective-permute-start | bytes 1179656 | tf_op jit(solution)/shard_map/ppermute | solution.py:96
  314.2 16.0 %collective-permute-start.14 = (bf16[256,512]{1,0:T(8,128)(2,1)}, bf16[256,512]{1,0:T(8,128)(2,1)}, u32[]{:S(2)}, u32[]{:S(2)}) collective-permute-start(bf16[256,512]{1,0:T(8,128)(2,1)} %collective-permute-done.13), channel_id=1, source_target_pairs={{0,1},{1,0},{2,3},{3,2},{4,5},{5,4},{6,7},{7,6},{8,9},{9,8},{10,11... | collective-permute-start | bytes 786440 | tf_op jit(solution)/shard_map/ppermute | solution.py:96
  314.7 18.5 %collective-permute-start.6 = (bf16[256,768]{1,0:T(8,128)(2,1)}, bf16[256,768]{1,0:T(8,128)(2,1)}, u32[]{:S(2)}, u32[]{:S(2)}) collective-permute-start(bf16[256,768]{1,0:T(8,128)(2,1)} %fusion.47), channel_id=1, source_target_pairs={{0,1},{1,0},{2,3},{3,2},{4,5},{5,4},{6,7},{7,6},{8,9},{9,8},{10,11... | collective-permute-start | bytes 1179656 | tf_op jit(solution)/shard_map/ppermute | solution.py:96
  315.8 16.0 %collective-permute-start.9 = (bf16[256,768]{1,0:T(8,128)(2,1)S(1)}, bf16[256,768]{1,0:T(8,128)(2,1)S(1)}, u32[]{:S(2)}, u32[]{:S(2)}) collective-permute-start(bf16[256,768]{1,0:T(8,128)(2,1)S(1)} %fusion.44), channel_id=1, source_target_pairs={{0,1},{1,0},{2,3},{3,2},{4,5},{5,4},{6,7},{7,6},{8,9},{9,8},{10,11... | collective-permute-start | bytes 1179656 | tf_op jit(solution)/shard_map/ppermute | solution.py:96
  444.7 32.7 %collective-permute-start.15 = (f16[656,1024]{1,0:T(8,128)(2,1)}, f16[656,1024]{1,0:T(8,128)(2,1)}, u32[]{:S(2)}, u32[]{:S(2)}) collective-permute-start(f16[656,1024]{1,0:T(8,128)(2,1)} %select_convert_fusion.2), channel_id=1, source_target_pairs={{0,4},{4,0},{8,12},{12,8},{16,20},{20,16},{24,28},{28,24},{1,5},{5... | collective-permute-start | bytes 4030472 | tf_op jit(solution)/shard_map/ppermute | solution.py:96
  463.2 63.6 %collective-permute-start.16 = (f16[656,1024]{1,0:T(8,128)(2,1)}, f16[656,1024]{1,0:T(8,128)(2,1)}, u32[]{:S(2)}, u32[]{:S(2)}) collective-permute-start(f16[656,1024]{1,0:T(8,128)(2,1)} %select_convert_fusion.1), channel_id=1, source_target_pairs={{0,4},{4,0},{8,12},{12,8},{16,20},{20,16},{24,28},{28,24},{1,5},{5... | collective-permute-start | bytes 4030472 | tf_op jit(solution)/shard_map/ppermute | solution.py:96
  493.5 43.9 %collective-permute-start.17 = (f16[176,1024]{1,0:T(8,128)(2,1)}, f16[176,1024]{1,0:T(8,128)(2,1)}, u32[]{:S(2)}, u32[]{:S(2)}) collective-permute-start(f16[176,1024]{1,0:T(8,128)(2,1)} %get-tuple-element.148), channel_id=1, source_target_pairs={{0,8},{4,12},{8,0},{12,4},{16,24},{20,28},{24,16},{28,20},{1,9},{5... | collective-permute-start | bytes 1081352 | tf_op jit(solution)/shard_map/ppermute | solution.py:460
  493.7 43.7 %collective-permute-start.18 = (f16[176,1024]{1,0:T(8,128)(2,1)}, f16[176,1024]{1,0:T(8,128)(2,1)}, u32[]{:S(2)}, u32[]{:S(2)}) collective-permute-start(f16[176,1024]{1,0:T(8,128)(2,1)} %get-tuple-element.149), channel_id=1, source_target_pairs={{0,16},{4,20},{8,24},{12,28},{16,0},{20,4},{24,8},{28,12},{1,17},{... | collective-permute-start | bytes 1081352 | tf_op jit(solution)/shard_map/ppermute | solution.py:460
  496.5 40.9 %collective-permute-start.19 = (f16[176,1024]{1,0:T(8,128)(2,1)}, f16[176,1024]{1,0:T(8,128)(2,1)}, u32[]{:S(2)}, u32[]{:S(2)}) collective-permute-start(f16[176,1024]{1,0:T(8,128)(2,1)} %get-tuple-element.150), channel_id=1, source_target_pairs={{0,24},{4,28},{8,16},{12,20},{16,8},{20,12},{24,0},{28,4},{1,25},{... | collective-permute-start | bytes 1081352 | tf_op jit(solution)/shard_map/ppermute | solution.py:460
  527.6 53.5 %collective-permute-start.20 = (f16[2512,256]{1,0:T(8,128)(2,1)}, f16[2512,256]{1,0:T(8,128)(2,1)}, u32[]{:S(2)}, u32[]{:S(2)}) collective-permute-start(f16[2512,256]{1,0:T(8,128)(2,1)} %select_convert_fusion.3), channel_id=1, source_target_pairs={{0,4},{4,0},{8,12},{12,8},{16,20},{20,16},{24,28},{28,24},{1,5},{5... | collective-permute-start | bytes 3858440 | tf_op jit(solution)/shard_map/ppermute | solution.py:96
  545.9 39.1 %collective-permute-start.21 = (f16[176,1024]{1,0:T(8,128)(2,1)}, f16[176,1024]{1,0:T(8,128)(2,1)}, u32[]{:S(2)}, u32[]{:S(2)}) collective-permute-start(f16[176,1024]{1,0:T(8,128)(2,1)} %get-tuple-element.156), channel_id=1, source_target_pairs={{0,8},{4,12},{8,0},{12,4},{16,24},{20,28},{24,16},{28,20},{1,9},{5... | collective-permute-start | bytes 1081352 | tf_op jit(solution)/shard_map/ppermute | solution.py:460
  546.0 39.1 %collective-permute-start.22 = (f16[176,1024]{1,0:T(8,128)(2,1)}, f16[176,1024]{1,0:T(8,128)(2,1)}, u32[]{:S(2)}, u32[]{:S(2)}) collective-permute-start(f16[176,1024]{1,0:T(8,128)(2,1)} %get-tuple-element.157), channel_id=1, source_target_pairs={{0,16},{4,20},{8,24},{12,28},{16,0},{20,4},{24,8},{28,12},{1,17},{... | collective-permute-start | bytes 1081352 | tf_op jit(solution)/shard_map/ppermute | solution.py:460
  549.4 35.6 %collective-permute-start.23 = (f16[176,1024]{1,0:T(8,128)(2,1)}, f16[176,1024]{1,0:T(8,128)(2,1)}, u32[]{:S(2)}, u32[]{:S(2)}) collective-permute-start(f16[176,1024]{1,0:T(8,128)(2,1)} %get-tuple-element.158), channel_id=1, source_target_pairs={{0,24},{4,28},{8,16},{12,20},{16,8},{20,12},{24,0},{28,4},{1,25},{... | collective-permute-start | bytes 1081352 | tf_op jit(solution)/shard_map/ppermute | solution.py:460
  572.7 51.1 %collective-permute-start.24 = (f16[1168,768]{1,0:T(8,128)(2,1)}, f16[1168,768]{1,0:T(8,128)(2,1)}, u32[]{:S(2)}, u32[]{:S(2)}) collective-permute-start(f16[1168,768]{1,0:T(8,128)(2,1)} %select_convert_fusion), channel_id=1, source_target_pairs={{0,4},{4,0},{8,12},{12,8},{16,20},{20,16},{24,28},{28,24},{1,5},{5... | collective-permute-start | bytes 5382152 | tf_op jit(solution)/shard_map/ppermute | solution.py:96
  590.7 37.8 %collective-permute-start.25 = (f16[640,256]{1,0:T(8,128)(2,1)}, f16[640,256]{1,0:T(8,128)(2,1)}, u32[]{:S(2)}, u32[]{:S(2)}) collective-permute-start(f16[640,256]{1,0:T(8,128)(2,1)} %get-tuple-element.163), channel_id=1, source_target_pairs={{0,8},{4,12},{8,0},{12,4},{16,24},{20,28},{24,16},{28,20},{1,9},{5... | collective-permute-start | bytes 983048 | tf_op jit(solution)/shard_map/ppermute | solution.py:460
  590.7 37.7 %collective-permute-start.26 = (f16[640,256]{1,0:T(8,128)(2,1)}, f16[640,256]{1,0:T(8,128)(2,1)}, u32[]{:S(2)}, u32[]{:S(2)}) collective-permute-start(f16[640,256]{1,0:T(8,128)(2,1)} %get-tuple-element.164), channel_id=1, source_target_pairs={{0,16},{4,20},{8,24},{12,28},{16,0},{20,4},{24,8},{28,12},{1,17},{... | collective-permute-start | bytes 983048 | tf_op jit(solution)/shard_map/ppermute | solution.py:460
  593.7 34.7 %collective-permute-start.27 = (f16[640,256]{1,0:T(8,128)(2,1)}, f16[640,256]{1,0:T(8,128)(2,1)}, u32[]{:S(2)}, u32[]{:S(2)}) collective-permute-start(f16[640,256]{1,0:T(8,128)(2,1)} %get-tuple-element.165), channel_id=1, source_target_pairs={{0,24},{4,28},{8,16},{12,20},{16,8},{20,12},{24,0},{28,4},{1,25},{... | collective-permute-start | bytes 983048 | tf_op jit(solution)/shard_map/ppermute | solution.py:460
  644.4 41.3 %collective-permute-start.30 = (f16[304,768]{1,0:T(8,128)(2,1)}, f16[304,768]{1,0:T(8,128)(2,1)}, u32[]{:S(2)}, u32[]{:S(2)}) collective-permute-start(f16[304,768]{1,0:T(8,128)(2,1)} %get-tuple-element.182), channel_id=1, source_target_pairs={{0,8},{4,12},{8,0},{12,4},{16,24},{20,28},{24,16},{28,20},{1,9},{5... | collective-permute-start | bytes 1400840 | tf_op jit(solution)/shard_map/ppermute | solution.py:460
  644.4 41.3 %collective-permute-start.31 = (f16[304,768]{1,0:T(8,128)(2,1)}, f16[304,768]{1,0:T(8,128)(2,1)}, u32[]{:S(2)}, u32[]{:S(2)}) collective-permute-start(f16[304,768]{1,0:T(8,128)(2,1)} %get-tuple-element.183), channel_id=1, source_target_pairs={{0,16},{4,20},{8,24},{12,28},{16,0},{20,4},{24,8},{28,12},{1,17},{... | collective-permute-start | bytes 1400840 | tf_op jit(solution)/shard_map/ppermute | solution.py:460
  647.4 38.2 %collective-permute-start.32 = (f16[304,768]{1,0:T(8,128)(2,1)}, f16[304,768]{1,0:T(8,128)(2,1)}, u32[]{:S(2)}, u32[]{:S(2)}) collective-permute-start(f16[304,768]{1,0:T(8,128)(2,1)} %get-tuple-element.184), channel_id=1, source_target_pairs={{0,24},{4,28},{8,16},{12,20},{16,8},{20,12},{24,0},{28,4},{1,25},{... | collective-permute-start | bytes 1400840 | tf_op jit(solution)/shard_map/ppermute | solution.py:460
  649.4 23.8 %collective-permute-start.29 = (f16[304,768]{1,0:T(8,128)(2,1)}, f16[304,768]{1,0:T(8,128)(2,1)S(1)}, u32[]{:S(2)}, u32[]{:S(2)}) collective-permute-start(f16[304,768]{1,0:T(8,128)(2,1)} %get-tuple-element.171), channel_id=1, source_target_pairs={{0,4},{4,0},{8,12},{12,8},{16,20},{20,16},{24,28},{28,24},{1,5},{5... | collective-permute-start | bytes 1400840 | tf_op jit(solution)/shard_map/ppermute | solution.py:96
  663.2 27.8 %collective-permute-start.34 = (f16[304,768]{1,0:T(8,128)(2,1)}, f16[304,768]{1,0:T(8,128)(2,1)}, u32[]{:S(2)}, u32[]{:S(2)}) collective-permute-start(f16[304,768]{1,0:T(8,128)(2,1)} %get-tuple-element.187), channel_id=1, source_target_pairs={{0,4},{4,0},{8,12},{12,8},{16,20},{20,16},{24,28},{28,24},{1,5},{5... | collective-permute-start | bytes 1400840 | tf_op jit(solution)/shard_map/ppermute | solution.py:96
  673.2 18.6 %collective-permute-start.33 = (f16[304,768]{1,0:T(8,128)(2,1)}, f16[304,768]{1,0:T(8,128)(2,1)}, u32[]{:S(2)}, u32[]{:S(2)}) collective-permute-start(f16[304,768]{1,0:T(8,128)(2,1)} %select_convert_fusion.7), channel_id=1, source_target_pairs={{0,4},{4,0},{8,12},{12,8},{16,20},{20,16},{24,28},{28,24},{1,5},{5... | collective-permute-start | bytes 1400840 | tf_op jit(solution)/shard_map/ppermute | solution.py:96
  703.9 22.1 %collective-permute-start.35 = (f16[304,768]{1,0:T(8,128)(2,1)S(1)}, f16[304,768]{1,0:T(8,128)(2,1)S(1)}, u32[]{:S(2)}, u32[]{:S(2)}) collective-permute-start(f16[304,768]{1,0:T(8,128)(2,1)S(1)} %get-tuple-element.197), channel_id=1, source_target_pairs={{0,8},{4,12},{8,0},{12,4},{16,24},{20,28},{24,16},{28,20},{1,9},{5... | collective-permute-start | bytes 1400840 | tf_op jit(solution)/shard_map/ppermute | solution.py:96
  706.7 57.2 %collective-permute-start.36 = (f16[304,768]{1,0:T(8,128)(2,1)}, f16[304,768]{1,0:T(8,128)(2,1)}, u32[]{:S(2)}, u32[]{:S(2)}) collective-permute-start(f16[304,768]{1,0:T(8,128)(2,1)} %get-tuple-element.199), channel_id=1, source_target_pairs={{0,16},{4,20},{8,24},{12,28},{16,0},{20,4},{24,8},{28,12},{1,17},{... | collective-permute-start | bytes 1400840 | tf_op jit(solution)/shard_map/ppermute | solution.py:96
  707.6 56.3 %collective-permute-start.37 = (f16[304,768]{1,0:T(8,128)(2,1)}, f16[304,768]{1,0:T(8,128)(2,1)}, u32[]{:S(2)}, u32[]{:S(2)}) collective-permute-start(f16[304,768]{1,0:T(8,128)(2,1)} %get-tuple-element.200), channel_id=1, source_target_pairs={{0,24},{4,28},{8,16},{12,20},{16,8},{20,12},{24,0},{28,4},{1,25},{... | collective-permute-start | bytes 1400840 | tf_op jit(solution)/shard_map/ppermute | solution.py:96
  (333 other events, 2150.7 us)
Sparse Core Ops, SparseCore 0:
  217.0 85.2 all-gather.1
